TPU v7x, 32 devices: a whole 2x2x4 slice. The times are simulated.
32 devices in a mesh: dp: 2 (over y), seq: 16 (over z, x, core).
Axes of the slice: x: 2, y: 2, z: 4, core: 2. Of those that a mesh axis runs over, the one named last changes fastest.
Arguments:
- q_rows: bfloat16 [4096, 32, 128], P(('dp', 'seq')), parts along dimension 0
- k_rows: bfloat16 [4096, 8, 128], P(('dp', 'seq')), parts along dimension 0
- v_rows: bfloat16 [4096, 8, 128], P(('dp', 'seq')), parts along dimension 0, may hold values from -5 to 5
- doc_lengths: int32 [32], P('dp'), parts along dimension 0, may hold values from 1 to 1024, 2048 in all
- plan_dest: int32 [512], P('dp'), parts along dimension 0, may hold values from 0 to 15, as said below
- plan_slot: int32 [512], P('dp'), parts along dimension 0, may hold values from 0 to 15, as said below
Outputs:
- attn_out: bfloat16 [4096, 32, 128], P(('dp', 'seq')), parts along dimension 0
There are 2 independent parts, one for each index of `dp`. A program takes and returns all parts, laid end to end along the dimension named above; each array names one. Nothing has to cross between parts.
Inputs may be any that keep to these rules, and one draw needn't show every extreme that they name: Loader block b is held by loader shard b // 16. plan_dest[b] is the sequence shard that block b goes to and plan_slot[b] its block position there. Every pair (plan_dest, plan_slot) occurs exactly once. One loader shard sends at most 2 blocks to one sequence shard, and exactly 2 to some. `plan_slot`: see plan_dest.
All inputs are finite; a program needn't handle non-finite values.
Results may differ from a plain program's by a relative error of at most 0.0034.
Values may be sent and summed in bfloat16 or wider, within the bound.
No kernel may reach another device: no remote copies, remote signals or barrier semaphores. Data moves between devices by JAX's collectives and lax.ppermute only.
A program may use at most 64 MiB of HBM per device.

v0:
```python
import jax
import jax.numpy as jnp
from jax import lax
from jax.sharding import PartitionSpec as P

far_below = -1e30


def doc_starts(doc_lengths, length_all):
    doc_ends = jnp.cumsum(doc_lengths)
    doc_begin = doc_ends - doc_lengths
    position = jnp.arange(length_all, dtype=jnp.int32)
    segment = jnp.sum((doc_ends[None, :] <= position[:, None]).astype(jnp.int32), axis=1)
    member = segment[:, None] == jnp.arange(doc_lengths.shape[0], dtype=jnp.int32)[None, :]
    return jnp.sum(jnp.where(member, doc_begin[None, :], 0), axis=1)


def attend(query_head, key_head, value_head, first_key, length_all, doc_span):
    query_block = min(512, length_all)
    key_window = min(length_all, query_block + doc_span)
    scaling = query_head.shape[-1] ** (-0.5)

    def one_block(number):
        query_start = number * query_block
        key_start = jnp.clip(query_start - doc_span, 0, length_all - key_window)
        rows_query = lax.dynamic_slice_in_dim(query_head, query_start, query_block, 0)
        rows_key = lax.dynamic_slice_in_dim(key_head, key_start, key_window, 0)
        rows_value = lax.dynamic_slice_in_dim(value_head, key_start, key_window, 0)
        scores = (
            lax.dot_general(
                rows_query, rows_key, (((1,), (1,)), ((), ())), preferred_element_type=jnp.float32
            )
            * scaling
        )
        query_pos = query_start + jnp.arange(query_block, dtype=jnp.int32)
        key_pos = key_start + jnp.arange(key_window, dtype=jnp.int32)
        first_rows = lax.dynamic_slice_in_dim(first_key, query_start, query_block, 0)
        allowed = (key_pos[None, :] <= query_pos[:, None]) & (
            key_pos[None, :] >= first_rows[:, None]
        )
        scores = jnp.where(allowed, scores, far_below)
        row_max = jnp.max(scores, axis=1, keepdims=True)
        weights = jnp.exp(scores - row_max)
        total_w = jnp.sum(weights, axis=1, keepdims=True)
        mixed_rows = (
            jnp.dot(weights.astype(jnp.bfloat16), rows_value, preferred_element_type=jnp.float32)
            / total_w
        )
        return mixed_rows.astype(jnp.bfloat16)

    blocks = lax.map(one_block, jnp.arange(length_all // query_block, dtype=jnp.int32))
    return blocks.reshape(length_all, query_head.shape[-1])


def widen(tensor, copies):
    return jnp.repeat(tensor, copies, axis=1)


def per_device(q_rows, k_rows, v_rows, doc_lengths, plan_dest, plan_slot):
    shards = lax.axis_size("seq")
    my_index = lax.axis_index("seq")
    tok_rows, heads_all, head_size = q_rows.shape
    kv_heads = k_rows.shape[1]
    length_all = tok_rows * shards
    doc_span = tok_rows * min(8, shards // 2)
    copies = max(1, shards // kv_heads)
    group = heads_all // kv_heads
    counter = jnp.arange(shards, dtype=jnp.int32)
    dest_table = plan_dest.reshape(shards, shards)
    slot_table = plan_slot.reshape(shards, shards)
    same_dest = dest_table[:, :, None] == dest_table[:, None, :]
    earlier = (counter[:, None] < counter[None, :])[None, :, :]
    rank_table = jnp.sum((same_dest & earlier).astype(jnp.int32), axis=1)
    my_dest = lax.dynamic_index_in_dim(dest_table, my_index, 0, keepdims=False)
    my_rank = lax.dynamic_index_in_dim(rank_table, my_index, 0, keepdims=False)
    send_target = my_dest * 2 + my_rank
    placer = (jnp.arange(2 * shards, dtype=jnp.int32)[:, None] == send_target[None, :]).astype(
        jnp.bfloat16
    )

    def spread(tensor):
        flattened = tensor.reshape(shards, -1)
        spread_rows = jnp.dot(placer, flattened, preferred_element_type=jnp.float32).astype(
            jnp.bfloat16
        )
        return spread_rows.reshape((shards, 2 * (tok_rows // shards)) + tensor.shape[1:])

    moved_q, moved_k, moved_v = (
        lax.all_to_all(spread(q_rows), "seq", split_axis=0, concat_axis=0, tiled=True),
        lax.all_to_all(spread(k_rows), "seq", split_axis=0, concat_axis=0, tiled=True),
        lax.all_to_all(spread(v_rows), "seq", split_axis=0, concat_axis=0, tiled=True),
    )
    source_code = counter[:, None] * 2 + rank_table
    matches = (dest_table[None, :, :] == my_index) & (
        slot_table[None, :, :] == counter[:, None, None]
    )
    source_index = jnp.sum(jnp.where(matches, source_code[None, :, :], 0), axis=(1, 2))
    picker = (jnp.arange(2 * shards, dtype=jnp.int32)[None, :] == source_index[:, None]).astype(
        jnp.bfloat16
    )

    def gather_slots(received):
        flattened = received.reshape(2 * shards, -1)
        chosen_rows = jnp.dot(picker, flattened, preferred_element_type=jnp.float32).astype(
            jnp.bfloat16
        )
        return chosen_rows.reshape((tok_rows,) + received.shape[2:])

    packed_q = gather_slots(moved_q)
    packed_k = widen(gather_slots(moved_k), copies)
    packed_v = widen(gather_slots(moved_v), copies)
    local_q, local_k, local_v = (
        lax.all_to_all(packed_q, "seq", split_axis=1, concat_axis=0, tiled=True),
        lax.all_to_all(packed_k, "seq", split_axis=1, concat_axis=0, tiled=True),
        lax.all_to_all(packed_v, "seq", split_axis=1, concat_axis=0, tiled=True),
    )
    first_key = doc_starts(doc_lengths, length_all)
    local_heads = heads_all // shards
    local_kv = local_k.shape[1]
    outputs = []
    for offset in range(local_heads):
        global_head = my_index * local_heads + offset
        kv_slot = jnp.maximum(global_head // group * copies - my_index * local_kv, 0)
        key_head = lax.dynamic_index_in_dim(local_k, kv_slot, 1, keepdims=False)
        value_head = lax.dynamic_index_in_dim(local_v, kv_slot, 1, keepdims=False)
        outputs.append(
            attend(local_q[:, offset, :], key_head, value_head, first_key, length_all, doc_span)
        )
    stacked = jnp.stack(outputs, axis=1)
    return lax.all_to_all(stacked, "seq", split_axis=0, concat_axis=1, tiled=True)


def solution(mesh):
    in_specs = (
        P(("dp", "seq"), None, None),
        P(("dp", "seq"), None, None),
        P(("dp", "seq"), None, None),
        P("dp"),
        P("dp"),
        P("dp"),
    )
    out_specs = P(("dp", "seq"), None, None)
    return jax.shard_map(
        per_device, mesh=mesh, in_specs=in_specs, out_specs=out_specs, check_vma=False
    )
```

profile of v0, /device:TPU:0, one launch (start us, length us, event | category | flops | bytes accessed | tf_op | source)
XLA Modules:
  0.0 234.0 jit_solution(10993867484713798714)
XLA Ops:
  0.0 0.8 broadcast_in_dim_reshape.2
  0.8 1.1 reshape.147
  2.3 1.0 reshape.148
  3.3 7.4 %all-to-all-start.2 = ((bf16[16,16,8,128]{3,2,1,0:T(8,128)(2,1)}), bf16[16,16,8,128]{3,2,1,0:T(8,128)(2,1)S(1)}, u32[]{:S(2)}, u32[]{:S(2)}) async-start(bf16[16,16,8,128]{3,2,1,0:T(8,128)(2,1)} %reshape.148), calls=%async_computation.2 | async-start | bytes 1048576 | tf_op jit(solution)/shard_map/all_to_all | solution.py:90
  11.1 1.1 reshape.153
  12.2 13.0 %all-to-all-done.2 = bf16[16,16,8,128]{3,2,1,0:T(8,128)(2,1)S(1)} async-done(((bf16[16,16,8,128]{3,2,1,0:T(8,128)(2,1)}), bf16[16,16,8,128]{3,2,1,0:T(8,128)(2,1)S(1)}, u32[]{:S(2)}, u32[]{:S(2)}) %all-to-all-start.2) | async-done | bytes 524320 | tf_op jit(solution)/shard_map/all_to_all | solution.py:90
  25.2 4.2 %all-to-all-start.4 = ((bf16[16,16,8,128]{3,2,1,0:T(8,128)(2,1)}), bf16[16,16,8,128]{3,2,1,0:T(8,128)(2,1)}, u32[]{:S(2)}, u32[]{:S(2)}) async-start(bf16[16,16,8,128]{3,2,1,0:T(8,128)(2,1)} %reshape.153), calls=%async_computation.4 | async-start | bytes 1048576 | tf_op jit(solution)/shard_map/all_to_all | solution.py:91
  29.9 0.7 convolution_convert_fusion
  30.6 2.4 %reshape.144 = bf16[16,16,32,128]{3,2,1,0:T(8,128)(2,1)} reshape(bf16[32,32768]{1,0:T(8,128)(2,1)S(1)} %convolution_convert_fusion) | data formatting | bytes 4194304 | tf_op jit(solution)/shard_map/reshape | solution.py:86
  33.0 10.9 %all-to-all-done.4 = bf16[16,16,8,128]{3,2,1,0:T(8,128)(2,1)} async-done(((bf16[16,16,8,128]{3,2,1,0:T(8,128)(2,1)}), bf16[16,16,8,128]{3,2,1,0:T(8,128)(2,1)}, u32[]{:S(2)}, u32[]{:S(2)}) %all-to-all-start.4) | async-done | bytes 524320 | tf_op jit(solution)/shard_map/all_to_all | solution.py:91
  43.9 4.1 %all-to-all-start = ((bf16[16,16,32,128]{3,2,1,0:T(8,128)(2,1)}), bf16[16,16,32,128]{3,2,1,0:T(8,128)(2,1)S(1)}, u32[]{:S(2)}, u32[]{:S(2)}) async-start(bf16[16,16,32,128]{3,2,1,0:T(8,128)(2,1)} %reshape.144), calls=%async_computation | async-start | bytes 4194304 | tf_op jit(solution)/shard_map/all_to_all | solution.py:89
  49.2 39.9 %all-to-all-done = bf16[16,16,32,128]{3,2,1,0:T(8,128)(2,1)S(1)} async-done(((bf16[16,16,32,128]{3,2,1,0:T(8,128)(2,1)}), bf16[16,16,32,128]{3,2,1,0:T(8,128)(2,1)S(1)}, u32[]{:S(2)}, u32[]{:S(2)}) %all-to-all-start) | async-done | bytes 2097184 | tf_op jit(solution)/shard_map/all_to_all | solution.py:89
  89.1 0.9 broadcast_in_dim.87
  90.0 11.2 %all-to-all-start.3 = ((bf16[128,16,128]{2,0,1:T(8,128)(2,1)}), bf16[128,16,128]{2,0,1:T(8,128)(2,1)S(1)}, u32[]{:S(2)}, u32[]{:S(2)}) async-start(bf16[128,16,128]{2,0,1:T(8,128)(2,1)} %bitcast.10), calls=%async_computation.3 | async-start | bytes 1048576 | tf_op jit(solution)/shard_map/all_to_all | solution.py:114
  101.2 2.3 reshape.145
  103.5 2.1 convolution_convert_fusion.1
  106.2 1.4 copy.39
  107.5 8.1 %all-to-all-done.3 = bf16[128,16,128]{2,0,1:T(8,128)(2,1)S(1)} async-done(((bf16[128,16,128]{2,0,1:T(8,128)(2,1)}), bf16[128,16,128]{2,0,1:T(8,128)(2,1)S(1)}, u32[]{:S(2)}, u32[]{:S(2)}) %all-to-all-start.3) | async-done | bytes 524320 | tf_op jit(solution)/shard_map/all_to_all | solution.py:114
  115.7 4.1 %all-to-all-start.1 = ((bf16[128,32,128]{2,0,1:T(8,128)(2,1)}), bf16[128,32,128]{2,0,1:T(8,128)(2,1)S(1)}, u32[]{:S(2)}, u32[]{:S(2)}) async-start(bf16[128,32,128]{2,0,1:T(8,128)(2,1)} %copy.39), calls=%async_computation.1 | async-start | bytes 2097152 | tf_op jit(solution)/shard_map/all_to_all | solution.py:113
  119.8 1.3 reshape.154
  121.5 21.2 %all-to-all-done.1 = bf16[128,32,128]{2,0,1:T(8,128)(2,1)S(1)} async-done(((bf16[128,32,128]{2,0,1:T(8,128)(2,1)}), bf16[128,32,128]{2,0,1:T(8,128)(2,1)S(1)}, u32[]{:S(2)}, u32[]{:S(2)}) %all-to-all-start.1) | async-done | bytes 1048608 | tf_op jit(solution)/shard_map/all_to_all | solution.py:113
  142.7 0.9 broadcast_in_dim.88
  143.6 6.9 %all-to-all-start.5 = ((bf16[128,16,128]{2,0,1:T(8,128)(2,1)}), bf16[128,16,128]{2,0,1:T(8,128)(2,1)S(1)}, u32[]{:S(2)}, u32[]{:S(2)}) async-start(bf16[128,16,128]{2,0,1:T(8,128)(2,1)} %bitcast.14), calls=%async_computation.5 | async-start | bytes 1048576 | tf_op jit(solution)/shard_map/all_to_all | solution.py:115
  151.1 13.8 %all-to-all-done.5 = bf16[128,16,128]{2,0,1:T(8,128)(2,1)S(1)} async-done(((bf16[128,16,128]{2,0,1:T(8,128)(2,1)}), bf16[128,16,128]{2,0,1:T(8,128)(2,1)S(1)}, u32[]{:S(2)}, u32[]{:S(2)}) %all-to-all-start.5) | async-done | bytes 524320 | tf_op jit(solution)/shard_map/all_to_all | solution.py:115
  165.0 14.7 %while.24 = (s32[]{:T(128)}, bf16[4,512,128]{2,1,0:T(8,128)(2,1)S(1)}, s32[4]{0:T(128)S(1)}, s32[2048]{0:T(1024)S(1)}, bf16[2048,128]{1,0:T(8,128)(2,1)S(1)}, /*...) while((s32[]{:T(128)}, ...), condition=%wide.region_8.9_spmd, body=%wide.region_5.8_spmd.sunk | while | flops 410649600 | bytes 10520823 | solution.py:51
  166.4 1.0 fusion.73
  168.0 0.7 fusion.75
  170.1 1.1 fusion.73
  171.7 0.7 fusion.75
  172.4 0.6 dynamic_slice.110
  173.8 1.0 fusion.73
  175.4 0.7 fusion.75
  176.1 0.6 dynamic_slice.110
  177.4 1.0 fusion.73
  179.0 0.7 fusion.75
  179.9 14.7 %while.25 = (s32[]{:T(128)}, bf16[4,512,128]{2,1,0:T(8,128)(2,1)S(1)}, s32[4]{0:T(128)S(1)}, s32[2048]{0:T(1024)S(1)}, bf16[2048,128]{1,0:T(8,128)(2,1)S(1)}, /*...) while((s32[]{:T(128)}, ...), condition=%wide.region_12.13_spmd, body=%wide.region_9.12_spmd.sunk | while | flops 410649600 | bytes 10520823 | solution.py:51
  181.2 1.0 fusion.78
  182.8 0.7 fusion.80
  183.5 0.6 dynamic_slice.115
  184.9 1.0 fusion.78
  186.5 0.7 fusion.80
  188.6 1.0 fusion.78
  190.2 0.7 fusion.80
  192.2 1.0 fusion.78
  193.8 0.7 fusion.80
  194.7 8.7 %copy.43 = bf16[2048,2,128]{2,1,0:T(2,128)(2,1)S(1)} copy(bf16[2048,2,128]{2,0,1:T(8,128)(2,1)S(1)} %pad_maximum_fusion) | data formatting | bytes 2097152 | tf_op jit(solution)/shard_map/stack | solution.py:129
  203.4 28.7 %all_to_all.81 = bf16[2048,2,128]{2,1,0:T(2,128)(2,1)S(1)} all-to-all(bf16[2048,2,128]{2,1,0:T(2,128)(2,1)S(1)} %copy.43), channel_id=1, replica_groups=mesh['dp'=2,'seq'=16] {'seq'}, dimensions={0} | all-to-all | bytes 2097152 | tf_op jit(solution)/shard_map/all_to_all | solution.py:130
  232.3 1.7 copy.46
  (84 shorter events, 12.8 us)
Async XLA Ops:
  0.0 10.7 %copy-start.3 = (bf16[128,8,128]{2,1,0:T(8,128)(2,1)S(1)}, bf16[128,8,128]{2,1,0:T(8,128)(2,1)}, u32[]{:S(2)}) copy-start(bf16[128,8,128]{2,1,0:T(8,128)(2,1)} %param.12) | copy-start | bytes 786436
  2.0 27.4 %copy-start.2 = (bf16[128,32,128]{2,1,0:T(8,128)(2,1)S(1)}, bf16[128,32,128]{2,1,0:T(8,128)(2,1)}, u32[]{:S(2)}) copy-start(bf16[128,32,128]{2,1,0:T(8,128)(2,1)} %param.10) | copy-start | bytes 3145732
  3.3 21.8 %all-to-all-start.2 = ((bf16[16,16,8,128]{3,2,1,0:T(8,128)(2,1)}), bf16[16,16,8,128]{3,2,1,0:T(8,128)(2,1)S(1)}, u32[]{:S(2)}, u32[]{:S(2)}) async-start(bf16[16,16,8,128]{3,2,1,0:T(8,128)(2,1)} %reshape.148), calls=%async_computation.2 | async-start | bytes 1048576 | tf_op jit(solution)/shard_map/all_to_all | solution.py:90
  25.2 4.2 %copy-start = (bf16[16,16,8,128]{3,2,1,0:T(8,128)(2,1)}, bf16[16,16,8,128]{3,2,1,0:T(8,128)(2,1)S(1)}, u32[]{:S(2)}) copy-start(bf16[16,16,8,128]{3,2,1,0:T(8,128)(2,1)S(1)} %all-to-all-done.2) | copy-start | bytes 1572868
  25.2 18.7 %all-to-all-start.4 = ((bf16[16,16,8,128]{3,2,1,0:T(8,128)(2,1)}), bf16[16,16,8,128]{3,2,1,0:T(8,128)(2,1)}, u32[]{:S(2)}, u32[]{:S(2)}) async-start(bf16[16,16,8,128]{3,2,1,0:T(8,128)(2,1)} %reshape.153), calls=%async_computation.4 | async-start | bytes 1048576 | tf_op jit(solution)/shard_map/all_to_all | solution.py:91
  30.6 17.3 %copy-start.4 = (s32[256]{0:T(256)S(1)}, s32[256]{0:T(256)}, u32[]{:S(2)}) copy-start(s32[256]{0:T(256)} %param.15) | copy-start | bytes 3076
  33.0 15.5 %copy-start.1 = (bf16[16,16,8,128]{3,2,1,0:T(8,128)(2,1)S(1)}, bf16[16,16,8,128]{3,2,1,0:T(8,128)(2,1)}, u32[]{:S(2)}) copy-start(bf16[16,16,8,128]{3,2,1,0:T(8,128)(2,1)} %copy-done) | copy-start | bytes 1572868
  43.9 45.2 %all-to-all-start = ((bf16[16,16,32,128]{3,2,1,0:T(8,128)(2,1)}), bf16[16,16,32,128]{3,2,1,0:T(8,128)(2,1)S(1)}, u32[]{:S(2)}, u32[]{:S(2)}) async-start(bf16[16,16,32,128]{3,2,1,0:T(8,128)(2,1)} %reshape.144), calls=%async_computation | async-start | bytes 4194304 | tf_op jit(solution)/shard_map/all_to_all | solution.py:89
  90.0 25.7 %all-to-all-start.3 = ((bf16[128,16,128]{2,0,1:T(8,128)(2,1)}), bf16[128,16,128]{2,0,1:T(8,128)(2,1)S(1)}, u32[]{:S(2)}, u32[]{:S(2)}) async-start(bf16[128,16,128]{2,0,1:T(8,128)(2,1)} %bitcast.10), calls=%async_computation.3 | async-start | bytes 1048576 | tf_op jit(solution)/shard_map/all_to_all | solution.py:114
  107.5 43.0 %copy-start.5 = (s32[16]{0:T(128)S(1)}, s32[16]{0:T(128)}, u32[]{:S(2)}) copy-start(s32[16]{0:T(128)} %param.13) | copy-start | bytes 196
  115.7 27.0 %all-to-all-start.1 = ((bf16[128,32,128]{2,0,1:T(8,128)(2,1)}), bf16[128,32,128]{2,0,1:T(8,128)(2,1)S(1)}, u32[]{:S(2)}, u32[]{:S(2)}) async-start(bf16[128,32,128]{2,0,1:T(8,128)(2,1)} %copy.39), calls=%async_computation.1 | async-start | bytes 2097152 | tf_op jit(solution)/shard_map/all_to_all | solution.py:113
  143.6 21.3 %all-to-all-start.5 = ((bf16[128,16,128]{2,0,1:T(8,128)(2,1)}), bf16[128,16,128]{2,0,1:T(8,128)(2,1)S(1)}, u32[]{:S(2)}, u32[]{:S(2)}) async-start(bf16[128,16,128]{2,0,1:T(8,128)(2,1)} %bitcast.14), calls=%async_computation.5 | async-start | bytes 1048576 | tf_op jit(solution)/shard_map/all_to_all | solution.py:115
where the time goes:
time: 235 us; the launch traced here: 234 us
  waiting for transfers between devices  107 us (46%)
  starting transfers between devices  37.8 us (16%)
  local copies, waits for them, and re-layouts  31.2 us (13%)
  blocking collectives  28.7 us (12%)
  matrix products  17.9 us (8%)
  other arithmetic  5.72 us (2%)
  loops' own time  5.4 us (2%)
    all_to_all x1, waiting for transfers between devices, per_device(): lax.all_to_all(spread(q_rows), 'seq', split_axis=0, concat_axis=0, tiled=...  39.9 us
    all_to_all x1, blocking collectives, per_device(): lax.all_to_all(stacked, 'seq', split_axis=0, concat_axis=1, tiled=True)  28.7 us
    all_to_all x1, waiting for transfers between devices, per_device(): lax.all_to_all(packed_q, 'seq', split_axis=1, concat_axis=0, tiled=True)  21.2 us
    all_to_all x1, waiting for transfers between devices, per_device(): lax.all_to_all(packed_v, 'seq', split_axis=1, concat_axis=0, tiled=True)  13.8 us
    all_to_all x1, waiting for transfers between devices, per_device(): lax.all_to_all(spread(k_rows), 'seq', split_axis=0, concat_axis=0, tiled=...  13 us
    all_to_all x1, starting transfers between devices, per_device(): lax.all_to_all(packed_k, 'seq', split_axis=1, concat_axis=0, tiled=True)  11.2 us
    all_to_all x1, waiting for transfers between devices, per_device(): lax.all_to_all(spread(v_rows), 'seq', split_axis=0, concat_axis=0, tiled=...  10.9 us
    another operation x1, local copies, waits for them, and re-layouts, per_device(): stacked = jnp.stack(outputs, axis=1)  8.68 us
  transfers between devices with their start and end apart: 6, of which 6 were waited for; matrix products, arithmetic and copies ran while one was open for 6% of the time, Pallas kernels for 0%

commit v1 on v0

v1 whole, which is shorter than its diff:
```python
import functools

import jax
import jax.numpy as jnp
import numpy as np
from jax import lax
from jax.experimental import pallas as pl
from jax.experimental.pallas import tpu as pltpu
from jax.sharding import PartitionSpec as P

far_below = -3e38


def attend_kernel(
    lengths, dest, slot, swap, *refs, heads, shards, rows, span, tile, paired
):
    if paired:
        mine, other, out, q_packed, kv_packed, begins = refs
    else:
        mine, out, q_packed, kv_packed, begins = refs
        other = None
    length = shards * rows
    docs = lengths.shape[0]
    slots = heads + (1 if paired else 2)
    head_size = out.shape[-1]

    begins[0] = 0
    for d in range(1, docs):
        begins[d] = begins[d - 1] + lengths[d - 1]

    own = swap[0]

    def pack_shard(source, carry):
        for b in range(shards):
            block = source * shards + b
            target = dest[block] * shards + slot[block]
            base = source * (slots * shards) + b
            for h in range(heads):
                q_packed[h, target] = mine[base + h * shards]
            if paired:
                kv_packed[own, target] = mine[base + heads * shards]
                kv_packed[1 - own, target] = other[block]
            else:
                kv_packed[0, target] = mine[base + heads * shards]
                kv_packed[1, target] = mine[base + (heads + 1) * shards]
        return carry

    lax.fori_loop(0, shards, pack_shard, 0)

    q_rows = q_packed.reshape(heads, length, head_size)
    kv_rows = kv_packed.reshape(2, length, head_size)
    factor = float(head_size ** (-0.5) * np.log2(np.e))
    most = min(span // tile + 1, length // tile)

    def one_tile(number, carry):
        q_start = pl.multiple_of(number * tile, tile)
        q_end = q_start + tile

        def scan_docs(d, state):
            first, before, within = state
            begin = begins[d]
            return (
                jnp.where(begin <= q_start, begin, first),
                before + (begin <= q_start).astype(jnp.int32),
                within + (begin < q_end).astype(jnp.int32),
            )

        first, before, within = lax.fori_loop(
            0, docs, scan_docs, (jnp.int32(0), jnp.int32(0), jnp.int32(0))
        )
        q_pos = q_start + lax.broadcasted_iota(jnp.int32, (tile, 1), 0)

        def later_doc(d, firsts):
            return jnp.where(q_pos >= begins[d], begins[d], firsts)

        firsts = lax.fori_loop(before, within, later_doc, jnp.full((tile, 1), first, jnp.int32))
        count = number + 1 - lax.div(first, tile)

        for n in range(1, most + 1):

            @pl.when(count == n)
            def _(n=n):
                keys = n * tile
                k_start = pl.multiple_of(q_end - keys, tile)
                q = q_rows[:, pl.ds(q_start, tile), :].reshape(heads * tile, head_size)
                k = kv_rows[0, pl.ds(k_start, keys), :]
                v = kv_rows[1, pl.ds(k_start, keys), :]
                scores = lax.dot_general(
                    q, k, (((1,), (1,)), ((), ())), preferred_element_type=jnp.float32
                )
                k_pos = k_start + lax.broadcasted_iota(jnp.int32, (tile, keys), 1)
                allowed = (k_pos <= q_pos) & (k_pos >= firsts)
                scores = jnp.where(
                    allowed[None], scores.reshape(heads, tile, keys), far_below
                ).reshape(heads * tile, keys)
                top = jnp.max(scores, axis=1, keepdims=True)
                weights = jnp.exp2(scores * factor - top * factor)
                total = jnp.sum(weights, axis=1, keepdims=True)
                mixed = jnp.dot(
                    weights.astype(jnp.bfloat16), v, preferred_element_type=jnp.float32
                )
                mixed = (mixed * (1.0 / total)).astype(jnp.bfloat16)
                per = tile // rows
                for h in range(heads):
                    for i in range(per):
                        at = h * tile + i * rows
                        out[number * per + i, h] = mixed[at : at + rows]

        return carry

    lax.fori_loop(0, length // tile, one_tile, 0)


def attend(received, other, doc_lengths, plan_dest, plan_slot, swap, heads, span):
    shards, slots, rows, head_size = received.shape
    paired = other is not None
    per = rows // shards
    length = shards * rows
    tile = min(256, length)
    blocks = [received.reshape(shards * slots * shards, per, head_size)]
    if paired:
        blocks.append(other.reshape(shards * shards, per, head_size))
    vmem = pl.BlockSpec(memory_space=pltpu.VMEM)
    smem = pl.BlockSpec(memory_space=pltpu.SMEM)
    return pl.pallas_call(
        functools.partial(
            attend_kernel,
            heads=heads,
            shards=shards,
            rows=rows,
            span=span,
            tile=tile,
            paired=paired,
        ),
        out_shape=jax.ShapeDtypeStruct((shards, heads, rows, head_size), jnp.bfloat16),
        in_specs=[smem] * 4 + [vmem] * len(blocks),
        out_specs=vmem,
        scratch_shapes=[
            pltpu.VMEM((heads, shards * shards, per, head_size), jnp.bfloat16),
            pltpu.VMEM((2, shards * shards, per, head_size), jnp.bfloat16),
            pltpu.SMEM((doc_lengths.shape[0],), jnp.int32),
        ],
        compiler_params=pltpu.CompilerParams(vmem_limit_bytes=40 << 20),
        name="packed_attention",
    )(doc_lengths, plan_dest, plan_slot, swap, *blocks)


def per_device(q_rows, k_rows, v_rows, doc_lengths, plan_dest, plan_slot):
    shards = lax.axis_size("seq")
    my_index = lax.axis_index("seq")
    rows, heads_all, head_size = q_rows.shape
    kv_heads = k_rows.shape[1]
    span = rows * min(8, shards // 2)
    heads = heads_all // shards
    copies = shards // kv_heads
    paired = copies == 2

    q_send = q_rows.reshape(rows, shards, heads, head_size).transpose(1, 2, 0, 3)
    k_heads, v_heads = k_rows.transpose(1, 0, 2), v_rows.transpose(1, 0, 2)
    kv_send = jnp.stack([k_heads, v_heads], axis=1)
    if paired:
        kv_send = kv_send.reshape(shards, 1, rows, head_size)
    else:
        kv_send = jnp.repeat(kv_send, copies, axis=0)
    sent = jnp.concatenate([q_send, kv_send], axis=1)
    received = lax.all_to_all(sent, "seq", split_axis=0, concat_axis=0, tiled=True)
    other = None
    if paired:
        other = lax.ppermute(received[:, heads], "seq", [(i, i ^ 1) for i in range(shards)])
    swap = (my_index % 2).astype(jnp.int32).reshape(1)
    mixed = attend(received, other, doc_lengths, plan_dest, plan_slot, swap, heads, span)
    returned = lax.all_to_all(mixed, "seq", split_axis=0, concat_axis=0, tiled=True)
    return returned.reshape(heads_all, rows, head_size).transpose(1, 0, 2)


def solution(mesh):
    whole = P(("dp", "seq"), None, None)
    return jax.shard_map(
        per_device,
        mesh=mesh,
        in_specs=(whole, whole, whole, P("dp"), P("dp"), P("dp")),
        out_specs=whole,
        check_vma=False,
    )
```

time: 235 us -> 91.2 us (0.39)
  waiting for transfers between devices: 107 us -> 1.54 us
  blocking collectives: 28.7 us -> 72.7 us
  starting transfers between devices: 37.8 us -> 0.84 us
  local copies, waits for them, and re-layouts: 31.2 us -> 3.49 us
  matrix products: 17.9 us -> 0 us
  Pallas kernels: 0 us -> 11.9 us
  other arithmetic: 5.72 us -> 0.19 us
  loops' own time: 5.4 us -> 0 us
    all_to_all x6 -> x0, waiting for transfers between devices: 107 us -> none  [the longest x1 39.9 us: per_device(): lax.all_to_all(spread(q_rows), 'seq', split_axis=0, concat_axis=0, tiled=...]
    all_to_all x1 -> x2, blocking collectives: 28.7 us -> 72.7 us  [the longest x1 43.4 us: per_device(): lax.all_to_all(sent, 'seq', split_axis=0, concat_axis=0, tiled=True)]
    all_to_all x6 -> x0, starting transfers between devices: 37.8 us -> none  [the longest x1 11.2 us: per_device(): lax.all_to_all(packed_k, 'seq', split_axis=1, concat_axis=0, tiled=True)]
    dot_general x22 -> x0, matrix products: 17.9 us -> none  [the longest x8 8.31 us: one_block(): lax.dot_general(rows_query, rows_key, (((1,), (1,)), ((), ())), preferred...]
    pallas_call x0 -> x1, Pallas kernels: none -> 11.9 us  [attend(): pl.pallas_call(functools.partial(attend_kernel, heads=heads, shards=shard...]
    reshape x15 -> x1, local copies, waits for them, and re-layouts: 12.2 us -> 1.65 us  [per_device(): return returned.reshape(heads_all, rows, head_size).transpose(1, 0, 2)]
    another operation x5 -> x1, local copies, waits for them, and re-layouts: 9.7 us -> 0.09 us  [per_device(): kv_send = jnp.stack([k_heads, v_heads], axis=1)]
    another operation x2 -> x0, loops' own time: 5.4 us -> none  [attend(): lax.map(one_block, jnp.arange(length_all // query_block, dtype=jnp.int32))]
  transfers between devices with their start and end apart: 6 -> 1, of which waited for: 6 -> 1; matrix products, arithmetic and copies ran while one was open for 6% -> 0% of each run, Pallas kernels for 0% -> 0%
where the time goes in v1:
time: 91.2 us; the launch traced here: 90.7 us
  blocking collectives  72.7 us (80%)
  Pallas kernels  11.9 us (13%)
  local copies, waits for them, and re-layouts  3.49 us (4%)
  waiting for transfers between devices  1.54 us (2%)
    all_to_all x1, blocking collectives, per_device(): lax.all_to_all(sent, 'seq', split_axis=0, concat_axis=0, tiled=True)  43.4 us
    all_to_all x1, blocking collectives, per_device(): lax.all_to_all(mixed, 'seq', split_axis=0, concat_axis=0, tiled=True)  29.3 us
    pallas_call x1, Pallas kernels, attend(): pl.pallas_call(functools.partial(attend_kernel, heads=heads, shards=shard...  11.9 us
  transfers between devices with their start and end apart: 1, of which 1 were waited for; matrix products, arithmetic and copies ran while one was open for 0% of the time, Pallas kernels for 0%

profile of v1, /device:TPU:0, one launch (start us, length us, event | category | flops | bytes accessed | tf_op | source)
XLA Modules:
  0.0 90.7 jit_solution(84325708734644182)
XLA Ops:
  0.0 0.0 copy-start.3
  0.0 0.0 copy-start.4
  0.0 1.7 %copy.15 = bf16[128,32,128]{2,0,1:T(8,128)(2,1)S(1)} copy(bf16[128,32,128]{2,1,0:T(8,128)(2,1)} %param.6) | data formatting | bytes 2097152 | tf_op args[0]
  1.7 0.0 copy-done.3
  1.7 0.0 copy-done.4
  1.7 0.1 copy_bitcast_fusion.1
  1.8 0.1 pad_maximum_fusion.1
  1.9 0.1 pad_maximum_fusion
  2.0 0.0 copy-start
  2.0 0.0 copy-start.1
  2.0 0.0 copy-start.2
  2.1 43.4 %all_to_all.10 = bf16[16,3,128,128]{3,2,1,0:T(8,128)(2,1)S(1)} all-to-all(bf16[16,3,128,128]{3,2,1,0:T(8,128)(2,1)S(1)} %pad_maximum_fusion), channel_id=1, replica_groups=mesh['dp'=2,'seq'=16] {'seq'}, dimensions={0} | all-to-all | bytes 3145728 | tf_op jit(solution)/shard_map/all_to_all | solution.py:166
  45.5 0.8 collective-permute-start
  46.3 1.5 %collective-permute-done = bf16[16,128,128]{2,1,0:T(8,128)(2,1)S(1)} collective-permute-done((bf16[16,128,128]{2,1,0:T(8,128)(2,1)S(1)}, bf16[16,128,128]{2,1,0:T(8,128)(2,1)S(1)}, u32[]{:S(2)}, u32[]{:S(2)}) %collective-permute-start) | collective-permute-done | bytes 524320 | tf_op jit(solution)/shard_map/ppermute | solution.py:169
  47.8 0.0 copy-done
  47.8 0.0 copy-done.1
  47.9 0.0 copy-done.2
  47.9 11.9 %packed_attention.1 = bf16[16,2,128,128]{3,2,1,0:T(8,128)(2,1)S(1)} custom-call(s32[16]{0:T(128)S(1)} %copy-done.2, s32[256]{0:T(256)S(1)} %copy-done, s32[256]{0:T(256)S(1)} %copy-done.1, s32[1]{0:T(128)} %bitcast.swap, bf16[768,8,128]{2,1,0:T(8,128)(2,1)S(1)} %bitcast.23, bf16[256,8,128]{2,1,0:T(8,128)(2,1)S(1)} %bitcast.24), custom_call_target="tpu_custom_call" | custom-call | tf_op jit(solution)/shard_map/packed_attention/pallas_call | solution.py:125
  59.7 29.3 %all_to_all.11 = bf16[16,2,128,128]{3,2,1,0:T(8,128)(2,1)S(1)} all-to-all(bf16[16,2,128,128]{3,2,1,0:T(8,128)(2,1)S(1)} %packed_attention.1), channel_id=1, replica_groups=mesh['dp'=2,'seq'=16] {'seq'}, dimensions={0} | all-to-all | bytes 2097152 | tf_op jit(solution)/shard_map/all_to_all | solution.py:172
  89.0 1.6 %copy.23 = bf16[32,128,128]{2,0,1:T(8,128)(2,1)} copy(bf16[32,128,128]{2,1,0:T(8,128)(2,1)S(1)} %bitcast.26) | data formatting | bytes 2097152 | tf_op jit(solution)/shard_map/reshape | solution.py:173
  (1 shorter events, 0.0 us)
Async XLA Ops:
  0.0 1.7 %copy-start.3 = (bf16[128,8,128]{2,1,0:T(8,128)(2,1)S(1)}, bf16[128,8,128]{2,1,0:T(8,128)(2,1)}, u32[]{:S(2)}) copy-start(bf16[128,8,128]{2,1,0:T(8,128)(2,1)} %param.8) | copy-start | bytes 786436
  0.0 1.7 %copy-start.4 = (bf16[128,8,128]{2,1,0:T(8,128)(2,1)S(1)}, bf16[128,8,128]{2,1,0:T(8,128)(2,1)}, u32[]{:S(2)}) copy-start(bf16[128,8,128]{2,1,0:T(8,128)(2,1)} %param.7) | copy-start | bytes 786436
  2.0 45.8 %copy-start = (s32[256]{0:T(256)S(1)}, s32[256]{0:T(256)}, u32[]{:S(2)}) copy-start(s32[256]{0:T(256)} %dest.1) | copy-start | bytes 3076
  2.0 45.8 %copy-start.1 = (s32[256]{0:T(256)S(1)}, s32[256]{0:T(256)}, u32[]{:S(2)}) copy-start(s32[256]{0:T(256)} %slot.1) | copy-start | bytes 3076
  2.0 45.8 %copy-start.2 = (s32[16]{0:T(128)S(1)}, s32[16]{0:T(128)}, u32[]{:S(2)}) copy-start(s32[16]{0:T(128)} %lengths.1) | copy-start | bytes 196
  45.5 2.4 %collective-permute-start = (bf16[16,128,128]{2,1,0:T(8,128)(2,1)S(1)}, bf16[16,128,128]{2,1,0:T(8,128)(2,1)S(1)}, u32[]{:S(2)}, u32[]{:S(2)}) collective-permute-start(bf16[16,128,128]{2,1,0:T(8,128)(2,1)S(1)} %slice_bitcast_fusion), channel_id=1, source_target_pairs={{0,1},{1,0},{2,3},{3,2},{4,5},{5,4},{6,7},{7,6},{8,9},{9,8},{10,11... | collective-permute-start | bytes 1572872 | tf_op jit(solution)/shard_map/ppermute | solution.py:169

commit v2 on v1

v2 whole, which is shorter than its diff:
```python
import functools

import jax
import jax.numpy as jnp
import numpy as np
from jax import lax
from jax.experimental import pallas as pl
from jax.experimental.pallas import tpu as pltpu
from jax.sharding import PartitionSpec as P

far_below = -3e38
vmem = pl.BlockSpec(memory_space=pltpu.VMEM)
smem = pl.BlockSpec(memory_space=pltpu.SMEM)
anywhere = pl.BlockSpec(memory_space=pl.ANY)
small = pl.CostEstimate(flops=1000, bytes_accessed=1000, transcendentals=0)


def pack_kernel(place, dest, slot, *refs, groups, heads, shards):
    units = shards // 2
    q_packed, kv_packed = refs[-2:]
    unit, core = place[0], place[1]

    def pack_block(b, carry):
        for (column, aways), blocks in zip(groups, refs):
            for i, away in enumerate(aways):
                at_chip = i * (heads + 2) * shards + b
                source = lax.bitwise_xor(unit, away) * 2 + lax.bitwise_xor(core, column)
                shard, at = dest[source * shards + b], slot[source * shards + b]
                tile = jnp.where(shard % 2 == core, shard // 2, units)
                base = tile * (heads * shards) + at
                for h in range(heads):
                    q_packed[base + h * shards] = blocks[at_chip + h * shards]
                kv_packed[0, shard * shards + at] = blocks[at_chip + heads * shards]
                kv_packed[1, shard * shards + at] = blocks[at_chip + (heads + 1) * shards]
        return carry

    lax.fori_loop(0, shards, pack_block, 0, unroll=4)


def fold(x, op):
    lanes = x[:, :128]
    for i in range(128, x.shape[1], 128):
        lanes = op(lanes, x[:, i : i + 128])
    return lanes


def attend_kernel(place, lengths, q_packed, kv_packed, *refs, away, heads, shards, rows, chunk):
    out, scores, top, total, mixed = refs[-5:]
    length = shards * rows
    head_size = q_packed.shape[-1]
    docs = lengths.shape[0]
    q_rows = q_packed.reshape(q_packed.shape[0] * q_packed.shape[1], head_size)
    kv_rows = kv_packed.reshape(2, length, head_size)
    factor = float(head_size ** (-0.5) * np.log2(np.e))
    tile = lax.bitwise_xor(place[0], away)
    q_start = (tile * 2 + place[1]) * rows
    q_end = q_start + rows

    def scan_docs(d, state):
        begin, first, before, within = state
        first = jnp.where(begin <= q_start, begin, first)
        before = before + (begin <= q_start).astype(jnp.int32)
        within = within + (begin < q_end).astype(jnp.int32)
        return begin + lengths[d], first, before, within

    zero = jnp.int32(0)
    _, first, before, within = lax.fori_loop(0, docs, scan_docs, (zero, zero, zero, zero))
    q_pos = q_start + lax.broadcasted_iota(jnp.int32, (rows, 1), 0)

    def sum_to(d, begin):
        return begin + lengths[d]

    def later_doc(d, state):
        begin, firsts = state
        return begin + lengths[d], jnp.where(q_pos >= begin, begin, firsts)

    _, firsts = lax.fori_loop(
        before,
        within,
        later_doc,
        (lax.fori_loop(0, before, sum_to, zero), jnp.full((rows, 1), first, jnp.int32)),
    )
    chunks = lax.div(q_end - first + chunk - 1, chunk)
    start = jnp.maximum(q_end - chunks * chunk, 0)
    q = q_rows[pl.ds(pl.multiple_of(tile * (heads * rows), rows), heads * rows), :]
    top[...] = jnp.full_like(top, far_below)

    def score_chunk(j, carry):
        k_start = pl.multiple_of(start + j * chunk, rows)
        k = kv_rows[0, pl.ds(k_start, chunk), :]
        s = lax.dot_general(q, k, (((1,), (1,)), ((), ())), preferred_element_type=jnp.float32)
        k_pos = k_start + lax.broadcasted_iota(jnp.int32, (rows, chunk), 1)
        allowed = (k_pos <= q_pos) & (k_pos >= firsts)
        s = jnp.where(allowed[None], s.reshape(heads, rows, chunk), far_below)
        s = s.reshape(heads * rows, chunk)
        scores[j] = s
        top[...] = jnp.maximum(top[...], fold(s, jnp.maximum))
        return carry

    lax.fori_loop(0, chunks, score_chunk, 0)
    top[...] = jnp.broadcast_to(jnp.max(top[...], axis=1, keepdims=True) * factor, top.shape)
    total[...] = jnp.zeros_like(total)
    mixed[...] = jnp.zeros_like(mixed)

    def mix_chunk(j, carry):
        v = kv_rows[1, pl.ds(pl.multiple_of(start + j * chunk, rows), chunk), :]
        shift = jnp.concatenate([top[...]] * (chunk // 128), axis=1)
        weights = jnp.exp2(scores[j] * factor - shift)
        total[...] += fold(weights, jnp.add)
        mixed[...] += jnp.dot(weights.astype(jnp.bfloat16), v, preferred_element_type=jnp.float32)
        return carry

    lax.fori_loop(0, chunks, mix_chunk, 0)
    sums = jnp.sum(total[...], axis=1, keepdims=True)
    out[...] = (mixed[...] * (1.0 / sums)).astype(jnp.bfloat16).reshape(out.shape)


def per_device(q_rows, k_rows, v_rows, doc_lengths, plan_dest, plan_slot):
    shards = lax.axis_size("seq")
    my_index = lax.axis_index("seq")
    rows, heads_all, head_size = q_rows.shape
    kv_heads = k_rows.shape[1]
    per = rows // shards
    span = rows * min(8, shards // 2)
    units = shards // 2
    unit, core = my_index // 2, my_index % 2
    heads = heads_all // units
    copies = units // kv_heads
    place = jnp.stack([unit, core]).astype(jnp.int32)

    q_send = q_rows.reshape(rows, units, heads, head_size).transpose(1, 2, 0, 3)
    kv_send = jnp.stack([k_rows, v_rows], axis=0).transpose(2, 0, 1, 3)
    kv_send = jnp.repeat(kv_send, copies, axis=0)
    sent = jnp.concatenate([q_send, kv_send], axis=1)

    def hop(x, distance):
        return lax.ppermute(x, "seq", [(i, i ^ distance) for i in range(shards)])

    def part(away):
        return lax.dynamic_index_in_dim(sent, unit ^ away, 0, keepdims=False)

    near = {away: part(away) for away in reversed(range(units))}
    for away in reversed(range(1, units)):
        near[away] = hop(near[away], 2 * away)
    half = units // 2
    far = {away: hop(near[away], 1) for away in range(units)}

    packed_shapes = (
        jax.ShapeDtypeStruct(((units + 1) * heads * shards, per, head_size), jnp.bfloat16),
        jax.ShapeDtypeStruct((2, shards * shards, per, head_size), jnp.bfloat16),
    )

    def pack(groups, arrays, packed, cost):
        blocks = [x.reshape(-1, per, head_size) for x in arrays]
        count = 3 + len(blocks)
        return pl.pallas_call(
            functools.partial(pack_kernel, groups=groups, heads=heads, shards=shards),
            out_shape=packed_shapes,
            in_specs=[smem] * 3 + [vmem] * (len(blocks) + len(packed)),
            out_specs=(vmem, vmem),
            input_output_aliases={count: 0, count + 1: 1} if packed else {},
            compiler_params=pltpu.CompilerParams(vmem_limit_bytes=24 << 20),
            cost_estimate=cost,
            name="pack_blocks",
        )(place, plan_dest, plan_slot, *blocks, *packed)

    everyone = list(range(units))
    groups = [(column, (away,)) for column in range(2) for away in everyone]
    packed = pack(groups, [x[away] for x in (near, far) for away in everyone], (), small)

    chunk = min(256, span)
    most = -(-(span + rows - 1) // chunk)
    tiles = {}
    sequence = list(reversed(range(units)))
    for turn, away in enumerate(sequence):
        after = []
        if 2 <= turn < half:
            after = [tiles[sequence[turn - 2]]]
        elif turn >= half:
            after = [tiles[sequence[half - 3 + (turn - half) * 2 // half]]]
        out = pl.pallas_call(
            functools.partial(
                attend_kernel, away=away, heads=heads, shards=shards, rows=rows, chunk=chunk
            ),
            out_shape=jax.ShapeDtypeStruct((heads, rows, head_size), jnp.bfloat16),
            in_specs=[smem] * 2 + [vmem] * 2 + [anywhere] * len(after),
            out_specs=vmem,
            scratch_shapes=[
                pltpu.VMEM((most, heads * rows, chunk), jnp.float32),
                pltpu.VMEM((heads * rows, 128), jnp.float32),
                pltpu.VMEM((heads * rows, 128), jnp.float32),
                pltpu.VMEM((heads * rows, head_size), jnp.float32),
            ],
            compiler_params=pltpu.CompilerParams(vmem_limit_bytes=24 << 20),
            cost_estimate=small,
            name="attend",
        )(place, doc_lengths, *packed, *after)
        tiles[away] = hop(out, 2 * away) if away else out
    gathered = jnp.zeros((units, heads, rows, head_size), jnp.bfloat16)
    for away in range(units):
        gathered = lax.dynamic_update_index_in_dim(gathered, tiles[away], unit ^ away, 0)
    return gathered.reshape(heads_all, rows, head_size).transpose(1, 0, 2)


def solution(mesh):
    whole = P(("dp", "seq"), None, None)
    return jax.shard_map(
        per_device,
        mesh=mesh,
        in_specs=(whole, whole, whole, P("dp"), P("dp"), P("dp")),
        out_specs=whole,
        check_vma=False,
    )
```

time: 91.2 us -> 85.5 us (0.938)
  blocking collectives: 72.7 us -> 0 us
  starting transfers between devices: 0.84 us -> 36.7 us
  waiting for transfers between devices: 1.54 us -> 21.6 us
  Pallas kernels: 11.9 us -> 21.2 us
  other arithmetic: 0.19 us -> 1.39 us
    all_to_all x2 -> x0, blocking collectives: 72.7 us -> none  [the longest x1 43.4 us: per_device(): lax.all_to_all(sent, 'seq', split_axis=0, concat_axis=0, tiled=True)]
    ppermute x1 -> x22, starting transfers between devices: 0.84 us -> 36.7 us  [hop(): return lax.ppermute(x, 'seq', [(i, i ^ distance) for i in range(shards)])]
    ppermute x1 -> x22, waiting for transfers between devices: 1.54 us -> 21.6 us  [hop(): return lax.ppermute(x, 'seq', [(i, i ^ distance) for i in range(shards)])]
    pallas_call x1 -> x9, Pallas kernels: 11.9 us -> 21.2 us  [the longest x8 17.6 us: per_device(): pl.pallas_call(functools.partial(attend_kernel, away=away, heads=heads, s...]
    dynamic_update_slice x0 -> x9, local copies, waits for them, and re-layouts: none -> 1.25 us  [per_device(): lax.dynamic_update_index_in_dim(gathered, tiles[away], unit ^ away, 0)]
    reshape x1, local copies, waits for them, and re-layouts: 1.65 us -> 0.41 us  [per_device(): q_send = q_rows.reshape(rows, units, heads, head_size).transpose(1, 2, 0, 3)]
    transpose x0 -> x1, other arithmetic: none -> 1.17 us  [per_device(): kv_send = jnp.stack([k_rows, v_rows], axis=0).transpose(2, 0, 1, 3)]
  transfers between devices with their start and end apart: 1 -> 22, of which waited for: 1 -> 9; matrix products, arithmetic and copies ran while one was open for 0% -> 1% of each run, Pallas kernels for 0% -> 17%
where the time goes in v2:
time: 85.5 us; the launch traced here: 84.1 us
  starting transfers between devices  36.7 us (43%)
  waiting for transfers between devices  21.6 us (25%)
  Pallas kernels  21.2 us (25%)
  local copies, waits for them, and re-layouts  3.07 us (4%)
  other arithmetic  1.39 us (2%)
    ppermute x22, starting transfers between devices, hop(): return lax.ppermute(x, 'seq', [(i, i ^ distance) for i in range(shards)])  36.7 us
    ppermute x22, waiting for transfers between devices, hop(): return lax.ppermute(x, 'seq', [(i, i ^ distance) for i in range(shards)])  21.6 us
    pallas_call x8, Pallas kernels, per_device(): pl.pallas_call(functools.partial(attend_kernel, away=away, heads=heads, s...  17.6 us
    pallas_call x1, Pallas kernels, pack(): pl.pallas_call(functools.partial(pack_kernel, groups=groups, heads=heads,...  3.62 us
  transfers between devices with their start and end apart: 22, of which 9 were waited for; matrix products, arithmetic and copies ran while one was open for 1% of the time, Pallas kernels for 17%

profile of v2, /device:TPU:0, one launch (start us, length us, event | category | flops | bytes accessed | tf_op | source)
XLA Modules:
  0.0 84.1 jit_solution(4024779155116637951)
XLA Ops:
  0.0 1.2 %maximum_bitcast_fusion = bf16[8,2,128,128]{3,0,2,1:T(8,128)(2,1)S(1)} fusion(bf16[1,128,8,128]{3,2,1,0:T(8,128)(2,1)} %bitcast.80, bf16[1,128,8,128]{3,2,1,0:T(8,128)(2,1)} %bitcast.81), kind=kLoop, calls=%fused_computation.17 | loop fusion | flops 262144 | bytes 1048576 | tf_op jit(solution)/shard_map/transpose | solution.py:132
  1.2 0.1 copy.8
  1.3 0.1 copy-done.3
  1.4 0.4 copy.15
  1.9 5.1 %collective-permute-start.5 = (bf16[6,128,128]{2,1,0:T(8,128)(2,1)S(1)}, bf16[6,128,128]{2,1,0:T(8,128)(2,1)S(1)}, u32[]{:S(2)}, u32[]{:S(2)}) collective-permute-start(bf16[6,128,128]{2,1,0:T(8,128)(2,1)S(1)} %get-tuple-element.15), channel_id=1, source_target_pairs={{0,12},{1,13},{2,14},{3,15},{4,8},{5,9},{6,10},{7,11},{8,4},{9,5},... | collective-permute-start | bytes 589832 | tf_op jit(solution)/shard_map/ppermute | solution.py:137
  7.0 0.4 collective-permute-start.4
  7.3 0.1 fusion.14
  7.4 2.5 %collective-permute-start.6 = (bf16[6,128,128]{2,1,0:T(8,128)(2,1)S(1)}, bf16[6,128,128]{2,1,0:T(8,128)(2,1)S(1)}, u32[]{:S(2)}, u32[]{:S(2)}) collective-permute-start(bf16[6,128,128]{2,1,0:T(8,128)(2,1)S(1)} %get-tuple-element.9), channel_id=1, source_target_pairs={{0,14},{1,15},{2,12},{3,13},{4,10},{5,11},{6,8},{7,9},{8,6},{9,7},... | collective-permute-start | bytes 589832 | tf_op jit(solution)/shard_map/ppermute | solution.py:137
  10.0 1.5 %collective-permute-start = (bf16[6,128,128]{2,1,0:T(8,128)(2,1)S(1)}, bf16[6,128,128]{2,1,0:T(8,128)(2,1)S(1)}, u32[]{:S(2)}, u32[]{:S(2)}) collective-permute-start(bf16[6,128,128]{2,1,0:T(8,128)(2,1)S(1)} %get-tuple-element.11), channel_id=1, source_target_pairs={{0,2},{1,3},{2,0},{3,1},{4,6},{5,7},{6,4},{7,5},{8,10},{9,11},{10,... | collective-permute-start | bytes 589832 | tf_op jit(solution)/shard_map/ppermute | solution.py:137
  11.4 1.6 %collective-permute-start.1 = (bf16[6,128,128]{2,1,0:T(8,128)(2,1)S(1)}, bf16[6,128,128]{2,1,0:T(8,128)(2,1)S(1)}, u32[]{:S(2)}, u32[]{:S(2)}) collective-permute-start(bf16[6,128,128]{2,1,0:T(8,128)(2,1)S(1)} %get-tuple-element.12), channel_id=1, source_target_pairs={{0,4},{1,5},{2,6},{3,7},{4,0},{5,1},{6,2},{7,3},{8,12},{9,13},{10,... | collective-permute-start | bytes 589832 | tf_op jit(solution)/shard_map/ppermute | solution.py:137
  13.0 13.1 %collective-permute-start.2 = (bf16[6,128,128]{2,1,0:T(8,128)(2,1)S(1)}, bf16[6,128,128]{2,1,0:T(8,128)(2,1)S(1)}, u32[]{:S(2)}, u32[]{:S(2)}) collective-permute-start(bf16[6,128,128]{2,1,0:T(8,128)(2,1)S(1)} %get-tuple-element.13), channel_id=1, source_target_pairs={{0,6},{1,7},{2,4},{3,5},{4,2},{5,3},{6,0},{7,1},{8,14},{9,15},{10,... | collective-permute-start | bytes 589832 | tf_op jit(solution)/shard_map/ppermute | solution.py:137
  26.1 3.7 %collective-permute-done.4 = bf16[6,128,128]{2,1,0:T(8,128)(2,1)S(1)} collective-permute-done((bf16[6,128,128]{2,1,0:T(8,128)(2,1)S(1)}, bf16[6,128,128]{2,1,0:T(8,128)(2,1)S(1)}, u32[]{:S(2)}, u32[]{:S(2)}) %collective-permute-start.4) | collective-permute-done | bytes 196640 | tf_op jit(solution)/shard_map/ppermute | solution.py:137
  29.8 0.5 collective-permute-start.13
  30.3 0.1 collective-permute-start.12
  30.4 2.4 %collective-permute-done.2 = bf16[6,128,128]{2,1,0:T(8,128)(2,1)S(1)} collective-permute-done((bf16[6,128,128]{2,1,0:T(8,128)(2,1)S(1)}, bf16[6,128,128]{2,1,0:T(8,128)(2,1)S(1)}, u32[]{:S(2)}, u32[]{:S(2)}) %collective-permute-start.2) | collective-permute-done | bytes 196640 | tf_op jit(solution)/shard_map/ppermute | solution.py:137
  32.8 8.7 %collective-permute-done.3 = bf16[6,128,128]{2,1,0:T(8,128)(2,1)S(1)} collective-permute-done((bf16[6,128,128]{2,1,0:T(8,128)(2,1)S(1)}, bf16[6,128,128]{2,1,0:T(8,128)(2,1)S(1)}, u32[]{:S(2)}, u32[]{:S(2)}) %collective-permute-start.3) | collective-permute-done | bytes 196640 | tf_op jit(solution)/shard_map/ppermute | solution.py:137
  41.5 0.5 collective-permute-start.9
  42.0 0.1 collective-permute-start.10
  42.1 0.4 collective-permute-start.11
  42.6 0.1 pad_add_fusion.place
  42.6 0.3 collective-permute-done.8
  43.0 0.3 collective-permute-done.9
  43.2 0.3 collective-permute-done.10
  43.5 0.3 collective-permute-done.11
  43.8 3.6 %pack_blocks.1 = (bf16[576,8,128]{2,1,0:T(8,128)(2,1)S(1)}, bf16[2,256,8,128]{3,2,1,0:T(8,128)(2,1)S(1)}) custom-call(s32[2]{0:T(128)S(1)} %pad_add_fusion.place, s32[256]{0:T(256)S(1)} %copy-done.1, s32[256]{0:T(256)S(1)} %copy-done.2, bf16[96,8,128]{2,1,0:T(8,128)(2,1)S(1)} %bitcast.60, bf16[96,8,128]{2,1,0:T(8,128)(2,1)S(1)} %bitcast.65, ...), custom_call_target="tpu_custom_call" | custom-call | flops 1000 | bytes 1000 | tf_op jit(solution)/shard_map/pack_blocks/pallas_call | solution.py:156
  47.5 3.5 %attend.8 = bf16[4,128,128]{2,1,0:T(8,128)(2,1)S(1)} custom-call(s32[2]{0:T(128)S(1)} %pad_add_fusion.place, s32[16]{0:T(128)S(1)} %copy-done, bf16[576,8,128]{2,1,0:T(8,128)(2,1)S(1)} %get-tuple-element.7.q_packed, bf16[2,256,8,128]{3,2,1,0:T(8,128)(2,1)S(1)} %get-tuple-element.8.kv_packed), custom_call_target="tpu_custom_call" | custom-call | flops 1000 | bytes 1000 | tf_op jit(solution)/shard_map/attend/pallas_call | solution.py:181
  50.9 0.6 collective-permute-start.15
  51.5 3.0 %attend.12 = bf16[4,128,128]{2,1,0:T(8,128)(2,1)S(1)} custom-call(s32[2]{0:T(128)S(1)} %pad_add_fusion.place, s32[16]{0:T(128)S(1)} %copy-done, bf16[576,8,128]{2,1,0:T(8,128)(2,1)S(1)} %get-tuple-element.7.q_packed, bf16[2,256,8,128]{3,2,1,0:T(8,128)(2,1)S(1)} %get-tuple-element.8.kv_packed), custom_call_target="tpu_custom_call" | custom-call | flops 1000 | bytes 1000 | tf_op jit(solution)/shard_map/attend/pallas_call | solution.py:181
  54.5 1.9 %collective-permute-start.18 = (bf16[4,128,128]{2,1,0:T(8,128)(2,1)S(1)}, bf16[4,128,128]{2,1,0:T(8,128)(2,1)S(1)}, u32[]{:S(2)}, u32[]{:S(2)}) collective-permute-start(bf16[4,128,128]{2,1,0:T(8,128)(2,1)S(1)} %attend.12), channel_id=1, source_target_pairs={{0,12},{1,13},{2,14},{3,15},{4,8},{5,9},{6,10},{7,11},{8,4},{9,5},... | collective-permute-start | bytes 393224 | tf_op jit(solution)/shard_map/ppermute | solution.py:137
  56.3 3.3 %collective-permute-done.15.refs_0_ = bf16[4,128,128]{2,1,0:T(8,128)(2,1)S(1)} collective-permute-done((bf16[4,128,128]{2,1,0:T(8,128)(2,1)S(1)}, bf16[4,128,128]{2,1,0:T(8,128)(2,1)S(1)}, u32[]{:S(2)}, u32[]{:S(2)}) %collective-permute-start.15) | collective-permute-done | bytes 131104 | tf_op jit(solution)/shard_map/ppermute | solution.py:137
  59.6 2.5 %attend.9 = bf16[4,128,128]{2,1,0:T(8,128)(2,1)S(1)} custom-call(s32[2]{0:T(128)S(1)} %pad_add_fusion.place, s32[16]{0:T(128)S(1)} %copy-done, bf16[576,8,128]{2,1,0:T(8,128)(2,1)S(1)} %get-tuple-element.7.q_packed, bf16[2,256,8,128]{3,2,1,0:T(8,128)(2,1)S(1)} %get-tuple-element.8.kv_packed, bf16[4,128,128]{2,1,0:T(8,128)(2,1)S(1)} %collective-permute-done.15.refs_0_), custom_call_target="tpu_custom_call" | custom-call | flops 1000 | bytes 1000 | tf_op jit(solution)/shard_map/attend/pallas_call | solution.py:181
  62.1 0.1 collective-permute-start.16
  62.2 0.0 collective-permute-done.18.refs_0_
  62.2 1.6 %attend.13 = bf16[4,128,128]{2,1,0:T(8,128)(2,1)S(1)} custom-call(s32[2]{0:T(128)S(1)} %pad_add_fusion.place, s32[16]{0:T(128)S(1)} %copy-done, bf16[576,8,128]{2,1,0:T(8,128)(2,1)S(1)} %get-tuple-element.7.q_packed, bf16[2,256,8,128]{3,2,1,0:T(8,128)(2,1)S(1)} %get-tuple-element.8.kv_packed, bf16[4,128,128]{2,1,0:T(8,128)(2,1)S(1)} %collective-permute-done.18.refs_0_), custom_call_target="tpu_custom_call" | custom-call | flops 1000 | bytes 1000 | tf_op jit(solution)/shard_map/attend/pallas_call | solution.py:181
  63.8 4.3 %collective-permute-start.19 = (bf16[4,128,128]{2,1,0:T(8,128)(2,1)S(1)}, bf16[4,128,128]{2,1,0:T(8,128)(2,1)S(1)}, u32[]{:S(2)}, u32[]{:S(2)}) collective-permute-start(bf16[4,128,128]{2,1,0:T(8,128)(2,1)S(1)} %attend.13), channel_id=1, source_target_pairs={{0,4},{1,5},{2,6},{3,7},{4,0},{5,1},{6,2},{7,3},{8,12},{9,13},{10,... | collective-permute-start | bytes 393224 | tf_op jit(solution)/shard_map/ppermute | solution.py:137
  68.1 2.0 %attend.14 = bf16[4,128,128]{2,1,0:T(8,128)(2,1)S(1)} custom-call(s32[2]{0:T(128)S(1)} %pad_add_fusion.place, s32[16]{0:T(128)S(1)} %copy-done, bf16[576,8,128]{2,1,0:T(8,128)(2,1)S(1)} %get-tuple-element.7.q_packed, bf16[2,256,8,128]{3,2,1,0:T(8,128)(2,1)S(1)} %get-tuple-element.8.kv_packed, bf16[4,128,128]{2,1,0:T(8,128)(2,1)S(1)} %collective-permute-done.18.refs_0_), custom_call_target="tpu_custom_call" | custom-call | flops 1000 | bytes 1000 | tf_op jit(solution)/shard_map/attend/pallas_call | solution.py:181
  70.2 0.1 collective-permute-start.20
  70.2 2.0 %attend.15 = bf16[4,128,128]{2,1,0:T(8,128)(2,1)S(1)} custom-call(s32[2]{0:T(128)S(1)} %pad_add_fusion.place, s32[16]{0:T(128)S(1)} %copy-done, bf16[576,8,128]{2,1,0:T(8,128)(2,1)S(1)} %get-tuple-element.7.q_packed, bf16[2,256,8,128]{3,2,1,0:T(8,128)(2,1)S(1)} %get-tuple-element.8.kv_packed, bf16[4,128,128]{2,1,0:T(8,128)(2,1)S(1)} %collective-permute-done.18.refs_0_), custom_call_target="tpu_custom_call" | custom-call | flops 1000 | bytes 1000 | tf_op jit(solution)/shard_map/attend/pallas_call | solution.py:181
  72.3 3.0 %collective-permute-start.21 = (bf16[4,128,128]{2,1,0:T(8,128)(2,1)S(1)}, bf16[4,128,128]{2,1,0:T(8,128)(2,1)S(1)}, u32[]{:S(2)}, u32[]{:S(2)}) collective-permute-start(bf16[4,128,128]{2,1,0:T(8,128)(2,1)S(1)} %attend.15), channel_id=1, source_target_pairs={{0,8},{1,9},{2,10},{3,11},{4,12},{5,13},{6,14},{7,15},{8,0},{9,1},... | collective-permute-start | bytes 393224 | tf_op jit(solution)/shard_map/ppermute | solution.py:137
  75.3 1.5 %attend.11 = bf16[4,128,128]{2,1,0:T(8,128)(2,1)S(1)} custom-call(s32[2]{0:T(128)S(1)} %pad_add_fusion.place, s32[16]{0:T(128)S(1)} %copy-done, bf16[576,8,128]{2,1,0:T(8,128)(2,1)S(1)} %get-tuple-element.7.q_packed, bf16[2,256,8,128]{3,2,1,0:T(8,128)(2,1)S(1)} %get-tuple-element.8.kv_packed, bf16[4,128,128]{2,1,0:T(8,128)(2,1)S(1)} %collective-permute-done.16.refs_0_), custom_call_target="tpu_custom_call" | custom-call | flops 1000 | bytes 1000 | tf_op jit(solution)/shard_map/attend/pallas_call | solution.py:181
  76.8 1.0 %collective-permute-start.17 = (bf16[4,128,128]{2,1,0:T(8,128)(2,1)S(1)}, bf16[4,128,128]{2,1,0:T(8,128)(2,1)S(1)}, u32[]{:S(2)}, u32[]{:S(2)}) collective-permute-start(bf16[4,128,128]{2,1,0:T(8,128)(2,1)S(1)} %attend.11), channel_id=1, source_target_pairs={{0,2},{1,3},{2,0},{3,1},{4,6},{5,7},{6,4},{7,5},{8,10},{9,11},{10,... | collective-permute-start | bytes 393224 | tf_op jit(solution)/shard_map/ppermute | solution.py:137
  77.8 1.5 %attend.10 = bf16[4,128,128]{2,1,0:T(8,128)(2,1)S(1)} custom-call(s32[2]{0:T(128)S(1)} %pad_add_fusion.place, s32[16]{0:T(128)S(1)} %copy-done, bf16[576,8,128]{2,1,0:T(8,128)(2,1)S(1)} %get-tuple-element.7.q_packed, bf16[2,256,8,128]{3,2,1,0:T(8,128)(2,1)S(1)} %get-tuple-element.8.kv_packed, bf16[4,128,128]{2,1,0:T(8,128)(2,1)S(1)} %collective-permute-done.16.refs_0_), custom_call_target="tpu_custom_call" | custom-call | flops 1000 | bytes 1000 | tf_op jit(solution)/shard_map/attend/pallas_call | solution.py:181
  79.3 0.2 broadcast_in_dim.28
  79.6 2.2 %collective-permute-done.17 = bf16[4,128,128]{2,1,0:T(8,128)(2,1)S(1)} collective-permute-done((bf16[4,128,128]{2,1,0:T(8,128)(2,1)S(1)}, bf16[4,128,128]{2,1,0:T(8,128)(2,1)S(1)}, u32[]{:S(2)}, u32[]{:S(2)}) %collective-permute-start.17) | collective-permute-done | bytes 131104 | tf_op jit(solution)/shard_map/ppermute | solution.py:137
  82.0 0.8 copy.9
  82.8 0.2 copy_dynamic-update-slice_fusion.1
  83.0 0.2 copy_dynamic-update-slice_fusion
  83.2 1.0 %copy-done.4 = bf16[8,4,128,128]{3,1,0,2:T(4,128)(2,1)} copy-done((bf16[8,4,128,128]{3,1,0,2:T(4,128)(2,1)}, bf16[8,4,128,128]{3,1,0,2:T(4,128)(2,1)S(1)}, u32[]{:S(2)}) %copy-start.4) | copy-done | bytes 1048600
  (31 shorter events, 0.2 us)
Async XLA Ops:
  0.0 1.4 %copy-start.3 = (bf16[128,32,128]{2,1,0:T(8,128)(2,1)S(1)}, bf16[128,32,128]{2,1,0:T(8,128)(2,1)}, u32[]{:S(2)}) copy-start(bf16[128,32,128]{2,1,0:T(8,128)(2,1)} %param.6) | copy-start | bytes 3145732
  1.9 11.2 %collective-permute-start.5 = (bf16[6,128,128]{2,1,0:T(8,128)(2,1)S(1)}, bf16[6,128,128]{2,1,0:T(8,128)(2,1)S(1)}, u32[]{:S(2)}, u32[]{:S(2)}) collective-permute-start(bf16[6,128,128]{2,1,0:T(8,128)(2,1)S(1)} %get-tuple-element.15), channel_id=1, source_target_pairs={{0,12},{1,13},{2,14},{3,15},{4,8},{5,9},{6,10},{7,11},{8,4},{9,5},... | collective-permute-start | bytes 589832 | tf_op jit(solution)/shard_map/ppermute | solution.py:137
  7.0 22.8 %collective-permute-start.4 = (bf16[6,128,128]{2,1,0:T(8,128)(2,1)S(1)}, bf16[6,128,128]{2,1,0:T(8,128)(2,1)S(1)}, u32[]{:S(2)}, u32[]{:S(2)}) collective-permute-start(bf16[6,128,128]{2,1,0:T(8,128)(2,1)S(1)} %get-tuple-element.16), channel_id=1, source_target_pairs={{0,10},{1,11},{2,8},{3,9},{4,14},{5,15},{6,12},{7,13},{8,2},{9,3},... | collective-permute-start | bytes 589832 | tf_op jit(solution)/shard_map/ppermute | solution.py:137
  7.3 36.5 %copy-start.1 = (s32[256]{0:T(256)S(1)}, s32[256]{0:T(256)}, u32[]{:S(2)}) copy-start(s32[256]{0:T(256)} %dest.1) | copy-start | bytes 3076
  7.3 36.5 %copy-start.2 = (s32[256]{0:T(256)S(1)}, s32[256]{0:T(256)}, u32[]{:S(2)}) copy-start(s32[256]{0:T(256)} %slot.1) | copy-start | bytes 3076
  7.4 22.4 %collective-permute-start.6 = (bf16[6,128,128]{2,1,0:T(8,128)(2,1)S(1)}, bf16[6,128,128]{2,1,0:T(8,128)(2,1)S(1)}, u32[]{:S(2)}, u32[]{:S(2)}) collective-permute-start(bf16[6,128,128]{2,1,0:T(8,128)(2,1)S(1)} %get-tuple-element.9), channel_id=1, source_target_pairs={{0,14},{1,15},{2,12},{3,13},{4,10},{5,11},{6,8},{7,9},{8,6},{9,7},... | collective-permute-start | bytes 589832 | tf_op jit(solution)/shard_map/ppermute | solution.py:137
  10.0 19.9 %collective-permute-start = (bf16[6,128,128]{2,1,0:T(8,128)(2,1)S(1)}, bf16[6,128,128]{2,1,0:T(8,128)(2,1)S(1)}, u32[]{:S(2)}, u32[]{:S(2)}) collective-permute-start(bf16[6,128,128]{2,1,0:T(8,128)(2,1)S(1)} %get-tuple-element.11), channel_id=1, source_target_pairs={{0,2},{1,3},{2,0},{3,1},{4,6},{5,7},{6,4},{7,5},{8,10},{9,11},{10,... | collective-permute-start | bytes 589832 | tf_op jit(solution)/shard_map/ppermute | solution.py:137
  11.4 18.9 %collective-permute-start.1 = (bf16[6,128,128]{2,1,0:T(8,128)(2,1)S(1)}, bf16[6,128,128]{2,1,0:T(8,128)(2,1)S(1)}, u32[]{:S(2)}, u32[]{:S(2)}) collective-permute-start(bf16[6,128,128]{2,1,0:T(8,128)(2,1)S(1)} %get-tuple-element.12), channel_id=1, source_target_pairs={{0,4},{1,5},{2,6},{3,7},{4,0},{5,1},{6,2},{7,3},{8,12},{9,13},{10,... | collective-permute-start | bytes 589832 | tf_op jit(solution)/shard_map/ppermute | solution.py:137
  13.0 19.8 %collective-permute-start.2 = (bf16[6,128,128]{2,1,0:T(8,128)(2,1)S(1)}, bf16[6,128,128]{2,1,0:T(8,128)(2,1)S(1)}, u32[]{:S(2)}, u32[]{:S(2)}) collective-permute-start(bf16[6,128,128]{2,1,0:T(8,128)(2,1)S(1)} %get-tuple-element.13), channel_id=1, source_target_pairs={{0,6},{1,7},{2,4},{3,5},{4,2},{5,3},{6,0},{7,1},{8,14},{9,15},{10,... | collective-permute-start | bytes 589832 | tf_op jit(solution)/shard_map/ppermute | solution.py:137
  29.8 11.7 %collective-permute-start.3 = (bf16[6,128,128]{2,1,0:T(8,128)(2,1)S(1)}, bf16[6,128,128]{2,1,0:T(8,128)(2,1)S(1)}, u32[]{:S(2)}, u32[]{:S(2)}) collective-permute-start(bf16[6,128,128]{2,1,0:T(8,128)(2,1)S(1)} %get-tuple-element.14), channel_id=1, source_target_pairs={{0,8},{1,9},{2,10},{3,11},{4,12},{5,13},{6,14},{7,15},{8,0},{9,1},... | collective-permute-start | bytes 589832 | tf_op jit(solution)/shard_map/ppermute | solution.py:137
  29.8 11.7 %collective-permute-start.7 = (bf16[6,128,128]{2,1,0:T(8,128)(2,1)S(1)}, bf16[6,128,128]{2,1,0:T(8,128)(2,1)S(1)}, u32[]{:S(2)}, u32[]{:S(2)}) collective-permute-start(bf16[6,128,128]{2,1,0:T(8,128)(2,1)S(1)} %bitcast.59), channel_id=1, source_target_pairs={{0,1},{1,0},{2,3},{3,2},{4,5},{5,4},{6,7},{7,6},{8,9},{9,8},{10,11... | collective-permute-start | bytes 589832 | tf_op jit(solution)/shard_map/ppermute | solution.py:137
  29.8 12.2 %collective-permute-start.13 = (bf16[6,128,128]{2,1,0:T(8,128)(2,1)S(1)}, bf16[6,128,128]{2,1,0:T(8,128)(2,1)S(1)}, u32[]{:S(2)}, u32[]{:S(2)}) collective-permute-start(bf16[6,128,128]{2,1,0:T(8,128)(2,1)S(1)} %collective-permute-done.5), channel_id=1, source_target_pairs={{0,1},{1,0},{2,3},{3,2},{4,5},{5,4},{6,7},{7,6},{8,9},{9,8},{10,11... | collective-permute-start | bytes 589832 | tf_op jit(solution)/shard_map/ppermute | solution.py:137
  30.3 11.8 %collective-permute-start.12 = (bf16[6,128,128]{2,1,0:T(8,128)(2,1)S(1)}, bf16[6,128,128]{2,1,0:T(8,128)(2,1)S(1)}, u32[]{:S(2)}, u32[]{:S(2)}) collective-permute-start(bf16[6,128,128]{2,1,0:T(8,128)(2,1)S(1)} %collective-permute-done.4), channel_id=1, source_target_pairs={{0,1},{1,0},{2,3},{3,2},{4,5},{5,4},{6,7},{7,6},{8,9},{9,8},{10,11... | collective-permute-start | bytes 589832 | tf_op jit(solution)/shard_map/ppermute | solution.py:137
  32.8 9.8 %collective-permute-start.14 = (bf16[6,128,128]{2,1,0:T(8,128)(2,1)S(1)}, bf16[6,128,128]{2,1,0:T(8,128)(2,1)S(1)}, u32[]{:S(2)}, u32[]{:S(2)}) collective-permute-start(bf16[6,128,128]{2,1,0:T(8,128)(2,1)S(1)} %collective-permute-done.6), channel_id=1, source_target_pairs={{0,1},{1,0},{2,3},{3,2},{4,5},{5,4},{6,7},{7,6},{8,9},{9,8},{10,11... | collective-permute-start | bytes 589832 | tf_op jit(solution)/shard_map/ppermute | solution.py:137
  41.5 1.4 %collective-permute-start.8 = (bf16[6,128,128]{2,1,0:T(8,128)(2,1)S(1)}, bf16[6,128,128]{2,1,0:T(8,128)(2,1)S(1)}, u32[]{:S(2)}, u32[]{:S(2)}) collective-permute-start(bf16[6,128,128]{2,1,0:T(8,128)(2,1)S(1)} %collective-permute-done), channel_id=1, source_target_pairs={{0,1},{1,0},{2,3},{3,2},{4,5},{5,4},{6,7},{7,6},{8,9},{9,8},{10,11... | collective-permute-start | bytes 589832 | tf_op jit(solution)/shard_map/ppermute | solution.py:137
  41.5 1.7 %collective-permute-start.9 = (bf16[6,128,128]{2,1,0:T(8,128)(2,1)S(1)}, bf16[6,128,128]{2,1,0:T(8,128)(2,1)S(1)}, u32[]{:S(2)}, u32[]{:S(2)}) collective-permute-start(bf16[6,128,128]{2,1,0:T(8,128)(2,1)S(1)} %collective-permute-done.1), channel_id=1, source_target_pairs={{0,1},{1,0},{2,3},{3,2},{4,5},{5,4},{6,7},{7,6},{8,9},{9,8},{10,11... | collective-permute-start | bytes 589832 | tf_op jit(solution)/shard_map/ppermute | solution.py:137
  42.0 1.5 %collective-permute-start.10 = (bf16[6,128,128]{2,1,0:T(8,128)(2,1)S(1)}, bf16[6,128,128]{2,1,0:T(8,128)(2,1)S(1)}, u32[]{:S(2)}, u32[]{:S(2)}) collective-permute-start(bf16[6,128,128]{2,1,0:T(8,128)(2,1)S(1)} %collective-permute-done.2), channel_id=1, source_target_pairs={{0,1},{1,0},{2,3},{3,2},{4,5},{5,4},{6,7},{7,6},{8,9},{9,8},{10,11... | collective-permute-start | bytes 589832 | tf_op jit(solution)/shard_map/ppermute | solution.py:137
  42.1 1.7 %collective-permute-start.11 = (bf16[6,128,128]{2,1,0:T(8,128)(2,1)S(1)}, bf16[6,128,128]{2,1,0:T(8,128)(2,1)S(1)}, u32[]{:S(2)}, u32[]{:S(2)}) collective-permute-start(bf16[6,128,128]{2,1,0:T(8,128)(2,1)S(1)} %collective-permute-done.3), channel_id=1, source_target_pairs={{0,1},{1,0},{2,3},{3,2},{4,5},{5,4},{6,7},{7,6},{8,9},{9,8},{10,11... | collective-permute-start | bytes 589832 | tf_op jit(solution)/shard_map/ppermute | solution.py:137
  43.8 3.6 %copy-start = (s32[16]{0:T(128)S(1)}, s32[16]{0:T(128)}, u32[]{:S(2)}) copy-start(s32[16]{0:T(128)} %lengths.15) | copy-start | bytes 196
  50.9 8.7 %collective-permute-start.15 = (bf16[4,128,128]{2,1,0:T(8,128)(2,1)S(1)}, bf16[4,128,128]{2,1,0:T(8,128)(2,1)S(1)}, u32[]{:S(2)}, u32[]{:S(2)}) collective-permute-start(bf16[4,128,128]{2,1,0:T(8,128)(2,1)S(1)} %attend.8), channel_id=1, source_target_pairs={{0,14},{1,15},{2,12},{3,13},{4,10},{5,11},{6,8},{7,9},{8,6},{9,7},... | collective-permute-start | bytes 393224 | tf_op jit(solution)/shard_map/ppermute | solution.py:137
  54.5 7.8 %collective-permute-start.18 = (bf16[4,128,128]{2,1,0:T(8,128)(2,1)S(1)}, bf16[4,128,128]{2,1,0:T(8,128)(2,1)S(1)}, u32[]{:S(2)}, u32[]{:S(2)}) collective-permute-start(bf16[4,128,128]{2,1,0:T(8,128)(2,1)S(1)} %attend.12), channel_id=1, source_target_pairs={{0,12},{1,13},{2,14},{3,15},{4,8},{5,9},{6,10},{7,11},{8,4},{9,5},... | collective-permute-start | bytes 393224 | tf_op jit(solution)/shard_map/ppermute | solution.py:137
  62.1 13.1 %collective-permute-start.16 = (bf16[4,128,128]{2,1,0:T(8,128)(2,1)S(1)}, bf16[4,128,128]{2,1,0:T(8,128)(2,1)S(1)}, u32[]{:S(2)}, u32[]{:S(2)}) collective-permute-start(bf16[4,128,128]{2,1,0:T(8,128)(2,1)S(1)} %attend.9), channel_id=1, source_target_pairs={{0,10},{1,11},{2,8},{3,9},{4,14},{5,15},{6,12},{7,13},{8,2},{9,3},... | collective-permute-start | bytes 393224 | tf_op jit(solution)/shard_map/ppermute | solution.py:137
  63.8 18.1 %collective-permute-start.19 = (bf16[4,128,128]{2,1,0:T(8,128)(2,1)S(1)}, bf16[4,128,128]{2,1,0:T(8,128)(2,1)S(1)}, u32[]{:S(2)}, u32[]{:S(2)}) collective-permute-start(bf16[4,128,128]{2,1,0:T(8,128)(2,1)S(1)} %attend.13), channel_id=1, source_target_pairs={{0,4},{1,5},{2,6},{3,7},{4,0},{5,1},{6,2},{7,3},{8,12},{9,13},{10,... | collective-permute-start | bytes 393224 | tf_op jit(solution)/shard_map/ppermute | solution.py:137
  70.2 11.7 %collective-permute-start.20 = (bf16[4,128,128]{2,1,0:T(8,128)(2,1)S(1)}, bf16[4,128,128]{2,1,0:T(8,128)(2,1)S(1)}, u32[]{:S(2)}, u32[]{:S(2)}) collective-permute-start(bf16[4,128,128]{2,1,0:T(8,128)(2,1)S(1)} %attend.14), channel_id=1, source_target_pairs={{0,6},{1,7},{2,4},{3,5},{4,2},{5,3},{6,0},{7,1},{8,14},{9,15},{10,... | collective-permute-start | bytes 393224 | tf_op jit(solution)/shard_map/ppermute | solution.py:137
  72.3 9.7 %collective-permute-start.21 = (bf16[4,128,128]{2,1,0:T(8,128)(2,1)S(1)}, bf16[4,128,128]{2,1,0:T(8,128)(2,1)S(1)}, u32[]{:S(2)}, u32[]{:S(2)}) collective-permute-start(bf16[4,128,128]{2,1,0:T(8,128)(2,1)S(1)} %attend.15), channel_id=1, source_target_pairs={{0,8},{1,9},{2,10},{3,11},{4,12},{5,13},{6,14},{7,15},{8,0},{9,1},... | collective-permute-start | bytes 393224 | tf_op jit(solution)/shard_map/ppermute | solution.py:137
  76.8 5.0 %collective-permute-start.17 = (bf16[4,128,128]{2,1,0:T(8,128)(2,1)S(1)}, bf16[4,128,128]{2,1,0:T(8,128)(2,1)S(1)}, u32[]{:S(2)}, u32[]{:S(2)}) collective-permute-start(bf16[4,128,128]{2,1,0:T(8,128)(2,1)S(1)} %attend.11), channel_id=1, source_target_pairs={{0,2},{1,3},{2,0},{3,1},{4,6},{5,7},{6,4},{7,5},{8,10},{9,11},{10,... | collective-permute-start | bytes 393224 | tf_op jit(solution)/shard_map/ppermute | solution.py:137
  83.1 1.0 %copy-start.4 = (bf16[8,4,128,128]{3,1,0,2:T(4,128)(2,1)}, bf16[8,4,128,128]{3,1,0,2:T(4,128)(2,1)S(1)}, u32[]{:S(2)}) copy-start(bf16[8,4,128,128]{3,1,0,2:T(4,128)(2,1)S(1)} %copy_dynamic-update-slice_fusion) | copy-start | bytes 3145732

commit v3 on v2

v3 whole, which is shorter than its diff:
```python
import functools

import jax
import jax.numpy as jnp
import numpy as np
from jax import lax
from jax.experimental import pallas as pl
from jax.experimental.pallas import tpu as pltpu
from jax.sharding import PartitionSpec as P

far_below = -3e38
vmem = pl.BlockSpec(memory_space=pltpu.VMEM)
smem = pl.BlockSpec(memory_space=pltpu.SMEM)
anywhere = pl.BlockSpec(memory_space=pl.ANY)
small = pl.CostEstimate(flops=1000, bytes_accessed=1000, transcendentals=0)


def pack_kernel(place, dest, slot, *refs, groups, heads, shards):
    units = shards // 2
    q_packed, kv_packed = refs[-2:]
    unit, core = place[0], place[1]
    bases = [
        (lax.bitwise_xor(unit, away) * 2 + lax.bitwise_xor(core, column)) * shards
        for column, away in groups
    ]

    def pack_block(b, carry):
        for base, blocks in zip(bases, refs):
            shard, at = dest[base + b], slot[base + b]
            mine = lax.bitwise_and(shard, 1) == core
            tile = jnp.where(mine, lax.shift_right_logical(shard, 1), units)
            q_at, kv_at = tile * (heads * shards) + at, shard * shards + at
            for h in range(heads):
                q_packed[q_at + h * shards] = blocks[b + h * shards]
            kv_packed[0, kv_at] = blocks[b + heads * shards]
            kv_packed[1, kv_at] = blocks[b + (heads + 1) * shards]
        return carry

    lax.fori_loop(0, shards, pack_block, 0, unroll=2)


def fold(x, op):
    lanes = x[:, :128]
    for i in range(128, x.shape[1], 128):
        lanes = op(lanes, x[:, i : i + 128])
    return lanes


def attend_kernel(place, lengths, q_packed, kv_packed, *refs, aways, heads, shards, rows, chunk):
    count = len(aways)
    outs, (begins, scores, top, total, mixed) = refs[-5 - count : -5], refs[-5:]
    length = shards * rows
    head_size = q_packed.shape[-1]
    docs = lengths.shape[0]
    q_rows = q_packed.reshape(q_packed.shape[0] * q_packed.shape[1], head_size)
    kv_rows = kv_packed.reshape(2, length, head_size)
    factor = float(head_size ** (-0.5) * np.log2(np.e))

    begin = jnp.int32(0)
    for d in range(docs):
        begins[d] = begin
        begin = begin + lengths[d]

    step = aways[1] - aways[0] if count > 1 else 0

    def one_tile(turn, carry):
        away = aways[0] + turn * step
        tile = lax.bitwise_xor(place[0], away)
        q_start = (tile * 2 + place[1]) * rows
        q_end = q_start + rows
        first, before, within = jnp.int32(0), jnp.int32(0), jnp.int32(0)
        for d in range(docs):
            begin = begins[d]
            first = jnp.where(begin <= q_start, begin, first)
            before = before + (begin <= q_start).astype(jnp.int32)
            within = within + (begin < q_end).astype(jnp.int32)
        q_pos = q_start + lax.broadcasted_iota(jnp.int32, (rows, 1), 0)

        def later_doc(d, firsts):
            begin = begins[d]
            return jnp.where(q_pos >= begin, begin, firsts)

        firsts = lax.fori_loop(before, within, later_doc, jnp.full((rows, 1), first, jnp.int32))
        chunks = lax.div(q_end - first + chunk - 1, chunk)
        start = jnp.maximum(q_end - chunks * chunk, 0)
        q_at = pl.multiple_of(tile * (heads * rows), rows)

        def masked_scores(k_start, width):
            q = q_rows[pl.ds(q_at, heads * rows), :]
            k = kv_rows[0, pl.ds(k_start, width), :]
            s = lax.dot_general(q, k, (((1,), (1,)), ((), ())), preferred_element_type=jnp.float32)
            k_pos = k_start + lax.broadcasted_iota(jnp.int32, (rows, width), 1)
            allowed = (k_pos <= q_pos) & (k_pos >= firsts)
            s = jnp.where(allowed[None], s.reshape(heads, rows, width), far_below)
            return s.reshape(heads * rows, width)

        def put(value):
            for i, out in enumerate(outs):

                @pl.when(turn == i)
                def _(out=out):
                    out[...] = value.astype(jnp.bfloat16).reshape(out.shape)

        for straight in range(1, 2 + 1):

            @pl.when(chunks == straight)
            def _(width=min(straight * chunk, length)):
                k_start = pl.multiple_of(start, rows)
                s = masked_scores(k_start, width)
                peak = jnp.max(s, axis=1, keepdims=True) * factor
                weights = jnp.exp2(s * factor - peak)
                sums = jnp.sum(weights, axis=1, keepdims=True)
                v = kv_rows[1, pl.ds(k_start, width), :]
                mixed[...] = jnp.dot(
                    weights.astype(jnp.bfloat16), v, preferred_element_type=jnp.float32
                ) * (1.0 / sums)

        @pl.when(chunks > 2)
        def _():
            top[...] = jnp.full_like(top, far_below)

            def score_chunk(j, carry):
                s = masked_scores(pl.multiple_of(start + j * chunk, rows), chunk)
                scores[j] = s
                top[...] = jnp.maximum(top[...], fold(s, jnp.maximum))
                return carry

            lax.fori_loop(0, chunks, score_chunk, 0)
            top[...] = jnp.broadcast_to(jnp.max(top[...], axis=1, keepdims=True) * factor, top.shape)
            total[...] = jnp.zeros_like(total)
            mixed[...] = jnp.zeros_like(mixed)

            def mix_chunk(j, carry):
                v = kv_rows[1, pl.ds(pl.multiple_of(start + j * chunk, rows), chunk), :]
                shift = jnp.concatenate([top[...]] * (chunk // 128), axis=1)
                weights = jnp.exp2(scores[j] * factor - shift)
                total[...] += fold(weights, jnp.add)
                mixed[...] += jnp.dot(
                    weights.astype(jnp.bfloat16), v, preferred_element_type=jnp.float32
                )
                return carry

            lax.fori_loop(0, chunks, mix_chunk, 0)
            mixed[...] = mixed[...] * (1.0 / jnp.sum(total[...], axis=1, keepdims=True))

        put(mixed[...])
        return carry

    lax.fori_loop(0, count, one_tile, 0)


def per_device(q_rows, k_rows, v_rows, doc_lengths, plan_dest, plan_slot):
    shards = lax.axis_size("seq")
    my_index = lax.axis_index("seq")
    rows, heads_all, head_size = q_rows.shape
    kv_heads = k_rows.shape[1]
    per = rows // shards
    span = rows * min(8, shards // 2)
    units = shards // 2
    unit, core = my_index // 2, my_index % 2
    heads = heads_all // units
    copies = units // kv_heads
    place = jnp.stack([unit, core]).astype(jnp.int32)

    q_send = q_rows.reshape(rows, units, heads, head_size).transpose(1, 2, 0, 3)
    kv_send = jnp.stack([k_rows, v_rows], axis=0).transpose(2, 0, 1, 3)
    kv_send = jnp.repeat(kv_send, copies, axis=0)
    sent = jnp.concatenate([q_send, kv_send], axis=1)

    def hop(x, distance):
        return lax.ppermute(x, "seq", [(i, i ^ distance) for i in range(shards)])

    def part(away):
        return lax.dynamic_index_in_dim(sent, unit ^ away, 0, keepdims=False)

    near = {away: part(away) for away in reversed(range(units))}
    for away in reversed(range(1, units)):
        near[away] = hop(near[away], 2 * away)
    half = units // 2
    far = {away: hop(near[away], 1) for away in range(units)}

    packed_shapes = (
        jax.ShapeDtypeStruct(((units + 1) * heads * shards, per, head_size), jnp.bfloat16),
        jax.ShapeDtypeStruct((2, shards * shards, per, head_size), jnp.bfloat16),
    )

    def pack(groups, arrays, packed, cost):
        blocks = [x.reshape(-1, per, head_size) for x in arrays]
        count = 3 + len(blocks)
        return pl.pallas_call(
            functools.partial(pack_kernel, groups=groups, heads=heads, shards=shards),
            out_shape=packed_shapes,
            in_specs=[smem] * 3 + [vmem] * (len(blocks) + len(packed)),
            out_specs=(vmem, vmem),
            input_output_aliases={count: 0, count + 1: 1} if packed else {},
            compiler_params=pltpu.CompilerParams(vmem_limit_bytes=24 << 20),
            cost_estimate=cost,
            name="pack_blocks",
        )(place, plan_dest, plan_slot, *blocks, *packed)

    everyone = list(range(units))
    groups = [(column, away) for column in range(2) for away in everyone]
    packed = pack(groups, [x[away] for x in (near, far) for away in everyone], (), small)

    chunk = min(256, span)
    most = -(-(span + rows - 1) // chunk)
    tiles = {}

    def attend(aways, after):
        outs = pl.pallas_call(
            functools.partial(
                attend_kernel, aways=aways, heads=heads, shards=shards, rows=rows, chunk=chunk
            ),
            out_shape=[jax.ShapeDtypeStruct((heads, rows, head_size), jnp.bfloat16)] * len(aways),
            in_specs=[smem] * 2 + [vmem] * 2 + [anywhere] * len(after),
            out_specs=[vmem] * len(aways),
            scratch_shapes=[
                pltpu.SMEM((doc_lengths.shape[0],), jnp.int32),
                pltpu.VMEM((most, heads * rows, chunk), jnp.float32),
                pltpu.VMEM((heads * rows, 128), jnp.float32),
                pltpu.VMEM((heads * rows, 128), jnp.float32),
                pltpu.VMEM((heads * rows, head_size), jnp.float32),
            ],
            compiler_params=pltpu.CompilerParams(vmem_limit_bytes=24 << 20),
            cost_estimate=small,
            name="attend",
        )(place, doc_lengths, *packed, *after)
        for away, out in zip(aways, outs):
            tiles[away] = hop(out, 2 * away) if away else out

    far_tiles, near_tiles = list(reversed(range(half, units))), list(reversed(range(half)))
    attend(far_tiles[:1], [])
    attend(far_tiles[1:2], [])
    for i in range(2, half, 2):
        attend(far_tiles[i : i + 2], [])
    for i, away in enumerate(near_tiles):
        attend([away], [tiles[far_tiles[2 * i // half]]])
    gathered = jnp.zeros((units, heads, rows, head_size), jnp.bfloat16)
    for away in range(units):
        gathered = lax.dynamic_update_index_in_dim(gathered, tiles[away], unit ^ away, 0)
    return gathered.reshape(heads_all, rows, head_size).transpose(1, 0, 2)


def solution(mesh):
    whole = P(("dp", "seq"), None, None)
    return jax.shard_map(
        per_device,
        mesh=mesh,
        in_specs=(whole, whole, whole, P("dp"), P("dp"), P("dp")),
        out_specs=whole,
        check_vma=False,
    )
```

time: 85.5 us -> 81.6 us (0.954); the launches traced: 84.1 us -> 82.1 us
  Pallas kernels: 21.2 us -> 14.3 us
  starting transfers between devices: 36.7 us -> 40.7 us
    pallas_call x8 -> x7, Pallas kernels: 17.6 us -> 11.9 us  [attend(): pl.pallas_call(functools.partial(attend_kernel, aways=aways, heads=heads,...]
    ppermute x22, starting transfers between devices: 36.7 us -> 40.7 us  [hop(): return lax.ppermute(x, 'seq', [(i, i ^ distance) for i in range(shards)])]
    pallas_call x1, Pallas kernels: 3.62 us -> 2.36 us  [pack(): pl.pallas_call(functools.partial(pack_kernel, groups=groups, heads=heads,...]
  transfers between devices with their start and end apart: 22 -> 22, of which waited for: 9 -> 9; matrix products, arithmetic and copies ran while one was open for 1% -> 2% of each run, Pallas kernels for 17% -> 13%
where the time goes in v3:
time: 81.6 us; the launch traced here: 82.1 us
  starting transfers between devices  40.7 us (50%)
  waiting for transfers between devices  22.1 us (27%)
  Pallas kernels  14.3 us (18%)
  local copies, waits for them, and re-layouts  3.32 us (4%)
  other arithmetic  1.39 us (2%)
    ppermute x22, starting transfers between devices, hop(): return lax.ppermute(x, 'seq', [(i, i ^ distance) for i in range(shards)])  40.7 us
    ppermute x22, waiting for transfers between devices, hop(): return lax.ppermute(x, 'seq', [(i, i ^ distance) for i in range(shards)])  22.1 us
    pallas_call x7, Pallas kernels, attend(): pl.pallas_call(functools.partial(attend_kernel, aways=aways, heads=heads,...  11.9 us
    pallas_call x1, Pallas kernels, pack(): pl.pallas_call(functools.partial(pack_kernel, groups=groups, heads=heads,...  2.36 us
  transfers between devices with their start and end apart: 22, of which 9 were waited for; matrix products, arithmetic and copies ran while one was open for 2% of the time, Pallas kernels for 13%

profile of v3, /device:TPU:0, one launch (start us, length us, event | category | flops | bytes accessed | tf_op | source)
XLA Modules:
  0.0 82.1 jit_solution(15437993544622484675)
XLA Ops:
  0.0 1.2 %maximum_bitcast_fusion = bf16[8,2,128,128]{3,0,2,1:T(8,128)(2,1)S(1)} fusion(bf16[1,128,8,128]{3,2,1,0:T(8,128)(2,1)} %bitcast.78, bf16[1,128,8,128]{3,2,1,0:T(8,128)(2,1)} %bitcast.79), kind=kLoop, calls=%fused_computation.17 | loop fusion | flops 262144 | bytes 1048576 | tf_op jit(solution)/shard_map/transpose | solution.py:166
  1.2 0.1 copy.8
  1.3 0.1 copy-done.3
  1.4 0.4 copy.19
  1.9 5.1 %collective-permute-start.5 = (bf16[6,128,128]{2,1,0:T(8,128)(2,1)S(1)}, bf16[6,128,128]{2,1,0:T(8,128)(2,1)S(1)}, u32[]{:S(2)}, u32[]{:S(2)}) collective-permute-start(bf16[6,128,128]{2,1,0:T(8,128)(2,1)S(1)} %get-tuple-element.19), channel_id=1, source_target_pairs={{0,12},{1,13},{2,14},{3,15},{4,8},{5,9},{6,10},{7,11},{8,4},{9,5},... | collective-permute-start | bytes 589832 | tf_op jit(solution)/shard_map/ppermute | solution.py:171
  7.0 0.4 collective-permute-start.4
  7.3 0.1 fusion.14
  7.4 2.5 %collective-permute-start.6 = (bf16[6,128,128]{2,1,0:T(8,128)(2,1)S(1)}, bf16[6,128,128]{2,1,0:T(8,128)(2,1)S(1)}, u32[]{:S(2)}, u32[]{:S(2)}) collective-permute-start(bf16[6,128,128]{2,1,0:T(8,128)(2,1)S(1)} %get-tuple-element.13), channel_id=1, source_target_pairs={{0,14},{1,15},{2,12},{3,13},{4,10},{5,11},{6,8},{7,9},{8,6},{9,7},... | collective-permute-start | bytes 589832 | tf_op jit(solution)/shard_map/ppermute | solution.py:171
  10.0 1.5 %collective-permute-start = (bf16[6,128,128]{2,1,0:T(8,128)(2,1)S(1)}, bf16[6,128,128]{2,1,0:T(8,128)(2,1)S(1)}, u32[]{:S(2)}, u32[]{:S(2)}) collective-permute-start(bf16[6,128,128]{2,1,0:T(8,128)(2,1)S(1)} %get-tuple-element.15), channel_id=1, source_target_pairs={{0,2},{1,3},{2,0},{3,1},{4,6},{5,7},{6,4},{7,5},{8,10},{9,11},{10,... | collective-permute-start | bytes 589832 | tf_op jit(solution)/shard_map/ppermute | solution.py:171
  11.4 1.6 %collective-permute-start.1 = (bf16[6,128,128]{2,1,0:T(8,128)(2,1)S(1)}, bf16[6,128,128]{2,1,0:T(8,128)(2,1)S(1)}, u32[]{:S(2)}, u32[]{:S(2)}) collective-permute-start(bf16[6,128,128]{2,1,0:T(8,128)(2,1)S(1)} %get-tuple-element.16), channel_id=1, source_target_pairs={{0,4},{1,5},{2,6},{3,7},{4,0},{5,1},{6,2},{7,3},{8,12},{9,13},{10,... | collective-permute-start | bytes 589832 | tf_op jit(solution)/shard_map/ppermute | solution.py:171
  13.0 13.1 %collective-permute-start.2 = (bf16[6,128,128]{2,1,0:T(8,128)(2,1)S(1)}, bf16[6,128,128]{2,1,0:T(8,128)(2,1)S(1)}, u32[]{:S(2)}, u32[]{:S(2)}) collective-permute-start(bf16[6,128,128]{2,1,0:T(8,128)(2,1)S(1)} %get-tuple-element.17), channel_id=1, source_target_pairs={{0,6},{1,7},{2,4},{3,5},{4,2},{5,3},{6,0},{7,1},{8,14},{9,15},{10,... | collective-permute-start | bytes 589832 | tf_op jit(solution)/shard_map/ppermute | solution.py:171
  26.1 3.7 %collective-permute-done.4 = bf16[6,128,128]{2,1,0:T(8,128)(2,1)S(1)} collective-permute-done((bf16[6,128,128]{2,1,0:T(8,128)(2,1)S(1)}, bf16[6,128,128]{2,1,0:T(8,128)(2,1)S(1)}, u32[]{:S(2)}, u32[]{:S(2)}) %collective-permute-start.4) | collective-permute-done | bytes 196640 | tf_op jit(solution)/shard_map/ppermute | solution.py:171
  29.8 0.5 collective-permute-start.13
  30.3 0.1 collective-permute-start.12
  30.4 2.4 %collective-permute-done.2 = bf16[6,128,128]{2,1,0:T(8,128)(2,1)S(1)} collective-permute-done((bf16[6,128,128]{2,1,0:T(8,128)(2,1)S(1)}, bf16[6,128,128]{2,1,0:T(8,128)(2,1)S(1)}, u32[]{:S(2)}, u32[]{:S(2)}) %collective-permute-start.2) | collective-permute-done | bytes 196640 | tf_op jit(solution)/shard_map/ppermute | solution.py:171
  32.8 8.7 %collective-permute-done.3 = bf16[6,128,128]{2,1,0:T(8,128)(2,1)S(1)} collective-permute-done((bf16[6,128,128]{2,1,0:T(8,128)(2,1)S(1)}, bf16[6,128,128]{2,1,0:T(8,128)(2,1)S(1)}, u32[]{:S(2)}, u32[]{:S(2)}) %collective-permute-start.3) | collective-permute-done | bytes 196640 | tf_op jit(solution)/shard_map/ppermute | solution.py:171
  41.5 0.5 collective-permute-start.9
  42.0 0.1 collective-permute-start.10
  42.1 0.4 collective-permute-start.11
  42.6 0.1 pad_add_fusion.place
  42.6 0.3 collective-permute-done.8
  43.0 0.3 collective-permute-done.9
  43.2 0.3 collective-permute-done.10
  43.5 0.3 collective-permute-done.11
  43.8 2.4 %pack_blocks.1 = (bf16[576,8,128]{2,1,0:T(8,128)(2,1)S(1)}, bf16[2,256,8,128]{3,2,1,0:T(8,128)(2,1)S(1)}) custom-call(s32[2]{0:T(128)S(1)} %pad_add_fusion.place, s32[256]{0:T(256)S(1)} %copy-done.1, s32[256]{0:T(256)S(1)} %copy-done.2, bf16[96,8,128]{2,1,0:T(8,128)(2,1)S(1)} %bitcast.59, bf16[96,8,128]{2,1,0:T(8,128)(2,1)S(1)} %bitcast.63, ...), custom_call_target="tpu_custom_call" | custom-call | flops 1000 | bytes 1000 | tf_op jit(solution)/shard_map/pack_blocks/pallas_call | solution.py:190
  46.2 1.1 %attend.7 = bf16[4,128,128]{2,1,0:T(8,128)(2,1)S(1)} custom-call(s32[2]{0:T(128)S(1)} %pad_add_fusion.place, s32[16]{0:T(128)S(1)} %copy-done, bf16[576,8,128]{2,1,0:T(8,128)(2,1)S(1)} %get-tuple-element.9.q_packed, bf16[2,256,8,128]{3,2,1,0:T(8,128)(2,1)S(1)} %get-tuple-element.10.kv_packed), custom_call_target="tpu_custom_call" | custom-call | flops 1000 | bytes 1000 | tf_op jit(solution)/shard_map/attend/pallas_call | solution.py:210
  47.3 1.9 %collective-permute-start.15 = (bf16[4,128,128]{2,1,0:T(8,128)(2,1)S(1)}, bf16[4,128,128]{2,1,0:T(8,128)(2,1)S(1)}, u32[]{:S(2)}, u32[]{:S(2)}) collective-permute-start(bf16[4,128,128]{2,1,0:T(8,128)(2,1)S(1)} %attend.7), channel_id=1, source_target_pairs={{0,12},{1,13},{2,14},{3,15},{4,8},{5,9},{6,10},{7,11},{8,4},{9,5},... | collective-permute-start | bytes 393224 | tf_op jit(solution)/shard_map/ppermute | solution.py:171
  49.2 1.1 %attend.10 = bf16[4,128,128]{2,1,0:T(8,128)(2,1)S(1)} custom-call(s32[2]{0:T(128)S(1)} %pad_add_fusion.place, s32[16]{0:T(128)S(1)} %copy-done, bf16[576,8,128]{2,1,0:T(8,128)(2,1)S(1)} %get-tuple-element.9.q_packed, bf16[2,256,8,128]{3,2,1,0:T(8,128)(2,1)S(1)} %get-tuple-element.10.kv_packed), custom_call_target="tpu_custom_call" | custom-call | flops 1000 | bytes 1000 | tf_op jit(solution)/shard_map/attend/pallas_call | solution.py:210
  50.4 2.5 %collective-permute-start.17 = (bf16[4,128,128]{2,1,0:T(8,128)(2,1)S(1)}, bf16[4,128,128]{2,1,0:T(8,128)(2,1)S(1)}, u32[]{:S(2)}, u32[]{:S(2)}) collective-permute-start(bf16[4,128,128]{2,1,0:T(8,128)(2,1)S(1)} %attend.10), channel_id=1, source_target_pairs={{0,14},{1,15},{2,12},{3,13},{4,10},{5,11},{6,8},{7,9},{8,6},{9,7},... | collective-permute-start | bytes 393224 | tf_op jit(solution)/shard_map/ppermute | solution.py:171
  52.9 4.7 %attend.13 = (bf16[4,128,128]{2,1,0:T(8,128)(2,1)S(1)}, bf16[4,128,128]{2,1,0:T(8,128)(2,1)S(1)}) custom-call(s32[2]{0:T(128)S(1)} %pad_add_fusion.place, s32[16]{0:T(128)S(1)} %copy-done, bf16[576,8,128]{2,1,0:T(8,128)(2,1)S(1)} %get-tuple-element.9.q_packed, bf16[2,256,8,128]{3,2,1,0:T(8,128)(2,1)S(1)} %get-tuple-element.10.kv_packed), custom_call_target="tpu_custom_call" | custom-call | flops 1000 | bytes 1000 | tf_op jit(solution)/shard_map/attend/pallas_call | solution.py:210
  57.6 0.1 collective-permute-start.20
  57.6 3.4 %collective-permute-start.21 = (bf16[4,128,128]{2,1,0:T(8,128)(2,1)S(1)}, bf16[4,128,128]{2,1,0:T(8,128)(2,1)S(1)}, u32[]{:S(2)}, u32[]{:S(2)}) collective-permute-start(bf16[4,128,128]{2,1,0:T(8,128)(2,1)S(1)} %get-tuple-element.12), channel_id=1, source_target_pairs={{0,10},{1,11},{2,8},{3,9},{4,14},{5,15},{6,12},{7,13},{8,2},{9,3},... | collective-permute-start | bytes 393224 | tf_op jit(solution)/shard_map/ppermute | solution.py:171
  61.0 1.1 %attend.9 = bf16[4,128,128]{2,1,0:T(8,128)(2,1)S(1)} custom-call(s32[2]{0:T(128)S(1)} %pad_add_fusion.place, s32[16]{0:T(128)S(1)} %copy-done, bf16[576,8,128]{2,1,0:T(8,128)(2,1)S(1)} %get-tuple-element.9.q_packed, bf16[2,256,8,128]{3,2,1,0:T(8,128)(2,1)S(1)} %get-tuple-element.10.kv_packed, bf16[4,128,128]{2,1,0:T(8,128)(2,1)S(1)} %collective-permute-done.15.refs_0_), custom_call_target="tpu_custom_call" | custom-call | flops 1000 | bytes 1000 | tf_op jit(solution)/shard_map/attend/pallas_call | solution.py:210
  62.2 1.1 %collective-permute-start.16 = (bf16[4,128,128]{2,1,0:T(8,128)(2,1)S(1)}, bf16[4,128,128]{2,1,0:T(8,128)(2,1)S(1)}, u32[]{:S(2)}, u32[]{:S(2)}) collective-permute-start(bf16[4,128,128]{2,1,0:T(8,128)(2,1)S(1)} %attend.9), channel_id=1, source_target_pairs={{0,2},{1,3},{2,0},{3,1},{4,6},{5,7},{6,4},{7,5},{8,10},{9,11},{10,... | collective-permute-start | bytes 393224 | tf_op jit(solution)/shard_map/ppermute | solution.py:171
  63.2 1.1 %attend.11 = bf16[4,128,128]{2,1,0:T(8,128)(2,1)S(1)} custom-call(s32[2]{0:T(128)S(1)} %pad_add_fusion.place, s32[16]{0:T(128)S(1)} %copy-done, bf16[576,8,128]{2,1,0:T(8,128)(2,1)S(1)} %get-tuple-element.9.q_packed, bf16[2,256,8,128]{3,2,1,0:T(8,128)(2,1)S(1)} %get-tuple-element.10.kv_packed, bf16[4,128,128]{2,1,0:T(8,128)(2,1)S(1)} %collective-permute-done.17.refs_0_), custom_call_target="tpu_custom_call" | custom-call | flops 1000 | bytes 1000 | tf_op jit(solution)/shard_map/attend/pallas_call | solution.py:210
  64.4 6.0 %collective-permute-start.18 = (bf16[4,128,128]{2,1,0:T(8,128)(2,1)S(1)}, bf16[4,128,128]{2,1,0:T(8,128)(2,1)S(1)}, u32[]{:S(2)}, u32[]{:S(2)}) collective-permute-start(bf16[4,128,128]{2,1,0:T(8,128)(2,1)S(1)} %attend.11), channel_id=1, source_target_pairs={{0,4},{1,5},{2,6},{3,7},{4,0},{5,1},{6,2},{7,3},{8,12},{9,13},{10,... | collective-permute-start | bytes 393224 | tf_op jit(solution)/shard_map/ppermute | solution.py:171
  70.4 1.6 %attend.12 = bf16[4,128,128]{2,1,0:T(8,128)(2,1)S(1)} custom-call(s32[2]{0:T(128)S(1)} %pad_add_fusion.place, s32[16]{0:T(128)S(1)} %copy-done, bf16[576,8,128]{2,1,0:T(8,128)(2,1)S(1)} %get-tuple-element.9.q_packed, bf16[2,256,8,128]{3,2,1,0:T(8,128)(2,1)S(1)} %get-tuple-element.10.kv_packed, bf16[4,128,128]{2,1,0:T(8,128)(2,1)S(1)} %collective-permute-done.17.refs_0_), custom_call_target="tpu_custom_call" | custom-call | flops 1000 | bytes 1000 | tf_op jit(solution)/shard_map/attend/pallas_call | solution.py:210
  72.0 0.1 collective-permute-start.19
  72.0 1.1 %attend.8 = bf16[4,128,128]{2,1,0:T(8,128)(2,1)S(1)} custom-call(s32[2]{0:T(128)S(1)} %pad_add_fusion.place, s32[16]{0:T(128)S(1)} %copy-done, bf16[576,8,128]{2,1,0:T(8,128)(2,1)S(1)} %get-tuple-element.9.q_packed, bf16[2,256,8,128]{3,2,1,0:T(8,128)(2,1)S(1)} %get-tuple-element.10.kv_packed, bf16[4,128,128]{2,1,0:T(8,128)(2,1)S(1)} %collective-permute-done.15.refs_0_), custom_call_target="tpu_custom_call" | custom-call | flops 1000 | bytes 1000 | tf_op jit(solution)/shard_map/attend/pallas_call | solution.py:210
  73.2 0.2 broadcast_in_dim.28
  73.5 2.3 %collective-permute-done.18 = bf16[4,128,128]{2,1,0:T(8,128)(2,1)S(1)} collective-permute-done((bf16[4,128,128]{2,1,0:T(8,128)(2,1)S(1)}, bf16[4,128,128]{2,1,0:T(8,128)(2,1)S(1)}, u32[]{:S(2)}, u32[]{:S(2)}) %collective-permute-start.18) | collective-permute-done | bytes 131104 | tf_op jit(solution)/shard_map/ppermute | solution.py:171
  75.8 3.8 %collective-permute-done.19 = bf16[4,128,128]{2,1,0:T(8,128)(2,1)S(1)} collective-permute-done((bf16[4,128,128]{2,1,0:T(8,128)(2,1)S(1)}, bf16[4,128,128]{2,1,0:T(8,128)(2,1)S(1)}, u32[]{:S(2)}, u32[]{:S(2)}) %collective-permute-start.19) | collective-permute-done | bytes 131104 | tf_op jit(solution)/shard_map/ppermute | solution.py:171
  79.6 0.8 copy.9
  80.4 0.2 copy_dynamic-update-slice_fusion.3
  80.6 0.2 copy_dynamic-update-slice_fusion.2
  80.8 0.2 copy_dynamic-update-slice_fusion.1
  80.9 0.2 copy_dynamic-update-slice_fusion
  81.1 1.0 %copy-done.4 = bf16[8,4,128,128]{3,1,0,2:T(4,128)(2,1)} copy-done((bf16[8,4,128,128]{3,1,0,2:T(4,128)(2,1)}, bf16[8,4,128,128]{3,1,0,2:T(4,128)(2,1)S(1)}, u32[]{:S(2)}) %copy-start.4) | copy-done | bytes 1048600
  (30 shorter events, 0.2 us)
Async XLA Ops:
  0.0 1.4 %copy-start.3 = (bf16[128,32,128]{2,1,0:T(8,128)(2,1)S(1)}, bf16[128,32,128]{2,1,0:T(8,128)(2,1)}, u32[]{:S(2)}) copy-start(bf16[128,32,128]{2,1,0:T(8,128)(2,1)} %param.6) | copy-start | bytes 3145732
  1.9 11.2 %collective-permute-start.5 = (bf16[6,128,128]{2,1,0:T(8,128)(2,1)S(1)}, bf16[6,128,128]{2,1,0:T(8,128)(2,1)S(1)}, u32[]{:S(2)}, u32[]{:S(2)}) collective-permute-start(bf16[6,128,128]{2,1,0:T(8,128)(2,1)S(1)} %get-tuple-element.19), channel_id=1, source_target_pairs={{0,12},{1,13},{2,14},{3,15},{4,8},{5,9},{6,10},{7,11},{8,4},{9,5},... | collective-permute-start | bytes 589832 | tf_op jit(solution)/shard_map/ppermute | solution.py:171
  7.0 22.8 %collective-permute-start.4 = (bf16[6,128,128]{2,1,0:T(8,128)(2,1)S(1)}, bf16[6,128,128]{2,1,0:T(8,128)(2,1)S(1)}, u32[]{:S(2)}, u32[]{:S(2)}) collective-permute-start(bf16[6,128,128]{2,1,0:T(8,128)(2,1)S(1)} %get-tuple-element.20), channel_id=1, source_target_pairs={{0,10},{1,11},{2,8},{3,9},{4,14},{5,15},{6,12},{7,13},{8,2},{9,3},... | collective-permute-start | bytes 589832 | tf_op jit(solution)/shard_map/ppermute | solution.py:171
  7.3 36.5 %copy-start.1 = (s32[256]{0:T(256)S(1)}, s32[256]{0:T(256)}, u32[]{:S(2)}) copy-start(s32[256]{0:T(256)} %dest.1) | copy-start | bytes 3076
  7.3 36.5 %copy-start.2 = (s32[256]{0:T(256)S(1)}, s32[256]{0:T(256)}, u32[]{:S(2)}) copy-start(s32[256]{0:T(256)} %slot.1) | copy-start | bytes 3076
  7.4 22.4 %collective-permute-start.6 = (bf16[6,128,128]{2,1,0:T(8,128)(2,1)S(1)}, bf16[6,128,128]{2,1,0:T(8,128)(2,1)S(1)}, u32[]{:S(2)}, u32[]{:S(2)}) collective-permute-start(bf16[6,128,128]{2,1,0:T(8,128)(2,1)S(1)} %get-tuple-element.13), channel_id=1, source_target_pairs={{0,14},{1,15},{2,12},{3,13},{4,10},{5,11},{6,8},{7,9},{8,6},{9,7},... | collective-permute-start | bytes 589832 | tf_op jit(solution)/shard_map/ppermute | solution.py:171
  10.0 19.9 %collective-permute-start = (bf16[6,128,128]{2,1,0:T(8,128)(2,1)S(1)}, bf16[6,128,128]{2,1,0:T(8,128)(2,1)S(1)}, u32[]{:S(2)}, u32[]{:S(2)}) collective-permute-start(bf16[6,128,128]{2,1,0:T(8,128)(2,1)S(1)} %get-tuple-element.15), channel_id=1, source_target_pairs={{0,2},{1,3},{2,0},{3,1},{4,6},{5,7},{6,4},{7,5},{8,10},{9,11},{10,... | collective-permute-start | bytes 589832 | tf_op jit(solution)/shard_map/ppermute | solution.py:171
  11.4 18.9 %collective-permute-start.1 = (bf16[6,128,128]{2,1,0:T(8,128)(2,1)S(1)}, bf16[6,128,128]{2,1,0:T(8,128)(2,1)S(1)}, u32[]{:S(2)}, u32[]{:S(2)}) collective-permute-start(bf16[6,128,128]{2,1,0:T(8,128)(2,1)S(1)} %get-tuple-element.16), channel_id=1, source_target_pairs={{0,4},{1,5},{2,6},{3,7},{4,0},{5,1},{6,2},{7,3},{8,12},{9,13},{10,... | collective-permute-start | bytes 589832 | tf_op jit(solution)/shard_map/ppermute | solution.py:171
  13.0 19.8 %collective-permute-start.2 = (bf16[6,128,128]{2,1,0:T(8,128)(2,1)S(1)}, bf16[6,128,128]{2,1,0:T(8,128)(2,1)S(1)}, u32[]{:S(2)}, u32[]{:S(2)}) collective-permute-start(bf16[6,128,128]{2,1,0:T(8,128)(2,1)S(1)} %get-tuple-element.17), channel_id=1, source_target_pairs={{0,6},{1,7},{2,4},{3,5},{4,2},{5,3},{6,0},{7,1},{8,14},{9,15},{10,... | collective-permute-start | bytes 589832 | tf_op jit(solution)/shard_map/ppermute | solution.py:171
  29.8 11.7 %collective-permute-start.3 = (bf16[6,128,128]{2,1,0:T(8,128)(2,1)S(1)}, bf16[6,128,128]{2,1,0:T(8,128)(2,1)S(1)}, u32[]{:S(2)}, u32[]{:S(2)}) collective-permute-start(bf16[6,128,128]{2,1,0:T(8,128)(2,1)S(1)} %get-tuple-element.18), channel_id=1, source_target_pairs={{0,8},{1,9},{2,10},{3,11},{4,12},{5,13},{6,14},{7,15},{8,0},{9,1},... | collective-permute-start | bytes 589832 | tf_op jit(solution)/shard_map/ppermute | solution.py:171
  29.8 11.7 %collective-permute-start.7 = (bf16[6,128,128]{2,1,0:T(8,128)(2,1)S(1)}, bf16[6,128,128]{2,1,0:T(8,128)(2,1)S(1)}, u32[]{:S(2)}, u32[]{:S(2)}) collective-permute-start(bf16[6,128,128]{2,1,0:T(8,128)(2,1)S(1)} %bitcast.58), channel_id=1, source_target_pairs={{0,1},{1,0},{2,3},{3,2},{4,5},{5,4},{6,7},{7,6},{8,9},{9,8},{10,11... | collective-permute-start | bytes 589832 | tf_op jit(solution)/shard_map/ppermute | solution.py:171
  29.8 12.2 %collective-permute-start.13 = (bf16[6,128,128]{2,1,0:T(8,128)(2,1)S(1)}, bf16[6,128,128]{2,1,0:T(8,128)(2,1)S(1)}, u32[]{:S(2)}, u32[]{:S(2)}) collective-permute-start(bf16[6,128,128]{2,1,0:T(8,128)(2,1)S(1)} %collective-permute-done.5), channel_id=1, source_target_pairs={{0,1},{1,0},{2,3},{3,2},{4,5},{5,4},{6,7},{7,6},{8,9},{9,8},{10,11... | collective-permute-start | bytes 589832 | tf_op jit(solution)/shard_map/ppermute | solution.py:171
  30.3 11.8 %collective-permute-start.12 = (bf16[6,128,128]{2,1,0:T(8,128)(2,1)S(1)}, bf16[6,128,128]{2,1,0:T(8,128)(2,1)S(1)}, u32[]{:S(2)}, u32[]{:S(2)}) collective-permute-start(bf16[6,128,128]{2,1,0:T(8,128)(2,1)S(1)} %collective-permute-done.4), channel_id=1, source_target_pairs={{0,1},{1,0},{2,3},{3,2},{4,5},{5,4},{6,7},{7,6},{8,9},{9,8},{10,11... | collective-permute-start | bytes 589832 | tf_op jit(solution)/shard_map/ppermute | solution.py:171
  32.8 9.8 %collective-permute-start.14 = (bf16[6,128,128]{2,1,0:T(8,128)(2,1)S(1)}, bf16[6,128,128]{2,1,0:T(8,128)(2,1)S(1)}, u32[]{:S(2)}, u32[]{:S(2)}) collective-permute-start(bf16[6,128,128]{2,1,0:T(8,128)(2,1)S(1)} %collective-permute-done.6), channel_id=1, source_target_pairs={{0,1},{1,0},{2,3},{3,2},{4,5},{5,4},{6,7},{7,6},{8,9},{9,8},{10,11... | collective-permute-start | bytes 589832 | tf_op jit(solution)/shard_map/ppermute | solution.py:171
  41.5 1.4 %collective-permute-start.8 = (bf16[6,128,128]{2,1,0:T(8,128)(2,1)S(1)}, bf16[6,128,128]{2,1,0:T(8,128)(2,1)S(1)}, u32[]{:S(2)}, u32[]{:S(2)}) collective-permute-start(bf16[6,128,128]{2,1,0:T(8,128)(2,1)S(1)} %collective-permute-done), channel_id=1, source_target_pairs={{0,1},{1,0},{2,3},{3,2},{4,5},{5,4},{6,7},{7,6},{8,9},{9,8},{10,11... | collective-permute-start | bytes 589832 | tf_op jit(solution)/shard_map/ppermute | solution.py:171
  41.5 1.7 %collective-permute-start.9 = (bf16[6,128,128]{2,1,0:T(8,128)(2,1)S(1)}, bf16[6,128,128]{2,1,0:T(8,128)(2,1)S(1)}, u32[]{:S(2)}, u32[]{:S(2)}) collective-permute-start(bf16[6,128,128]{2,1,0:T(8,128)(2,1)S(1)} %collective-permute-done.1), channel_id=1, source_target_pairs={{0,1},{1,0},{2,3},{3,2},{4,5},{5,4},{6,7},{7,6},{8,9},{9,8},{10,11... | collective-permute-start | bytes 589832 | tf_op jit(solution)/shard_map/ppermute | solution.py:171
  42.0 1.5 %collective-permute-start.10 = (bf16[6,128,128]{2,1,0:T(8,128)(2,1)S(1)}, bf16[6,128,128]{2,1,0:T(8,128)(2,1)S(1)}, u32[]{:S(2)}, u32[]{:S(2)}) collective-permute-start(bf16[6,128,128]{2,1,0:T(8,128)(2,1)S(1)} %collective-permute-done.2), channel_id=1, source_target_pairs={{0,1},{1,0},{2,3},{3,2},{4,5},{5,4},{6,7},{7,6},{8,9},{9,8},{10,11... | collective-permute-start | bytes 589832 | tf_op jit(solution)/shard_map/ppermute | solution.py:171
  42.1 1.7 %collective-permute-start.11 = (bf16[6,128,128]{2,1,0:T(8,128)(2,1)S(1)}, bf16[6,128,128]{2,1,0:T(8,128)(2,1)S(1)}, u32[]{:S(2)}, u32[]{:S(2)}) collective-permute-start(bf16[6,128,128]{2,1,0:T(8,128)(2,1)S(1)} %collective-permute-done.3), channel_id=1, source_target_pairs={{0,1},{1,0},{2,3},{3,2},{4,5},{5,4},{6,7},{7,6},{8,9},{9,8},{10,11... | collective-permute-start | bytes 589832 | tf_op jit(solution)/shard_map/ppermute | solution.py:171
  43.8 2.4 %copy-start = (s32[16]{0:T(128)S(1)}, s32[16]{0:T(128)}, u32[]{:S(2)}) copy-start(s32[16]{0:T(128)} %lengths.13) | copy-start | bytes 196
  47.3 13.7 %collective-permute-start.15 = (bf16[4,128,128]{2,1,0:T(8,128)(2,1)S(1)}, bf16[4,128,128]{2,1,0:T(8,128)(2,1)S(1)}, u32[]{:S(2)}, u32[]{:S(2)}) collective-permute-start(bf16[4,128,128]{2,1,0:T(8,128)(2,1)S(1)} %attend.7), channel_id=1, source_target_pairs={{0,12},{1,13},{2,14},{3,15},{4,8},{5,9},{6,10},{7,11},{8,4},{9,5},... | collective-permute-start | bytes 393224 | tf_op jit(solution)/shard_map/ppermute | solution.py:171
  50.4 12.9 %collective-permute-start.17 = (bf16[4,128,128]{2,1,0:T(8,128)(2,1)S(1)}, bf16[4,128,128]{2,1,0:T(8,128)(2,1)S(1)}, u32[]{:S(2)}, u32[]{:S(2)}) collective-permute-start(bf16[4,128,128]{2,1,0:T(8,128)(2,1)S(1)} %attend.10), channel_id=1, source_target_pairs={{0,14},{1,15},{2,12},{3,13},{4,10},{5,11},{6,8},{7,9},{8,6},{9,7},... | collective-permute-start | bytes 393224 | tf_op jit(solution)/shard_map/ppermute | solution.py:171
  57.6 22.9 %collective-permute-start.20 = (bf16[4,128,128]{2,1,0:T(8,128)(2,1)S(1)}, bf16[4,128,128]{2,1,0:T(8,128)(2,1)S(1)}, u32[]{:S(2)}, u32[]{:S(2)}) collective-permute-start(bf16[4,128,128]{2,1,0:T(8,128)(2,1)S(1)} %get-tuple-element.11), channel_id=1, source_target_pairs={{0,8},{1,9},{2,10},{3,11},{4,12},{5,13},{6,14},{7,15},{8,0},{9,1},... | collective-permute-start | bytes 393224 | tf_op jit(solution)/shard_map/ppermute | solution.py:171
  57.6 23.0 %collective-permute-start.21 = (bf16[4,128,128]{2,1,0:T(8,128)(2,1)S(1)}, bf16[4,128,128]{2,1,0:T(8,128)(2,1)S(1)}, u32[]{:S(2)}, u32[]{:S(2)}) collective-permute-start(bf16[4,128,128]{2,1,0:T(8,128)(2,1)S(1)} %get-tuple-element.12), channel_id=1, source_target_pairs={{0,10},{1,11},{2,8},{3,9},{4,14},{5,15},{6,12},{7,13},{8,2},{9,3},... | collective-permute-start | bytes 393224 | tf_op jit(solution)/shard_map/ppermute | solution.py:171
  62.2 11.3 %collective-permute-start.16 = (bf16[4,128,128]{2,1,0:T(8,128)(2,1)S(1)}, bf16[4,128,128]{2,1,0:T(8,128)(2,1)S(1)}, u32[]{:S(2)}, u32[]{:S(2)}) collective-permute-start(bf16[4,128,128]{2,1,0:T(8,128)(2,1)S(1)} %attend.9), channel_id=1, source_target_pairs={{0,2},{1,3},{2,0},{3,1},{4,6},{5,7},{6,4},{7,5},{8,10},{9,11},{10,... | collective-permute-start | bytes 393224 | tf_op jit(solution)/shard_map/ppermute | solution.py:171
  64.4 11.4 %collective-permute-start.18 = (bf16[4,128,128]{2,1,0:T(8,128)(2,1)S(1)}, bf16[4,128,128]{2,1,0:T(8,128)(2,1)S(1)}, u32[]{:S(2)}, u32[]{:S(2)}) collective-permute-start(bf16[4,128,128]{2,1,0:T(8,128)(2,1)S(1)} %attend.11), channel_id=1, source_target_pairs={{0,4},{1,5},{2,6},{3,7},{4,0},{5,1},{6,2},{7,3},{8,12},{9,13},{10,... | collective-permute-start | bytes 393224 | tf_op jit(solution)/shard_map/ppermute | solution.py:171
  72.0 7.6 %collective-permute-start.19 = (bf16[4,128,128]{2,1,0:T(8,128)(2,1)S(1)}, bf16[4,128,128]{2,1,0:T(8,128)(2,1)S(1)}, u32[]{:S(2)}, u32[]{:S(2)}) collective-permute-start(bf16[4,128,128]{2,1,0:T(8,128)(2,1)S(1)} %attend.12), channel_id=1, source_target_pairs={{0,6},{1,7},{2,4},{3,5},{4,2},{5,3},{6,0},{7,1},{8,14},{9,15},{10,... | collective-permute-start | bytes 393224 | tf_op jit(solution)/shard_map/ppermute | solution.py:171
  81.1 1.0 %copy-start.4 = (bf16[8,4,128,128]{3,1,0,2:T(4,128)(2,1)}, bf16[8,4,128,128]{3,1,0,2:T(4,128)(2,1)S(1)}, u32[]{:S(2)}) copy-start(bf16[8,4,128,128]{3,1,0,2:T(4,128)(2,1)S(1)} %copy_dynamic-update-slice_fusion) | copy-start | bytes 3145732

commit v4 on v3

--- a/solution.py
+++ b/solution.py
@@ -228,13 +228,14 @@
         for away, out in zip(aways, outs):
             tiles[away] = hop(out, 2 * away) if away else out
 
-    far_tiles, near_tiles = list(reversed(range(half, units))), list(reversed(range(half)))
-    attend(far_tiles[:1], [])
-    attend(far_tiles[1:2], [])
+    far_tiles = list(reversed(range(half, units)))
+    for away in far_tiles[:2] + [1]:
+        attend([away], [])
     for i in range(2, half, 2):
-        attend(far_tiles[i : i + 2], [])
-    for i, away in enumerate(near_tiles):
-        attend([away], [tiles[far_tiles[2 * i // half]]])
+        attend(far_tiles[i : i + 2], [tiles[1]])
+    for away in range(2, half):
+        attend([away], [tiles[1] if away <= half // 2 else tiles[far_tiles[0]]])
+    attend([0], [tiles[far_tiles[1]]])
     gathered = jnp.zeros((units, heads, rows, head_size), jnp.bfloat16)
     for away in range(units):
         gathered = lax.dynamic_update_index_in_dim(gathered, tiles[away], unit ^ away, 0)

time: 81.6 us -> 78.8 us (0.966); the launches traced: 82.1 us -> 77.8 us
  waiting for transfers between devices: 22.1 us -> 17.9 us
  starting transfers between devices: 40.7 us -> 37.7 us
  Pallas kernels: 14.3 us -> 16.8 us
    ppermute x22, waiting for transfers between devices: 22.1 us -> 17.9 us  [hop(): return lax.ppermute(x, 'seq', [(i, i ^ distance) for i in range(shards)])]
    ppermute x22, starting transfers between devices: 40.7 us -> 37.7 us  [hop(): return lax.ppermute(x, 'seq', [(i, i ^ distance) for i in range(shards)])]
    pallas_call x7, Pallas kernels: 11.9 us -> 14.5 us  [attend(): pl.pallas_call(functools.partial(attend_kernel, aways=aways, heads=heads,...]
  transfers between devices with their start and end apart: 22 -> 22, of which waited for: 9 -> 9; matrix products, arithmetic and copies ran while one was open for 2% -> 2% of each run, Pallas kernels for 13% -> 17%
where the time goes in v4:
time: 78.8 us; the launch traced here: 77.8 us
  starting transfers between devices  37.7 us (48%)
  waiting for transfers between devices  17.9 us (23%)
  Pallas kernels  16.8 us (21%)
  local copies, waits for them, and re-layouts  3.7 us (5%)
  other arithmetic  1.39 us (2%)
    ppermute x22, starting transfers between devices, hop(): return lax.ppermute(x, 'seq', [(i, i ^ distance) for i in range(shards)])  37.7 us
    ppermute x22, waiting for transfers between devices, hop(): return lax.ppermute(x, 'seq', [(i, i ^ distance) for i in range(shards)])  17.9 us
    pallas_call x7, Pallas kernels, attend(): pl.pallas_call(functools.partial(attend_kernel, aways=aways, heads=heads,...  14.5 us
    pallas_call x1, Pallas kernels, pack(): pl.pallas_call(functools.partial(pack_kernel, groups=groups, heads=heads,...  2.38 us
    dynamic_update_slice x9, local copies, waits for them, and re-layouts, per_device(): lax.dynamic_update_index_in_dim(gathered, tiles[away], unit ^ away, 0)  1.89 us
  transfers between devices with their start and end apart: 22, of which 9 were waited for; matrix products, arithmetic and copies ran while one was open for 2% of the time, Pallas kernels for 17%

profile of v4, /device:TPU:0, one launch (start us, length us, event | category | flops | bytes accessed | tf_op | source)
XLA Modules:
  0.0 77.8 jit_solution(17238271666390118924)
XLA Ops:
  0.0 1.2 %maximum_bitcast_fusion = bf16[8,2,128,128]{3,0,2,1:T(8,128)(2,1)S(1)} fusion(bf16[1,128,8,128]{3,2,1,0:T(8,128)(2,1)} %bitcast.76, bf16[1,128,8,128]{3,2,1,0:T(8,128)(2,1)} %bitcast.77), kind=kLoop, calls=%fused_computation.17 | loop fusion | flops 262144 | bytes 1048576 | tf_op jit(solution)/shard_map/transpose | solution.py:166
  1.2 0.1 copy.8
  1.3 0.1 copy-done.3
  1.4 0.4 copy.25
  1.9 5.1 %collective-permute-start.5 = (bf16[6,128,128]{2,1,0:T(8,128)(2,1)S(1)}, bf16[6,128,128]{2,1,0:T(8,128)(2,1)S(1)}, u32[]{:S(2)}, u32[]{:S(2)}) collective-permute-start(bf16[6,128,128]{2,1,0:T(8,128)(2,1)S(1)} %get-tuple-element.19), channel_id=1, source_target_pairs={{0,12},{1,13},{2,14},{3,15},{4,8},{5,9},{6,10},{7,11},{8,4},{9,5},... | collective-permute-start | bytes 589832 | tf_op jit(solution)/shard_map/ppermute | solution.py:171
  7.0 0.4 collective-permute-start.4
  7.3 0.1 fusion.14
  7.4 2.5 %collective-permute-start.6 = (bf16[6,128,128]{2,1,0:T(8,128)(2,1)S(1)}, bf16[6,128,128]{2,1,0:T(8,128)(2,1)S(1)}, u32[]{:S(2)}, u32[]{:S(2)}) collective-permute-start(bf16[6,128,128]{2,1,0:T(8,128)(2,1)S(1)} %get-tuple-element.13), channel_id=1, source_target_pairs={{0,14},{1,15},{2,12},{3,13},{4,10},{5,11},{6,8},{7,9},{8,6},{9,7},... | collective-permute-start | bytes 589832 | tf_op jit(solution)/shard_map/ppermute | solution.py:171
  10.0 1.5 %collective-permute-start = (bf16[6,128,128]{2,1,0:T(8,128)(2,1)S(1)}, bf16[6,128,128]{2,1,0:T(8,128)(2,1)S(1)}, u32[]{:S(2)}, u32[]{:S(2)}) collective-permute-start(bf16[6,128,128]{2,1,0:T(8,128)(2,1)S(1)} %get-tuple-element.15), channel_id=1, source_target_pairs={{0,2},{1,3},{2,0},{3,1},{4,6},{5,7},{6,4},{7,5},{8,10},{9,11},{10,... | collective-permute-start | bytes 589832 | tf_op jit(solution)/shard_map/ppermute | solution.py:171
  11.4 1.6 %collective-permute-start.1 = (bf16[6,128,128]{2,1,0:T(8,128)(2,1)S(1)}, bf16[6,128,128]{2,1,0:T(8,128)(2,1)S(1)}, u32[]{:S(2)}, u32[]{:S(2)}) collective-permute-start(bf16[6,128,128]{2,1,0:T(8,128)(2,1)S(1)} %get-tuple-element.16), channel_id=1, source_target_pairs={{0,4},{1,5},{2,6},{3,7},{4,0},{5,1},{6,2},{7,3},{8,12},{9,13},{10,... | collective-permute-start | bytes 589832 | tf_op jit(solution)/shard_map/ppermute | solution.py:171
  13.0 13.1 %collective-permute-start.2 = (bf16[6,128,128]{2,1,0:T(8,128)(2,1)S(1)}, bf16[6,128,128]{2,1,0:T(8,128)(2,1)S(1)}, u32[]{:S(2)}, u32[]{:S(2)}) collective-permute-start(bf16[6,128,128]{2,1,0:T(8,128)(2,1)S(1)} %get-tuple-element.17), channel_id=1, source_target_pairs={{0,6},{1,7},{2,4},{3,5},{4,2},{5,3},{6,0},{7,1},{8,14},{9,15},{10,... | collective-permute-start | bytes 589832 | tf_op jit(solution)/shard_map/ppermute | solution.py:171
  26.1 3.7 %collective-permute-done.4 = bf16[6,128,128]{2,1,0:T(8,128)(2,1)S(1)} collective-permute-done((bf16[6,128,128]{2,1,0:T(8,128)(2,1)S(1)}, bf16[6,128,128]{2,1,0:T(8,128)(2,1)S(1)}, u32[]{:S(2)}, u32[]{:S(2)}) %collective-permute-start.4) | collective-permute-done | bytes 196640 | tf_op jit(solution)/shard_map/ppermute | solution.py:171
  29.8 0.5 collective-permute-start.13
  30.3 0.1 collective-permute-start.12
  30.4 2.4 %collective-permute-done.2 = bf16[6,128,128]{2,1,0:T(8,128)(2,1)S(1)} collective-permute-done((bf16[6,128,128]{2,1,0:T(8,128)(2,1)S(1)}, bf16[6,128,128]{2,1,0:T(8,128)(2,1)S(1)}, u32[]{:S(2)}, u32[]{:S(2)}) %collective-permute-start.2) | collective-permute-done | bytes 196640 | tf_op jit(solution)/shard_map/ppermute | solution.py:171
  32.8 8.7 %collective-permute-done.3 = bf16[6,128,128]{2,1,0:T(8,128)(2,1)S(1)} collective-permute-done((bf16[6,128,128]{2,1,0:T(8,128)(2,1)S(1)}, bf16[6,128,128]{2,1,0:T(8,128)(2,1)S(1)}, u32[]{:S(2)}, u32[]{:S(2)}) %collective-permute-start.3) | collective-permute-done | bytes 196640 | tf_op jit(solution)/shard_map/ppermute | solution.py:171
  41.5 0.5 collective-permute-start.9
  42.1 0.4 collective-permute-start.11
  42.6 0.1 pad_add_fusion.place
  42.6 0.3 collective-permute-done.8
  43.0 0.3 collective-permute-done.9
  43.2 0.3 collective-permute-done.10
  43.5 0.3 collective-permute-done.11
  43.8 2.4 %pack_blocks.1 = (bf16[576,8,128]{2,1,0:T(8,128)(2,1)S(1)}, bf16[2,256,8,128]{3,2,1,0:T(8,128)(2,1)S(1)}) custom-call(s32[2]{0:T(128)S(1)} %pad_add_fusion.place, s32[256]{0:T(256)S(1)} %copy-done.1, s32[256]{0:T(256)S(1)} %copy-done.2, bf16[96,8,128]{2,1,0:T(8,128)(2,1)S(1)} %bitcast.55, bf16[96,8,128]{2,1,0:T(8,128)(2,1)S(1)} %bitcast.61, ...), custom_call_target="tpu_custom_call" | custom-call | flops 1000 | bytes 1000 | tf_op jit(solution)/shard_map/pack_blocks/pallas_call | solution.py:190
  46.2 1.1 %attend.9 = bf16[4,128,128]{2,1,0:T(8,128)(2,1)S(1)} custom-call(s32[2]{0:T(128)S(1)} %pad_add_fusion.place, s32[16]{0:T(128)S(1)} %copy-done, bf16[576,8,128]{2,1,0:T(8,128)(2,1)S(1)} %get-tuple-element.9.q_packed, bf16[2,256,8,128]{3,2,1,0:T(8,128)(2,1)S(1)} %get-tuple-element.10.kv_packed), custom_call_target="tpu_custom_call" | custom-call | flops 1000 | bytes 1000 | tf_op jit(solution)/shard_map/attend/pallas_call | solution.py:210
  47.3 1.1 %collective-permute-start.16 = (bf16[4,128,128]{2,1,0:T(8,128)(2,1)S(1)}, bf16[4,128,128]{2,1,0:T(8,128)(2,1)S(1)}, u32[]{:S(2)}, u32[]{:S(2)}) collective-permute-start(bf16[4,128,128]{2,1,0:T(8,128)(2,1)S(1)} %attend.9), channel_id=1, source_target_pairs={{0,2},{1,3},{2,0},{3,1},{4,6},{5,7},{6,4},{7,5},{8,10},{9,11},{10,... | collective-permute-start | bytes 393224 | tf_op jit(solution)/shard_map/ppermute | solution.py:171
  48.4 3.3 %attend.11 = bf16[4,128,128]{2,1,0:T(8,128)(2,1)S(1)} custom-call(s32[2]{0:T(128)S(1)} %pad_add_fusion.place, s32[16]{0:T(128)S(1)} %copy-done, bf16[576,8,128]{2,1,0:T(8,128)(2,1)S(1)} %get-tuple-element.9.q_packed, bf16[2,256,8,128]{3,2,1,0:T(8,128)(2,1)S(1)} %get-tuple-element.10.kv_packed), custom_call_target="tpu_custom_call" | custom-call | flops 1000 | bytes 1000 | tf_op jit(solution)/shard_map/attend/pallas_call | solution.py:210
  51.8 2.4 %collective-permute-start.18 = (bf16[4,128,128]{2,1,0:T(8,128)(2,1)S(1)}, bf16[4,128,128]{2,1,0:T(8,128)(2,1)S(1)}, u32[]{:S(2)}, u32[]{:S(2)}) collective-permute-start(bf16[4,128,128]{2,1,0:T(8,128)(2,1)S(1)} %attend.11), channel_id=1, source_target_pairs={{0,14},{1,15},{2,12},{3,13},{4,10},{5,11},{6,8},{7,9},{8,6},{9,7},... | collective-permute-start | bytes 393224 | tf_op jit(solution)/shard_map/ppermute | solution.py:171
  54.1 2.8 %attend.7 = bf16[4,128,128]{2,1,0:T(8,128)(2,1)S(1)} custom-call(s32[2]{0:T(128)S(1)} %pad_add_fusion.place, s32[16]{0:T(128)S(1)} %copy-done, bf16[576,8,128]{2,1,0:T(8,128)(2,1)S(1)} %get-tuple-element.9.q_packed, bf16[2,256,8,128]{3,2,1,0:T(8,128)(2,1)S(1)} %get-tuple-element.10.kv_packed), custom_call_target="tpu_custom_call" | custom-call | flops 1000 | bytes 1000 | tf_op jit(solution)/shard_map/attend/pallas_call | solution.py:210
  57.0 1.4 %attend.10 = bf16[4,128,128]{2,1,0:T(8,128)(2,1)S(1)} custom-call(s32[2]{0:T(128)S(1)} %pad_add_fusion.place, s32[16]{0:T(128)S(1)} %copy-done, bf16[576,8,128]{2,1,0:T(8,128)(2,1)S(1)} %get-tuple-element.9.q_packed, bf16[2,256,8,128]{3,2,1,0:T(8,128)(2,1)S(1)} %get-tuple-element.10.kv_packed, bf16[4,128,128]{2,1,0:T(8,128)(2,1)S(1)} %collective-permute-done.16.refs_0_), custom_call_target="tpu_custom_call" | custom-call | flops 1000 | bytes 1000 | tf_op jit(solution)/shard_map/attend/pallas_call | solution.py:210
  58.6 3.3 %attend.13 = (bf16[4,128,128]{2,1,0:T(8,128)(2,1)S(1)}, bf16[4,128,128]{2,1,0:T(8,128)(2,1)S(1)}) custom-call(s32[2]{0:T(128)S(1)} %pad_add_fusion.place, s32[16]{0:T(128)S(1)} %copy-done, bf16[576,8,128]{2,1,0:T(8,128)(2,1)S(1)} %get-tuple-element.9.q_packed, bf16[2,256,8,128]{3,2,1,0:T(8,128)(2,1)S(1)} %get-tuple-element.10.kv_packed, ...), custom_call_target="tpu_custom_call" | custom-call | flops 1000 | bytes 1000 | tf_op jit(solution)/shard_map/attend/pallas_call | solution.py:210
  61.9 2.9 %collective-permute-start.20 = (bf16[4,128,128]{2,1,0:T(8,128)(2,1)S(1)}, bf16[4,128,128]{2,1,0:T(8,128)(2,1)S(1)}, u32[]{:S(2)}, u32[]{:S(2)}) collective-permute-start(bf16[4,128,128]{2,1,0:T(8,128)(2,1)S(1)} %get-tuple-element.11), channel_id=1, source_target_pairs={{0,8},{1,9},{2,10},{3,11},{4,12},{5,13},{6,14},{7,15},{8,0},{9,1},... | collective-permute-start | bytes 393224 | tf_op jit(solution)/shard_map/ppermute | solution.py:171
  64.7 1.6 %collective-permute-start.21 = (bf16[4,128,128]{2,1,0:T(8,128)(2,1)S(1)}, bf16[4,128,128]{2,1,0:T(8,128)(2,1)S(1)}, u32[]{:S(2)}, u32[]{:S(2)}) collective-permute-start(bf16[4,128,128]{2,1,0:T(8,128)(2,1)S(1)} %get-tuple-element.12), channel_id=1, source_target_pairs={{0,10},{1,11},{2,8},{3,9},{4,14},{5,15},{6,12},{7,13},{8,2},{9,3},... | collective-permute-start | bytes 393224 | tf_op jit(solution)/shard_map/ppermute | solution.py:171
  66.3 1.3 %attend.12 = bf16[4,128,128]{2,1,0:T(8,128)(2,1)S(1)} custom-call(s32[2]{0:T(128)S(1)} %pad_add_fusion.place, s32[16]{0:T(128)S(1)} %copy-done, bf16[576,8,128]{2,1,0:T(8,128)(2,1)S(1)} %get-tuple-element.9.q_packed, bf16[2,256,8,128]{3,2,1,0:T(8,128)(2,1)S(1)} %get-tuple-element.10.kv_packed, bf16[4,128,128]{2,1,0:T(8,128)(2,1)S(1)} %collective-permute-done.18.refs_0_), custom_call_target="tpu_custom_call" | custom-call | flops 1000 | bytes 1000 | tf_op jit(solution)/shard_map/attend/pallas_call | solution.py:210
  67.7 3.9 %collective-permute-start.19 = (bf16[4,128,128]{2,1,0:T(8,128)(2,1)S(1)}, bf16[4,128,128]{2,1,0:T(8,128)(2,1)S(1)}, u32[]{:S(2)}, u32[]{:S(2)}) collective-permute-start(bf16[4,128,128]{2,1,0:T(8,128)(2,1)S(1)} %attend.12), channel_id=1, source_target_pairs={{0,6},{1,7},{2,4},{3,5},{4,2},{5,3},{6,0},{7,1},{8,14},{9,15},{10,... | collective-permute-start | bytes 393224 | tf_op jit(solution)/shard_map/ppermute | solution.py:171
  71.5 1.1 %attend.8 = bf16[4,128,128]{2,1,0:T(8,128)(2,1)S(1)} custom-call(s32[2]{0:T(128)S(1)} %pad_add_fusion.place, s32[16]{0:T(128)S(1)} %copy-done, bf16[576,8,128]{2,1,0:T(8,128)(2,1)S(1)} %get-tuple-element.9.q_packed, bf16[2,256,8,128]{3,2,1,0:T(8,128)(2,1)S(1)} %get-tuple-element.10.kv_packed, bf16[4,128,128]{2,1,0:T(8,128)(2,1)S(1)} %collective-permute-done.15.refs_0_), custom_call_target="tpu_custom_call" | custom-call | flops 1000 | bytes 1000 | tf_op jit(solution)/shard_map/attend/pallas_call | solution.py:210
  72.7 0.2 broadcast_in_dim.28
  73.0 0.8 %copy.9 = bf16[8,4,128,128]{3,1,0,2:T(4,128)(2,1)S(1)} copy(bf16[8,4,128,128]{3,2,1,0:T(8,128)(2,1)S(1)} %bitcast_dynamic-update-slice_fusion) | data formatting | bytes 2097152 | tf_op jit(solution)/shard_map/jit(dynamic_update_index_in_dim)/dynamic_update_slice | solution.py:241
  73.8 0.2 copy_dynamic-update-slice_fusion.6
  73.9 0.2 copy_dynamic-update-slice_fusion.5
  74.1 0.5 collective-permute-done.19
  74.6 0.1 copy_dynamic-update-slice_fusion.4
  74.8 0.2 copy_dynamic-update-slice_fusion.3
  74.9 1.4 %collective-permute-done.21 = bf16[4,128,128]{2,1,0:T(8,128)(2,1)S(1)} collective-permute-done((bf16[4,128,128]{2,1,0:T(8,128)(2,1)S(1)}, bf16[4,128,128]{2,1,0:T(8,128)(2,1)S(1)}, u32[]{:S(2)}, u32[]{:S(2)}) %collective-permute-start.21) | collective-permute-done | bytes 131104 | tf_op jit(solution)/shard_map/ppermute | solution.py:171
  76.3 0.1 copy_dynamic-update-slice_fusion.2
  76.5 0.2 copy_dynamic-update-slice_fusion.1
  76.6 0.2 copy_dynamic-update-slice_fusion
  76.8 1.0 %copy-done.4 = bf16[8,4,128,128]{3,1,0,2:T(4,128)(2,1)} copy-done((bf16[8,4,128,128]{3,1,0,2:T(4,128)(2,1)}, bf16[8,4,128,128]{3,1,0,2:T(4,128)(2,1)S(1)}, u32[]{:S(2)}) %copy-start.4) | copy-done | bytes 1048600
  (30 shorter events, 0.3 us)
Async XLA Ops:
  0.0 1.4 %copy-start.3 = (bf16[128,32,128]{2,1,0:T(8,128)(2,1)S(1)}, bf16[128,32,128]{2,1,0:T(8,128)(2,1)}, u32[]{:S(2)}) copy-start(bf16[128,32,128]{2,1,0:T(8,128)(2,1)} %param.6) | copy-start | bytes 3145732
  1.9 11.2 %collective-permute-start.5 = (bf16[6,128,128]{2,1,0:T(8,128)(2,1)S(1)}, bf16[6,128,128]{2,1,0:T(8,128)(2,1)S(1)}, u32[]{:S(2)}, u32[]{:S(2)}) collective-permute-start(bf16[6,128,128]{2,1,0:T(8,128)(2,1)S(1)} %get-tuple-element.19), channel_id=1, source_target_pairs={{0,12},{1,13},{2,14},{3,15},{4,8},{5,9},{6,10},{7,11},{8,4},{9,5},... | collective-permute-start | bytes 589832 | tf_op jit(solution)/shard_map/ppermute | solution.py:171
  7.0 22.8 %collective-permute-start.4 = (bf16[6,128,128]{2,1,0:T(8,128)(2,1)S(1)}, bf16[6,128,128]{2,1,0:T(8,128)(2,1)S(1)}, u32[]{:S(2)}, u32[]{:S(2)}) collective-permute-start(bf16[6,128,128]{2,1,0:T(8,128)(2,1)S(1)} %get-tuple-element.20), channel_id=1, source_target_pairs={{0,10},{1,11},{2,8},{3,9},{4,14},{5,15},{6,12},{7,13},{8,2},{9,3},... | collective-permute-start | bytes 589832 | tf_op jit(solution)/shard_map/ppermute | solution.py:171
  7.3 36.5 %copy-start.1 = (s32[256]{0:T(256)S(1)}, s32[256]{0:T(256)}, u32[]{:S(2)}) copy-start(s32[256]{0:T(256)} %dest.1) | copy-start | bytes 3076
  7.3 36.5 %copy-start.2 = (s32[256]{0:T(256)S(1)}, s32[256]{0:T(256)}, u32[]{:S(2)}) copy-start(s32[256]{0:T(256)} %slot.1) | copy-start | bytes 3076
  7.4 22.4 %collective-permute-start.6 = (bf16[6,128,128]{2,1,0:T(8,128)(2,1)S(1)}, bf16[6,128,128]{2,1,0:T(8,128)(2,1)S(1)}, u32[]{:S(2)}, u32[]{:S(2)}) collective-permute-start(bf16[6,128,128]{2,1,0:T(8,128)(2,1)S(1)} %get-tuple-element.13), channel_id=1, source_target_pairs={{0,14},{1,15},{2,12},{3,13},{4,10},{5,11},{6,8},{7,9},{8,6},{9,7},... | collective-permute-start | bytes 589832 | tf_op jit(solution)/shard_map/ppermute | solution.py:171
  10.0 19.9 %collective-permute-start = (bf16[6,128,128]{2,1,0:T(8,128)(2,1)S(1)}, bf16[6,128,128]{2,1,0:T(8,128)(2,1)S(1)}, u32[]{:S(2)}, u32[]{:S(2)}) collective-permute-start(bf16[6,128,128]{2,1,0:T(8,128)(2,1)S(1)} %get-tuple-element.15), channel_id=1, source_target_pairs={{0,2},{1,3},{2,0},{3,1},{4,6},{5,7},{6,4},{7,5},{8,10},{9,11},{10,... | collective-permute-start | bytes 589832 | tf_op jit(solution)/shard_map/ppermute | solution.py:171
  11.4 18.9 %collective-permute-start.1 = (bf16[6,128,128]{2,1,0:T(8,128)(2,1)S(1)}, bf16[6,128,128]{2,1,0:T(8,128)(2,1)S(1)}, u32[]{:S(2)}, u32[]{:S(2)}) collective-permute-start(bf16[6,128,128]{2,1,0:T(8,128)(2,1)S(1)} %get-tuple-element.16), channel_id=1, source_target_pairs={{0,4},{1,5},{2,6},{3,7},{4,0},{5,1},{6,2},{7,3},{8,12},{9,13},{10,... | collective-permute-start | bytes 589832 | tf_op jit(solution)/shard_map/ppermute | solution.py:171
  13.0 19.8 %collective-permute-start.2 = (bf16[6,128,128]{2,1,0:T(8,128)(2,1)S(1)}, bf16[6,128,128]{2,1,0:T(8,128)(2,1)S(1)}, u32[]{:S(2)}, u32[]{:S(2)}) collective-permute-start(bf16[6,128,128]{2,1,0:T(8,128)(2,1)S(1)} %get-tuple-element.17), channel_id=1, source_target_pairs={{0,6},{1,7},{2,4},{3,5},{4,2},{5,3},{6,0},{7,1},{8,14},{9,15},{10,... | collective-permute-start | bytes 589832 | tf_op jit(solution)/shard_map/ppermute | solution.py:171
  29.8 11.7 %collective-permute-start.3 = (bf16[6,128,128]{2,1,0:T(8,128)(2,1)S(1)}, bf16[6,128,128]{2,1,0:T(8,128)(2,1)S(1)}, u32[]{:S(2)}, u32[]{:S(2)}) collective-permute-start(bf16[6,128,128]{2,1,0:T(8,128)(2,1)S(1)} %get-tuple-element.18), channel_id=1, source_target_pairs={{0,8},{1,9},{2,10},{3,11},{4,12},{5,13},{6,14},{7,15},{8,0},{9,1},... | collective-permute-start | bytes 589832 | tf_op jit(solution)/shard_map/ppermute | solution.py:171
  29.8 11.7 %collective-permute-start.7 = (bf16[6,128,128]{2,1,0:T(8,128)(2,1)S(1)}, bf16[6,128,128]{2,1,0:T(8,128)(2,1)S(1)}, u32[]{:S(2)}, u32[]{:S(2)}) collective-permute-start(bf16[6,128,128]{2,1,0:T(8,128)(2,1)S(1)} %bitcast.54), channel_id=1, source_target_pairs={{0,1},{1,0},{2,3},{3,2},{4,5},{5,4},{6,7},{7,6},{8,9},{9,8},{10,11... | collective-permute-start | bytes 589832 | tf_op jit(solution)/shard_map/ppermute | solution.py:171
  29.8 12.2 %collective-permute-start.13 = (bf16[6,128,128]{2,1,0:T(8,128)(2,1)S(1)}, bf16[6,128,128]{2,1,0:T(8,128)(2,1)S(1)}, u32[]{:S(2)}, u32[]{:S(2)}) collective-permute-start(bf16[6,128,128]{2,1,0:T(8,128)(2,1)S(1)} %collective-permute-done.5), channel_id=1, source_target_pairs={{0,1},{1,0},{2,3},{3,2},{4,5},{5,4},{6,7},{7,6},{8,9},{9,8},{10,11... | collective-permute-start | bytes 589832 | tf_op jit(solution)/shard_map/ppermute | solution.py:171
  30.3 11.8 %collective-permute-start.12 = (bf16[6,128,128]{2,1,0:T(8,128)(2,1)S(1)}, bf16[6,128,128]{2,1,0:T(8,128)(2,1)S(1)}, u32[]{:S(2)}, u32[]{:S(2)}) collective-permute-start(bf16[6,128,128]{2,1,0:T(8,128)(2,1)S(1)} %collective-permute-done.4), channel_id=1, source_target_pairs={{0,1},{1,0},{2,3},{3,2},{4,5},{5,4},{6,7},{7,6},{8,9},{9,8},{10,11... | collective-permute-start | bytes 589832 | tf_op jit(solution)/shard_map/ppermute | solution.py:171
  32.8 9.8 %collective-permute-start.14 = (bf16[6,128,128]{2,1,0:T(8,128)(2,1)S(1)}, bf16[6,128,128]{2,1,0:T(8,128)(2,1)S(1)}, u32[]{:S(2)}, u32[]{:S(2)}) collective-permute-start(bf16[6,128,128]{2,1,0:T(8,128)(2,1)S(1)} %collective-permute-done.6), channel_id=1, source_target_pairs={{0,1},{1,0},{2,3},{3,2},{4,5},{5,4},{6,7},{7,6},{8,9},{9,8},{10,11... | collective-permute-start | bytes 589832 | tf_op jit(solution)/shard_map/ppermute | solution.py:171
  41.5 1.4 %collective-permute-start.8 = (bf16[6,128,128]{2,1,0:T(8,128)(2,1)S(1)}, bf16[6,128,128]{2,1,0:T(8,128)(2,1)S(1)}, u32[]{:S(2)}, u32[]{:S(2)}) collective-permute-start(bf16[6,128,128]{2,1,0:T(8,128)(2,1)S(1)} %collective-permute-done), channel_id=1, source_target_pairs={{0,1},{1,0},{2,3},{3,2},{4,5},{5,4},{6,7},{7,6},{8,9},{9,8},{10,11... | collective-permute-start | bytes 589832 | tf_op jit(solution)/shard_map/ppermute | solution.py:171
  41.5 1.7 %collective-permute-start.9 = (bf16[6,128,128]{2,1,0:T(8,128)(2,1)S(1)}, bf16[6,128,128]{2,1,0:T(8,128)(2,1)S(1)}, u32[]{:S(2)}, u32[]{:S(2)}) collective-permute-start(bf16[6,128,128]{2,1,0:T(8,128)(2,1)S(1)} %collective-permute-done.1), channel_id=1, source_target_pairs={{0,1},{1,0},{2,3},{3,2},{4,5},{5,4},{6,7},{7,6},{8,9},{9,8},{10,11... | collective-permute-start | bytes 589832 | tf_op jit(solution)/shard_map/ppermute | solution.py:171
  42.0 1.5 %collective-permute-start.10 = (bf16[6,128,128]{2,1,0:T(8,128)(2,1)S(1)}, bf16[6,128,128]{2,1,0:T(8,128)(2,1)S(1)}, u32[]{:S(2)}, u32[]{:S(2)}) collective-permute-start(bf16[6,128,128]{2,1,0:T(8,128)(2,1)S(1)} %collective-permute-done.2), channel_id=1, source_target_pairs={{0,1},{1,0},{2,3},{3,2},{4,5},{5,4},{6,7},{7,6},{8,9},{9,8},{10,11... | collective-permute-start | bytes 589832 | tf_op jit(solution)/shard_map/ppermute | solution.py:171
  42.1 1.7 %collective-permute-start.11 = (bf16[6,128,128]{2,1,0:T(8,128)(2,1)S(1)}, bf16[6,128,128]{2,1,0:T(8,128)(2,1)S(1)}, u32[]{:S(2)}, u32[]{:S(2)}) collective-permute-start(bf16[6,128,128]{2,1,0:T(8,128)(2,1)S(1)} %collective-permute-done.3), channel_id=1, source_target_pairs={{0,1},{1,0},{2,3},{3,2},{4,5},{5,4},{6,7},{7,6},{8,9},{9,8},{10,11... | collective-permute-start | bytes 589832 | tf_op jit(solution)/shard_map/ppermute | solution.py:171
  43.8 2.4 %copy-start = (s32[16]{0:T(128)S(1)}, s32[16]{0:T(128)}, u32[]{:S(2)}) copy-start(s32[16]{0:T(128)} %lengths.13) | copy-start | bytes 196
  47.3 9.7 %collective-permute-start.16 = (bf16[4,128,128]{2,1,0:T(8,128)(2,1)S(1)}, bf16[4,128,128]{2,1,0:T(8,128)(2,1)S(1)}, u32[]{:S(2)}, u32[]{:S(2)}) collective-permute-start(bf16[4,128,128]{2,1,0:T(8,128)(2,1)S(1)} %attend.9), channel_id=1, source_target_pairs={{0,2},{1,3},{2,0},{3,1},{4,6},{5,7},{6,4},{7,5},{8,10},{9,11},{10,... | collective-permute-start | bytes 393224 | tf_op jit(solution)/shard_map/ppermute | solution.py:171
  51.8 14.6 %collective-permute-start.18 = (bf16[4,128,128]{2,1,0:T(8,128)(2,1)S(1)}, bf16[4,128,128]{2,1,0:T(8,128)(2,1)S(1)}, u32[]{:S(2)}, u32[]{:S(2)}) collective-permute-start(bf16[4,128,128]{2,1,0:T(8,128)(2,1)S(1)} %attend.11), channel_id=1, source_target_pairs={{0,14},{1,15},{2,12},{3,13},{4,10},{5,11},{6,8},{7,9},{8,6},{9,7},... | collective-permute-start | bytes 393224 | tf_op jit(solution)/shard_map/ppermute | solution.py:171
  57.0 14.6 %collective-permute-start.15 = (bf16[4,128,128]{2,1,0:T(8,128)(2,1)S(1)}, bf16[4,128,128]{2,1,0:T(8,128)(2,1)S(1)}, u32[]{:S(2)}, u32[]{:S(2)}) collective-permute-start(bf16[4,128,128]{2,1,0:T(8,128)(2,1)S(1)} %attend.7), channel_id=1, source_target_pairs={{0,12},{1,13},{2,14},{3,15},{4,8},{5,9},{6,10},{7,11},{8,4},{9,5},... | collective-permute-start | bytes 393224 | tf_op jit(solution)/shard_map/ppermute | solution.py:171
  58.5 15.4 %collective-permute-start.17 = (bf16[4,128,128]{2,1,0:T(8,128)(2,1)S(1)}, bf16[4,128,128]{2,1,0:T(8,128)(2,1)S(1)}, u32[]{:S(2)}, u32[]{:S(2)}) collective-permute-start(bf16[4,128,128]{2,1,0:T(8,128)(2,1)S(1)} %attend.10), channel_id=1, source_target_pairs={{0,4},{1,5},{2,6},{3,7},{4,0},{5,1},{6,2},{7,3},{8,12},{9,13},{10,... | collective-permute-start | bytes 393224 | tf_op jit(solution)/shard_map/ppermute | solution.py:171
  61.9 12.9 %collective-permute-start.20 = (bf16[4,128,128]{2,1,0:T(8,128)(2,1)S(1)}, bf16[4,128,128]{2,1,0:T(8,128)(2,1)S(1)}, u32[]{:S(2)}, u32[]{:S(2)}) collective-permute-start(bf16[4,128,128]{2,1,0:T(8,128)(2,1)S(1)} %get-tuple-element.11), channel_id=1, source_target_pairs={{0,8},{1,9},{2,10},{3,11},{4,12},{5,13},{6,14},{7,15},{8,0},{9,1},... | collective-permute-start | bytes 393224 | tf_op jit(solution)/shard_map/ppermute | solution.py:171
  64.7 11.6 %collective-permute-start.21 = (bf16[4,128,128]{2,1,0:T(8,128)(2,1)S(1)}, bf16[4,128,128]{2,1,0:T(8,128)(2,1)S(1)}, u32[]{:S(2)}, u32[]{:S(2)}) collective-permute-start(bf16[4,128,128]{2,1,0:T(8,128)(2,1)S(1)} %get-tuple-element.12), channel_id=1, source_target_pairs={{0,10},{1,11},{2,8},{3,9},{4,14},{5,15},{6,12},{7,13},{8,2},{9,3},... | collective-permute-start | bytes 393224 | tf_op jit(solution)/shard_map/ppermute | solution.py:171
  67.7 7.0 %collective-permute-start.19 = (bf16[4,128,128]{2,1,0:T(8,128)(2,1)S(1)}, bf16[4,128,128]{2,1,0:T(8,128)(2,1)S(1)}, u32[]{:S(2)}, u32[]{:S(2)}) collective-permute-start(bf16[4,128,128]{2,1,0:T(8,128)(2,1)S(1)} %attend.12), channel_id=1, source_target_pairs={{0,6},{1,7},{2,4},{3,5},{4,2},{5,3},{6,0},{7,1},{8,14},{9,15},{10,... | collective-permute-start | bytes 393224 | tf_op jit(solution)/shard_map/ppermute | solution.py:171
  76.8 1.0 %copy-start.4 = (bf16[8,4,128,128]{3,1,0,2:T(4,128)(2,1)}, bf16[8,4,128,128]{3,1,0,2:T(4,128)(2,1)S(1)}, u32[]{:S(2)}) copy-start(bf16[8,4,128,128]{3,1,0,2:T(4,128)(2,1)S(1)} %copy_dynamic-update-slice_fusion) | copy-start | bytes 3145732

commit v5 on v4

--- a/solution.py
+++ b/solution.py
@@ -61,10 +61,10 @@
         begins[d] = begin
         begin = begin + lengths[d]
 
-    step = aways[1] - aways[0] if count > 1 else 0
-
     def one_tile(turn, carry):
-        away = aways[0] + turn * step
+        away = aways[0]
+        for i in range(1, count):
+            away = jnp.where(turn == i, aways[i], away)
         tile = lax.bitwise_xor(place[0], away)
         q_start = (tile * 2 + place[1]) * rows
         q_end = q_start + rows
@@ -81,8 +81,7 @@
             return jnp.where(q_pos >= begin, begin, firsts)
 
         firsts = lax.fori_loop(before, within, later_doc, jnp.full((rows, 1), first, jnp.int32))
-        chunks = lax.div(q_end - first + chunk - 1, chunk)
-        start = jnp.maximum(q_end - chunks * chunk, 0)
+        needed = q_end - first
         q_at = pl.multiple_of(tile * (heads * rows), rows)
 
         def masked_scores(k_start, width):
@@ -101,11 +100,11 @@
                 def _(out=out):
                     out[...] = value.astype(jnp.bfloat16).reshape(out.shape)
 
-        for straight in range(1, 2 + 1):
-
-            @pl.when(chunks == straight)
-            def _(width=min(straight * chunk, length)):
-                k_start = pl.multiple_of(start, rows)
+        for lower, width in ((0, chunk // 2), (chunk // 2, chunk)):
+
+            @pl.when((needed > lower) & (needed <= width))
+            def _(width=width):
+                k_start = pl.multiple_of(jnp.maximum(q_end - width, 0), rows)
                 s = masked_scores(k_start, width)
                 peak = jnp.max(s, axis=1, keepdims=True) * factor
                 weights = jnp.exp2(s * factor - peak)
@@ -115,8 +114,10 @@
                     weights.astype(jnp.bfloat16), v, preferred_element_type=jnp.float32
                 ) * (1.0 / sums)
 
-        @pl.when(chunks > 2)
+        @pl.when(needed > chunk)
         def _():
+            chunks = lax.div(needed + chunk - 1, chunk)
+            start = jnp.maximum(q_end - chunks * chunk, 0)
             top[...] = jnp.full_like(top, far_below)
 
             def score_chunk(j, carry):
@@ -202,9 +203,9 @@
     groups = [(column, away) for column in range(2) for away in everyone]
     packed = pack(groups, [x[away] for x in (near, far) for away in everyone], (), small)
 
-    chunk = min(256, span)
+    chunk = min(512, span)
     most = -(-(span + rows - 1) // chunk)
-    tiles = {}
+    tiles, raw = {}, {}
 
     def attend(aways, after):
         outs = pl.pallas_call(
@@ -226,16 +227,17 @@
             name="attend",
         )(place, doc_lengths, *packed, *after)
         for away, out in zip(aways, outs):
+            raw[away] = out
             tiles[away] = hop(out, 2 * away) if away else out
 
     far_tiles = list(reversed(range(half, units)))
-    for away in far_tiles[:2] + [1]:
-        attend([away], [])
+    attend((far_tiles[0], 1), [])
+    attend((far_tiles[1], 2), [raw[far_tiles[0]]])
     for i in range(2, half, 2):
-        attend(far_tiles[i : i + 2], [tiles[1]])
-    for away in range(2, half):
-        attend([away], [tiles[1] if away <= half // 2 else tiles[far_tiles[0]]])
-    attend([0], [tiles[far_tiles[1]]])
+        attend(tuple(far_tiles[i : i + 2]), [tiles[1]])
+    for away in range(3, half):
+        attend((away,), [tiles[far_tiles[0]]])
+    attend((0,), [tiles[far_tiles[1]]])
     gathered = jnp.zeros((units, heads, rows, head_size), jnp.bfloat16)
     for away in range(units):
         gathered = lax.dynamic_update_index_in_dim(gathered, tiles[away], unit ^ away, 0)

time: 78.8 us -> 76.7 us (0.973)
  Pallas kernels: 16.8 us -> 12.3 us
  waiting for transfers between devices: 17.9 us -> 20.4 us
    pallas_call x7 -> x5, Pallas kernels: 14.5 us -> 9.9 us  [attend(): pl.pallas_call(functools.partial(attend_kernel, aways=aways, heads=heads,...]
    ppermute x22, waiting for transfers between devices: 17.9 us -> 20.4 us  [hop(): return lax.ppermute(x, 'seq', [(i, i ^ distance) for i in range(shards)])]
  transfers between devices with their start and end apart: 22 -> 22, of which waited for: 9 -> 10; matrix products, arithmetic and copies ran while one was open for 2% -> 2% of each run, Pallas kernels for 17% -> 9%
where the time goes in v5:
time: 76.7 us; the launch traced here: 75.9 us
  starting transfers between devices  37.9 us (49%)
  waiting for transfers between devices  20.4 us (27%)
  Pallas kernels  12.3 us (16%)
  local copies, waits for them, and re-layouts  3.7 us (5%)
  other arithmetic  1.39 us (2%)
    ppermute x22, starting transfers between devices, hop(): return lax.ppermute(x, 'seq', [(i, i ^ distance) for i in range(shards)])  37.9 us
    ppermute x22, waiting for transfers between devices, hop(): return lax.ppermute(x, 'seq', [(i, i ^ distance) for i in range(shards)])  20.4 us
    pallas_call x5, Pallas kernels, attend(): pl.pallas_call(functools.partial(attend_kernel, aways=aways, heads=heads,...  9.9 us
    pallas_call x1, Pallas kernels, pack(): pl.pallas_call(functools.partial(pack_kernel, groups=groups, heads=heads,...  2.36 us
    dynamic_update_slice x9, local copies, waits for them, and re-layouts, per_device(): lax.dynamic_update_index_in_dim(gathered, tiles[away], unit ^ away, 0)  1.88 us
  transfers between devices with their start and end apart: 22, of which 10 were waited for; matrix products, arithmetic and copies ran while one was open for 2% of the time, Pallas kernels for 9%

profile of v5, /device:TPU:0, one launch (start us, length us, event | category | flops | bytes accessed | tf_op | source)
XLA Modules:
  0.0 75.9 jit_solution(7552623525920223109)
XLA Ops:
  0.0 1.2 %maximum_bitcast_fusion = bf16[8,2,128,128]{3,0,2,1:T(8,128)(2,1)S(1)} fusion(bf16[1,128,8,128]{3,2,1,0:T(8,128)(2,1)} %bitcast.76, bf16[1,128,8,128]{3,2,1,0:T(8,128)(2,1)} %bitcast.77), kind=kLoop, calls=%fused_computation.17 | loop fusion | flops 262144 | bytes 1048576 | tf_op jit(solution)/shard_map/transpose | solution.py:167
  1.2 0.1 copy.8
  1.3 0.1 copy-done.3
  1.4 0.4 copy.25
  1.9 5.1 %collective-permute-start.5 = (bf16[6,128,128]{2,1,0:T(8,128)(2,1)S(1)}, bf16[6,128,128]{2,1,0:T(8,128)(2,1)S(1)}, u32[]{:S(2)}, u32[]{:S(2)}) collective-permute-start(bf16[6,128,128]{2,1,0:T(8,128)(2,1)S(1)} %get-tuple-element.27), channel_id=1, source_target_pairs={{0,12},{1,13},{2,14},{3,15},{4,8},{5,9},{6,10},{7,11},{8,4},{9,5},... | collective-permute-start | bytes 589832 | tf_op jit(solution)/shard_map/ppermute | solution.py:172
  7.0 0.4 collective-permute-start.4
  7.3 0.1 fusion.14
  7.4 2.5 %collective-permute-start.6 = (bf16[6,128,128]{2,1,0:T(8,128)(2,1)S(1)}, bf16[6,128,128]{2,1,0:T(8,128)(2,1)S(1)}, u32[]{:S(2)}, u32[]{:S(2)}) collective-permute-start(bf16[6,128,128]{2,1,0:T(8,128)(2,1)S(1)} %get-tuple-element.21), channel_id=1, source_target_pairs={{0,14},{1,15},{2,12},{3,13},{4,10},{5,11},{6,8},{7,9},{8,6},{9,7},... | collective-permute-start | bytes 589832 | tf_op jit(solution)/shard_map/ppermute | solution.py:172
  10.0 1.5 %collective-permute-start = (bf16[6,128,128]{2,1,0:T(8,128)(2,1)S(1)}, bf16[6,128,128]{2,1,0:T(8,128)(2,1)S(1)}, u32[]{:S(2)}, u32[]{:S(2)}) collective-permute-start(bf16[6,128,128]{2,1,0:T(8,128)(2,1)S(1)} %get-tuple-element.23), channel_id=1, source_target_pairs={{0,2},{1,3},{2,0},{3,1},{4,6},{5,7},{6,4},{7,5},{8,10},{9,11},{10,... | collective-permute-start | bytes 589832 | tf_op jit(solution)/shard_map/ppermute | solution.py:172
  11.4 1.6 %collective-permute-start.1 = (bf16[6,128,128]{2,1,0:T(8,128)(2,1)S(1)}, bf16[6,128,128]{2,1,0:T(8,128)(2,1)S(1)}, u32[]{:S(2)}, u32[]{:S(2)}) collective-permute-start(bf16[6,128,128]{2,1,0:T(8,128)(2,1)S(1)} %get-tuple-element.24), channel_id=1, source_target_pairs={{0,4},{1,5},{2,6},{3,7},{4,0},{5,1},{6,2},{7,3},{8,12},{9,13},{10,... | collective-permute-start | bytes 589832 | tf_op jit(solution)/shard_map/ppermute | solution.py:172
  13.0 13.1 %collective-permute-start.2 = (bf16[6,128,128]{2,1,0:T(8,128)(2,1)S(1)}, bf16[6,128,128]{2,1,0:T(8,128)(2,1)S(1)}, u32[]{:S(2)}, u32[]{:S(2)}) collective-permute-start(bf16[6,128,128]{2,1,0:T(8,128)(2,1)S(1)} %get-tuple-element.25), channel_id=1, source_target_pairs={{0,6},{1,7},{2,4},{3,5},{4,2},{5,3},{6,0},{7,1},{8,14},{9,15},{10,... | collective-permute-start | bytes 589832 | tf_op jit(solution)/shard_map/ppermute | solution.py:172
  26.1 3.7 %collective-permute-done.4 = bf16[6,128,128]{2,1,0:T(8,128)(2,1)S(1)} collective-permute-done((bf16[6,128,128]{2,1,0:T(8,128)(2,1)S(1)}, bf16[6,128,128]{2,1,0:T(8,128)(2,1)S(1)}, u32[]{:S(2)}, u32[]{:S(2)}) %collective-permute-start.4) | collective-permute-done | bytes 196640 | tf_op jit(solution)/shard_map/ppermute | solution.py:172
  29.8 0.5 collective-permute-start.13
  30.3 0.1 collective-permute-start.12
  30.4 2.4 %collective-permute-done.2 = bf16[6,128,128]{2,1,0:T(8,128)(2,1)S(1)} collective-permute-done((bf16[6,128,128]{2,1,0:T(8,128)(2,1)S(1)}, bf16[6,128,128]{2,1,0:T(8,128)(2,1)S(1)}, u32[]{:S(2)}, u32[]{:S(2)}) %collective-permute-start.2) | collective-permute-done | bytes 196640 | tf_op jit(solution)/shard_map/ppermute | solution.py:172
  32.8 8.7 %collective-permute-done.3 = bf16[6,128,128]{2,1,0:T(8,128)(2,1)S(1)} collective-permute-done((bf16[6,128,128]{2,1,0:T(8,128)(2,1)S(1)}, bf16[6,128,128]{2,1,0:T(8,128)(2,1)S(1)}, u32[]{:S(2)}, u32[]{:S(2)}) %collective-permute-start.3) | collective-permute-done | bytes 196640 | tf_op jit(solution)/shard_map/ppermute | solution.py:172
  41.5 0.5 collective-permute-start.9
  42.1 0.4 collective-permute-start.11
  42.6 0.1 pad_add_fusion.place
  42.6 0.3 collective-permute-done.8
  43.0 0.3 collective-permute-done.9
  43.2 0.3 collective-permute-done.10
  43.5 0.3 collective-permute-done.11
  43.8 2.4 %pack_blocks.1 = (bf16[576,8,128]{2,1,0:T(8,128)(2,1)S(1)}, bf16[2,256,8,128]{3,2,1,0:T(8,128)(2,1)S(1)}) custom-call(s32[2]{0:T(128)S(1)} %pad_add_fusion.place, s32[256]{0:T(256)S(1)} %copy-done.1, s32[256]{0:T(256)S(1)} %copy-done.2, bf16[96,8,128]{2,1,0:T(8,128)(2,1)S(1)} %bitcast.54, bf16[96,8,128]{2,1,0:T(8,128)(2,1)S(1)} %bitcast.61, ...), custom_call_target="tpu_custom_call" | custom-call | flops 1000 | bytes 1000 | tf_op jit(solution)/shard_map/pack_blocks/pallas_call | solution.py:191
  46.2 2.8 %attend.5 = (bf16[4,128,128]{2,1,0:T(8,128)(2,1)S(1)}, bf16[4,128,128]{2,1,0:T(8,128)(2,1)S(1)}) custom-call(s32[2]{0:T(128)S(1)} %pad_add_fusion.place, s32[16]{0:T(128)S(1)} %copy-done, bf16[576,8,128]{2,1,0:T(8,128)(2,1)S(1)} %get-tuple-element.13.q_packed, bf16[2,256,8,128]{3,2,1,0:T(8,128)(2,1)S(1)} %get-tuple-element.14.kv_packed), custom_call_target="tpu_custom_call" | custom-call | flops 1000 | bytes 1000 | tf_op jit(solution)/shard_map/attend/pallas_call | solution.py:211
  49.0 1.1 %collective-permute-start.16 = (bf16[4,128,128]{2,1,0:T(8,128)(2,1)S(1)}, bf16[4,128,128]{2,1,0:T(8,128)(2,1)S(1)}, u32[]{:S(2)}, u32[]{:S(2)}) collective-permute-start(bf16[4,128,128]{2,1,0:T(8,128)(2,1)S(1)} %get-tuple-element.17), channel_id=1, source_target_pairs={{0,2},{1,3},{2,0},{3,1},{4,6},{5,7},{6,4},{7,5},{8,10},{9,11},{10,... | collective-permute-start | bytes 393224 | tf_op jit(solution)/shard_map/ppermute | solution.py:172
  50.1 2.3 %collective-permute-start.18 = (bf16[4,128,128]{2,1,0:T(8,128)(2,1)S(1)}, bf16[4,128,128]{2,1,0:T(8,128)(2,1)S(1)}, u32[]{:S(2)}, u32[]{:S(2)}) collective-permute-start(bf16[4,128,128]{2,1,0:T(8,128)(2,1)S(1)} %get-tuple-element.15.refs_0_), channel_id=1, source_target_pairs={{0,14},{1,15},{2,12},{3,13},{4,10},{5,11},{6,8},{7,9},{8,6},{9,7},... | collective-permute-start | bytes 393224 | tf_op jit(solution)/shard_map/ppermute | solution.py:172
  52.4 2.8 %attend.6 = (bf16[4,128,128]{2,1,0:T(8,128)(2,1)S(1)}, bf16[4,128,128]{2,1,0:T(8,128)(2,1)S(1)}) custom-call(s32[2]{0:T(128)S(1)} %pad_add_fusion.place, s32[16]{0:T(128)S(1)} %copy-done, bf16[576,8,128]{2,1,0:T(8,128)(2,1)S(1)} %get-tuple-element.13.q_packed, bf16[2,256,8,128]{3,2,1,0:T(8,128)(2,1)S(1)} %get-tuple-element.14.kv_packed, ...), custom_call_target="tpu_custom_call" | custom-call | flops 1000 | bytes 1000 | tf_op jit(solution)/shard_map/attend/pallas_call | solution.py:211
  55.2 1.0 %collective-permute-start.15 = (bf16[4,128,128]{2,1,0:T(8,128)(2,1)S(1)}, bf16[4,128,128]{2,1,0:T(8,128)(2,1)S(1)}, u32[]{:S(2)}, u32[]{:S(2)}) collective-permute-start(bf16[4,128,128]{2,1,0:T(8,128)(2,1)S(1)} %get-tuple-element.16), channel_id=1, source_target_pairs={{0,12},{1,13},{2,14},{3,15},{4,8},{5,9},{6,10},{7,11},{8,4},{9,5},... | collective-permute-start | bytes 393224 | tf_op jit(solution)/shard_map/ppermute | solution.py:172
  56.2 2.0 %attend.9 = (bf16[4,128,128]{2,1,0:T(8,128)(2,1)S(1)}, bf16[4,128,128]{2,1,0:T(8,128)(2,1)S(1)}) custom-call(s32[2]{0:T(128)S(1)} %pad_add_fusion.place, s32[16]{0:T(128)S(1)} %copy-done, bf16[576,8,128]{2,1,0:T(8,128)(2,1)S(1)} %get-tuple-element.13.q_packed, bf16[2,256,8,128]{3,2,1,0:T(8,128)(2,1)S(1)} %get-tuple-element.14.kv_packed, ...), custom_call_target="tpu_custom_call" | custom-call | flops 1000 | bytes 1000 | tf_op jit(solution)/shard_map/attend/pallas_call | solution.py:211
  58.2 3.3 %collective-permute-start.20 = (bf16[4,128,128]{2,1,0:T(8,128)(2,1)S(1)}, bf16[4,128,128]{2,1,0:T(8,128)(2,1)S(1)}, u32[]{:S(2)}, u32[]{:S(2)}) collective-permute-start(bf16[4,128,128]{2,1,0:T(8,128)(2,1)S(1)} %get-tuple-element.19), channel_id=1, source_target_pairs={{0,8},{1,9},{2,10},{3,11},{4,12},{5,13},{6,14},{7,15},{8,0},{9,1},... | collective-permute-start | bytes 393224 | tf_op jit(solution)/shard_map/ppermute | solution.py:172
  61.5 0.7 collective-permute-start.21
  62.2 1.1 %attend.8 = bf16[4,128,128]{2,1,0:T(8,128)(2,1)S(1)} custom-call(s32[2]{0:T(128)S(1)} %pad_add_fusion.place, s32[16]{0:T(128)S(1)} %copy-done, bf16[576,8,128]{2,1,0:T(8,128)(2,1)S(1)} %get-tuple-element.13.q_packed, bf16[2,256,8,128]{3,2,1,0:T(8,128)(2,1)S(1)} %get-tuple-element.14.kv_packed, bf16[4,128,128]{2,1,0:T(8,128)(2,1)S(1)} %collective-permute-done.18.refs_0_), custom_call_target="tpu_custom_call" | custom-call | flops 1000 | bytes 1000 | tf_op jit(solution)/shard_map/attend/pallas_call | solution.py:211
  63.3 3.9 %collective-permute-start.19 = (bf16[4,128,128]{2,1,0:T(8,128)(2,1)S(1)}, bf16[4,128,128]{2,1,0:T(8,128)(2,1)S(1)}, u32[]{:S(2)}, u32[]{:S(2)}) collective-permute-start(bf16[4,128,128]{2,1,0:T(8,128)(2,1)S(1)} %attend.8), channel_id=1, source_target_pairs={{0,6},{1,7},{2,4},{3,5},{4,2},{5,3},{6,0},{7,1},{8,14},{9,15},{10,... | collective-permute-start | bytes 393224 | tf_op jit(solution)/shard_map/ppermute | solution.py:172
  67.2 1.1 %attend.7 = bf16[4,128,128]{2,1,0:T(8,128)(2,1)S(1)} custom-call(s32[2]{0:T(128)S(1)} %pad_add_fusion.place, s32[16]{0:T(128)S(1)} %copy-done, bf16[576,8,128]{2,1,0:T(8,128)(2,1)S(1)} %get-tuple-element.13.q_packed, bf16[2,256,8,128]{3,2,1,0:T(8,128)(2,1)S(1)} %get-tuple-element.14.kv_packed, bf16[4,128,128]{2,1,0:T(8,128)(2,1)S(1)} %collective-permute-done.15.refs_0_), custom_call_target="tpu_custom_call" | custom-call | flops 1000 | bytes 1000 | tf_op jit(solution)/shard_map/attend/pallas_call | solution.py:211
  68.3 0.2 broadcast_in_dim.28
  68.6 0.8 %copy.9 = bf16[8,4,128,128]{3,1,0,2:T(4,128)(2,1)S(1)} copy(bf16[8,4,128,128]{3,2,1,0:T(8,128)(2,1)S(1)} %bitcast_dynamic-update-slice_fusion) | data formatting | bytes 2097152 | tf_op jit(solution)/shard_map/jit(dynamic_update_index_in_dim)/dynamic_update_slice | solution.py:243
  69.4 0.2 copy_dynamic-update-slice_fusion.6
  69.6 0.2 copy_dynamic-update-slice_fusion.5
  69.8 1.1 %collective-permute-done.19 = bf16[4,128,128]{2,1,0:T(8,128)(2,1)S(1)} collective-permute-done((bf16[4,128,128]{2,1,0:T(8,128)(2,1)S(1)}, bf16[4,128,128]{2,1,0:T(8,128)(2,1)S(1)}, u32[]{:S(2)}, u32[]{:S(2)}) %collective-permute-start.19) | collective-permute-done | bytes 131104 | tf_op jit(solution)/shard_map/ppermute | solution.py:172
  70.9 0.1 copy_dynamic-update-slice_fusion.4
  71.0 0.4 collective-permute-done.20
  71.4 0.1 copy_dynamic-update-slice_fusion.3
  71.6 2.9 %collective-permute-done.21 = bf16[4,128,128]{2,1,0:T(8,128)(2,1)S(1)} collective-permute-done((bf16[4,128,128]{2,1,0:T(8,128)(2,1)S(1)}, bf16[4,128,128]{2,1,0:T(8,128)(2,1)S(1)}, u32[]{:S(2)}, u32[]{:S(2)}) %collective-permute-start.21) | collective-permute-done | bytes 131104 | tf_op jit(solution)/shard_map/ppermute | solution.py:172
  74.4 0.1 copy_dynamic-update-slice_fusion.2
  74.6 0.2 copy_dynamic-update-slice_fusion.1
  74.8 0.2 copy_dynamic-update-slice_fusion
  74.9 1.0 %copy-done.4 = bf16[8,4,128,128]{3,1,0,2:T(4,128)(2,1)} copy-done((bf16[8,4,128,128]{3,1,0,2:T(4,128)(2,1)}, bf16[8,4,128,128]{3,1,0,2:T(4,128)(2,1)S(1)}, u32[]{:S(2)}) %copy-start.4) | copy-done | bytes 1048600
  (28 shorter events, 0.2 us)
Async XLA Ops:
  0.0 1.4 %copy-start.3 = (bf16[128,32,128]{2,1,0:T(8,128)(2,1)S(1)}, bf16[128,32,128]{2,1,0:T(8,128)(2,1)}, u32[]{:S(2)}) copy-start(bf16[128,32,128]{2,1,0:T(8,128)(2,1)} %param.6) | copy-start | bytes 3145732
  1.9 11.2 %collective-permute-start.5 = (bf16[6,128,128]{2,1,0:T(8,128)(2,1)S(1)}, bf16[6,128,128]{2,1,0:T(8,128)(2,1)S(1)}, u32[]{:S(2)}, u32[]{:S(2)}) collective-permute-start(bf16[6,128,128]{2,1,0:T(8,128)(2,1)S(1)} %get-tuple-element.27), channel_id=1, source_target_pairs={{0,12},{1,13},{2,14},{3,15},{4,8},{5,9},{6,10},{7,11},{8,4},{9,5},... | collective-permute-start | bytes 589832 | tf_op jit(solution)/shard_map/ppermute | solution.py:172
  7.0 22.8 %collective-permute-start.4 = (bf16[6,128,128]{2,1,0:T(8,128)(2,1)S(1)}, bf16[6,128,128]{2,1,0:T(8,128)(2,1)S(1)}, u32[]{:S(2)}, u32[]{:S(2)}) collective-permute-start(bf16[6,128,128]{2,1,0:T(8,128)(2,1)S(1)} %get-tuple-element.28), channel_id=1, source_target_pairs={{0,10},{1,11},{2,8},{3,9},{4,14},{5,15},{6,12},{7,13},{8,2},{9,3},... | collective-permute-start | bytes 589832 | tf_op jit(solution)/shard_map/ppermute | solution.py:172
  7.3 36.5 %copy-start.1 = (s32[256]{0:T(256)S(1)}, s32[256]{0:T(256)}, u32[]{:S(2)}) copy-start(s32[256]{0:T(256)} %dest.1) | copy-start | bytes 3076
  7.3 36.5 %copy-start.2 = (s32[256]{0:T(256)S(1)}, s32[256]{0:T(256)}, u32[]{:S(2)}) copy-start(s32[256]{0:T(256)} %slot.1) | copy-start | bytes 3076
  7.4 22.4 %collective-permute-start.6 = (bf16[6,128,128]{2,1,0:T(8,128)(2,1)S(1)}, bf16[6,128,128]{2,1,0:T(8,128)(2,1)S(1)}, u32[]{:S(2)}, u32[]{:S(2)}) collective-permute-start(bf16[6,128,128]{2,1,0:T(8,128)(2,1)S(1)} %get-tuple-element.21), channel_id=1, source_target_pairs={{0,14},{1,15},{2,12},{3,13},{4,10},{5,11},{6,8},{7,9},{8,6},{9,7},... | collective-permute-start | bytes 589832 | tf_op jit(solution)/shard_map/ppermute | solution.py:172
  10.0 19.9 %collective-permute-start = (bf16[6,128,128]{2,1,0:T(8,128)(2,1)S(1)}, bf16[6,128,128]{2,1,0:T(8,128)(2,1)S(1)}, u32[]{:S(2)}, u32[]{:S(2)}) collective-permute-start(bf16[6,128,128]{2,1,0:T(8,128)(2,1)S(1)} %get-tuple-element.23), channel_id=1, source_target_pairs={{0,2},{1,3},{2,0},{3,1},{4,6},{5,7},{6,4},{7,5},{8,10},{9,11},{10,... | collective-permute-start | bytes 589832 | tf_op jit(solution)/shard_map/ppermute | solution.py:172
  11.4 18.9 %collective-permute-start.1 = (bf16[6,128,128]{2,1,0:T(8,128)(2,1)S(1)}, bf16[6,128,128]{2,1,0:T(8,128)(2,1)S(1)}, u32[]{:S(2)}, u32[]{:S(2)}) collective-permute-start(bf16[6,128,128]{2,1,0:T(8,128)(2,1)S(1)} %get-tuple-element.24), channel_id=1, source_target_pairs={{0,4},{1,5},{2,6},{3,7},{4,0},{5,1},{6,2},{7,3},{8,12},{9,13},{10,... | collective-permute-start | bytes 589832 | tf_op jit(solution)/shard_map/ppermute | solution.py:172
  13.0 19.8 %collective-permute-start.2 = (bf16[6,128,128]{2,1,0:T(8,128)(2,1)S(1)}, bf16[6,128,128]{2,1,0:T(8,128)(2,1)S(1)}, u32[]{:S(2)}, u32[]{:S(2)}) collective-permute-start(bf16[6,128,128]{2,1,0:T(8,128)(2,1)S(1)} %get-tuple-element.25), channel_id=1, source_target_pairs={{0,6},{1,7},{2,4},{3,5},{4,2},{5,3},{6,0},{7,1},{8,14},{9,15},{10,... | collective-permute-start | bytes 589832 | tf_op jit(solution)/shard_map/ppermute | solution.py:172
  29.8 11.7 %collective-permute-start.3 = (bf16[6,128,128]{2,1,0:T(8,128)(2,1)S(1)}, bf16[6,128,128]{2,1,0:T(8,128)(2,1)S(1)}, u32[]{:S(2)}, u32[]{:S(2)}) collective-permute-start(bf16[6,128,128]{2,1,0:T(8,128)(2,1)S(1)} %get-tuple-element.26), channel_id=1, source_target_pairs={{0,8},{1,9},{2,10},{3,11},{4,12},{5,13},{6,14},{7,15},{8,0},{9,1},... | collective-permute-start | bytes 589832 | tf_op jit(solution)/shard_map/ppermute | solution.py:172
  29.8 11.7 %collective-permute-start.7 = (bf16[6,128,128]{2,1,0:T(8,128)(2,1)S(1)}, bf16[6,128,128]{2,1,0:T(8,128)(2,1)S(1)}, u32[]{:S(2)}, u32[]{:S(2)}) collective-permute-start(bf16[6,128,128]{2,1,0:T(8,128)(2,1)S(1)} %bitcast.53), channel_id=1, source_target_pairs={{0,1},{1,0},{2,3},{3,2},{4,5},{5,4},{6,7},{7,6},{8,9},{9,8},{10,11... | collective-permute-start | bytes 589832 | tf_op jit(solution)/shard_map/ppermute | solution.py:172
  29.8 12.2 %collective-permute-start.13 = (bf16[6,128,128]{2,1,0:T(8,128)(2,1)S(1)}, bf16[6,128,128]{2,1,0:T(8,128)(2,1)S(1)}, u32[]{:S(2)}, u32[]{:S(2)}) collective-permute-start(bf16[6,128,128]{2,1,0:T(8,128)(2,1)S(1)} %collective-permute-done.5), channel_id=1, source_target_pairs={{0,1},{1,0},{2,3},{3,2},{4,5},{5,4},{6,7},{7,6},{8,9},{9,8},{10,11... | collective-permute-start | bytes 589832 | tf_op jit(solution)/shard_map/ppermute | solution.py:172
  30.3 11.8 %collective-permute-start.12 = (bf16[6,128,128]{2,1,0:T(8,128)(2,1)S(1)}, bf16[6,128,128]{2,1,0:T(8,128)(2,1)S(1)}, u32[]{:S(2)}, u32[]{:S(2)}) collective-permute-start(bf16[6,128,128]{2,1,0:T(8,128)(2,1)S(1)} %collective-permute-done.4), channel_id=1, source_target_pairs={{0,1},{1,0},{2,3},{3,2},{4,5},{5,4},{6,7},{7,6},{8,9},{9,8},{10,11... | collective-permute-start | bytes 589832 | tf_op jit(solution)/shard_map/ppermute | solution.py:172
  32.8 9.8 %collective-permute-start.14 = (bf16[6,128,128]{2,1,0:T(8,128)(2,1)S(1)}, bf16[6,128,128]{2,1,0:T(8,128)(2,1)S(1)}, u32[]{:S(2)}, u32[]{:S(2)}) collective-permute-start(bf16[6,128,128]{2,1,0:T(8,128)(2,1)S(1)} %collective-permute-done.6), channel_id=1, source_target_pairs={{0,1},{1,0},{2,3},{3,2},{4,5},{5,4},{6,7},{7,6},{8,9},{9,8},{10,11... | collective-permute-start | bytes 589832 | tf_op jit(solution)/shard_map/ppermute | solution.py:172
  41.5 1.4 %collective-permute-start.8 = (bf16[6,128,128]{2,1,0:T(8,128)(2,1)S(1)}, bf16[6,128,128]{2,1,0:T(8,128)(2,1)S(1)}, u32[]{:S(2)}, u32[]{:S(2)}) collective-permute-start(bf16[6,128,128]{2,1,0:T(8,128)(2,1)S(1)} %collective-permute-done), channel_id=1, source_target_pairs={{0,1},{1,0},{2,3},{3,2},{4,5},{5,4},{6,7},{7,6},{8,9},{9,8},{10,11... | collective-permute-start | bytes 589832 | tf_op jit(solution)/shard_map/ppermute | solution.py:172
  41.5 1.7 %collective-permute-start.9 = (bf16[6,128,128]{2,1,0:T(8,128)(2,1)S(1)}, bf16[6,128,128]{2,1,0:T(8,128)(2,1)S(1)}, u32[]{:S(2)}, u32[]{:S(2)}) collective-permute-start(bf16[6,128,128]{2,1,0:T(8,128)(2,1)S(1)} %collective-permute-done.1), channel_id=1, source_target_pairs={{0,1},{1,0},{2,3},{3,2},{4,5},{5,4},{6,7},{7,6},{8,9},{9,8},{10,11... | collective-permute-start | bytes 589832 | tf_op jit(solution)/shard_map/ppermute | solution.py:172
  42.0 1.5 %collective-permute-start.10 = (bf16[6,128,128]{2,1,0:T(8,128)(2,1)S(1)}, bf16[6,128,128]{2,1,0:T(8,128)(2,1)S(1)}, u32[]{:S(2)}, u32[]{:S(2)}) collective-permute-start(bf16[6,128,128]{2,1,0:T(8,128)(2,1)S(1)} %collective-permute-done.2), channel_id=1, source_target_pairs={{0,1},{1,0},{2,3},{3,2},{4,5},{5,4},{6,7},{7,6},{8,9},{9,8},{10,11... | collective-permute-start | bytes 589832 | tf_op jit(solution)/shard_map/ppermute | solution.py:172
  42.1 1.7 %collective-permute-start.11 = (bf16[6,128,128]{2,1,0:T(8,128)(2,1)S(1)}, bf16[6,128,128]{2,1,0:T(8,128)(2,1)S(1)}, u32[]{:S(2)}, u32[]{:S(2)}) collective-permute-start(bf16[6,128,128]{2,1,0:T(8,128)(2,1)S(1)} %collective-permute-done.3), channel_id=1, source_target_pairs={{0,1},{1,0},{2,3},{3,2},{4,5},{5,4},{6,7},{7,6},{8,9},{9,8},{10,11... | collective-permute-start | bytes 589832 | tf_op jit(solution)/shard_map/ppermute | solution.py:172
  43.8 2.4 %copy-start = (s32[16]{0:T(128)S(1)}, s32[16]{0:T(128)}, u32[]{:S(2)}) copy-start(s32[16]{0:T(128)} %lengths.9) | copy-start | bytes 196
  49.0 7.2 %collective-permute-start.16 = (bf16[4,128,128]{2,1,0:T(8,128)(2,1)S(1)}, bf16[4,128,128]{2,1,0:T(8,128)(2,1)S(1)}, u32[]{:S(2)}, u32[]{:S(2)}) collective-permute-start(bf16[4,128,128]{2,1,0:T(8,128)(2,1)S(1)} %get-tuple-element.17), channel_id=1, source_target_pairs={{0,2},{1,3},{2,0},{3,1},{4,6},{5,7},{6,4},{7,5},{8,10},{9,11},{10,... | collective-permute-start | bytes 393224 | tf_op jit(solution)/shard_map/ppermute | solution.py:172
  50.1 12.1 %collective-permute-start.18 = (bf16[4,128,128]{2,1,0:T(8,128)(2,1)S(1)}, bf16[4,128,128]{2,1,0:T(8,128)(2,1)S(1)}, u32[]{:S(2)}, u32[]{:S(2)}) collective-permute-start(bf16[4,128,128]{2,1,0:T(8,128)(2,1)S(1)} %get-tuple-element.15.refs_0_), channel_id=1, source_target_pairs={{0,14},{1,15},{2,12},{3,13},{4,10},{5,11},{6,8},{7,9},{8,6},{9,7},... | collective-permute-start | bytes 393224 | tf_op jit(solution)/shard_map/ppermute | solution.py:172
  55.2 12.0 %collective-permute-start.15 = (bf16[4,128,128]{2,1,0:T(8,128)(2,1)S(1)}, bf16[4,128,128]{2,1,0:T(8,128)(2,1)S(1)}, u32[]{:S(2)}, u32[]{:S(2)}) collective-permute-start(bf16[4,128,128]{2,1,0:T(8,128)(2,1)S(1)} %get-tuple-element.16), channel_id=1, source_target_pairs={{0,12},{1,13},{2,14},{3,15},{4,8},{5,9},{6,10},{7,11},{8,4},{9,5},... | collective-permute-start | bytes 393224 | tf_op jit(solution)/shard_map/ppermute | solution.py:172
  56.2 13.4 %collective-permute-start.17 = (bf16[4,128,128]{2,1,0:T(8,128)(2,1)S(1)}, bf16[4,128,128]{2,1,0:T(8,128)(2,1)S(1)}, u32[]{:S(2)}, u32[]{:S(2)}) collective-permute-start(bf16[4,128,128]{2,1,0:T(8,128)(2,1)S(1)} %get-tuple-element.18), channel_id=1, source_target_pairs={{0,4},{1,5},{2,6},{3,7},{4,0},{5,1},{6,2},{7,3},{8,12},{9,13},{10,... | collective-permute-start | bytes 393224 | tf_op jit(solution)/shard_map/ppermute | solution.py:172
  58.2 13.2 %collective-permute-start.20 = (bf16[4,128,128]{2,1,0:T(8,128)(2,1)S(1)}, bf16[4,128,128]{2,1,0:T(8,128)(2,1)S(1)}, u32[]{:S(2)}, u32[]{:S(2)}) collective-permute-start(bf16[4,128,128]{2,1,0:T(8,128)(2,1)S(1)} %get-tuple-element.19), channel_id=1, source_target_pairs={{0,8},{1,9},{2,10},{3,11},{4,12},{5,13},{6,14},{7,15},{8,0},{9,1},... | collective-permute-start | bytes 393224 | tf_op jit(solution)/shard_map/ppermute | solution.py:172
  61.5 13.0 %collective-permute-start.21 = (bf16[4,128,128]{2,1,0:T(8,128)(2,1)S(1)}, bf16[4,128,128]{2,1,0:T(8,128)(2,1)S(1)}, u32[]{:S(2)}, u32[]{:S(2)}) collective-permute-start(bf16[4,128,128]{2,1,0:T(8,128)(2,1)S(1)} %get-tuple-element.20), channel_id=1, source_target_pairs={{0,10},{1,11},{2,8},{3,9},{4,14},{5,15},{6,12},{7,13},{8,2},{9,3},... | collective-permute-start | bytes 393224 | tf_op jit(solution)/shard_map/ppermute | solution.py:172
  63.3 7.6 %collective-permute-start.19 = (bf16[4,128,128]{2,1,0:T(8,128)(2,1)S(1)}, bf16[4,128,128]{2,1,0:T(8,128)(2,1)S(1)}, u32[]{:S(2)}, u32[]{:S(2)}) collective-permute-start(bf16[4,128,128]{2,1,0:T(8,128)(2,1)S(1)} %attend.8), channel_id=1, source_target_pairs={{0,6},{1,7},{2,4},{3,5},{4,2},{5,3},{6,0},{7,1},{8,14},{9,15},{10,... | collective-permute-start | bytes 393224 | tf_op jit(solution)/shard_map/ppermute | solution.py:172
  74.9 1.0 %copy-start.4 = (bf16[8,4,128,128]{3,1,0,2:T(4,128)(2,1)}, bf16[8,4,128,128]{3,1,0,2:T(4,128)(2,1)S(1)}, u32[]{:S(2)}) copy-start(bf16[8,4,128,128]{3,1,0,2:T(4,128)(2,1)S(1)} %copy_dynamic-update-slice_fusion) | copy-start | bytes 3145732

commit v6 on v5

--- a/solution.py
+++ b/solution.py
@@ -15,9 +15,10 @@
 small = pl.CostEstimate(flops=1000, bytes_accessed=1000, transcendentals=0)
 
 
-def pack_kernel(place, dest, slot, *refs, groups, heads, shards):
+def pack_kernel(place, targets, *refs, groups, heads, shards):
     units = shards // 2
     q_packed, kv_packed = refs[-2:]
+    bits = shards.bit_length() - 1
     unit, core = place[0], place[1]
     bases = [
         (lax.bitwise_xor(unit, away) * 2 + lax.bitwise_xor(core, column)) * shards
@@ -26,10 +27,12 @@
 
     def pack_block(b, carry):
         for base, blocks in zip(bases, refs):
-            shard, at = dest[base + b], slot[base + b]
+            kv_at = targets[base + b]
+            shard = lax.shift_right_logical(kv_at, bits)
+            at = lax.bitwise_and(kv_at, shards - 1)
             mine = lax.bitwise_and(shard, 1) == core
             tile = jnp.where(mine, lax.shift_right_logical(shard, 1), units)
-            q_at, kv_at = tile * (heads * shards) + at, shard * shards + at
+            q_at = tile * (heads * shards) + at
             for h in range(heads):
                 q_packed[q_at + h * shards] = blocks[b + h * shards]
             kv_packed[0, kv_at] = blocks[b + heads * shards]
@@ -187,17 +190,17 @@
 
     def pack(groups, arrays, packed, cost):
         blocks = [x.reshape(-1, per, head_size) for x in arrays]
-        count = 3 + len(blocks)
+        count = 2 + len(blocks)
         return pl.pallas_call(
             functools.partial(pack_kernel, groups=groups, heads=heads, shards=shards),
             out_shape=packed_shapes,
-            in_specs=[smem] * 3 + [vmem] * (len(blocks) + len(packed)),
+            in_specs=[smem] * 2 + [vmem] * (len(blocks) + len(packed)),
             out_specs=(vmem, vmem),
             input_output_aliases={count: 0, count + 1: 1} if packed else {},
             compiler_params=pltpu.CompilerParams(vmem_limit_bytes=24 << 20),
             cost_estimate=cost,
             name="pack_blocks",
-        )(place, plan_dest, plan_slot, *blocks, *packed)
+        )(place, plan_dest * shards + plan_slot, *blocks, *packed)
 
     everyone = list(range(units))
     groups = [(column, away) for column in range(2) for away in everyone]
@@ -230,7 +233,7 @@
             raw[away] = out
             tiles[away] = hop(out, 2 * away) if away else out
 
-    far_tiles = list(reversed(range(half, units)))
+    far_tiles = [half + 1, half] + list(reversed(range(half + 2, units)))
     attend((far_tiles[0], 1), [])
     attend((far_tiles[1], 2), [raw[far_tiles[0]]])
     for i in range(2, half, 2):

time: 76.7 us -> 75.5 us (0.984); the launches traced: 75.9 us -> 75.8 us
  starting transfers between devices: 37.9 us -> 36.2 us
  waiting for transfers between devices: 20.4 us -> 21.7 us
    ppermute x22, starting transfers between devices: 37.9 us -> 36.2 us  [hop(): return lax.ppermute(x, 'seq', [(i, i ^ distance) for i in range(shards)])]
    ppermute x22, waiting for transfers between devices: 20.4 us -> 21.7 us  [hop(): return lax.ppermute(x, 'seq', [(i, i ^ distance) for i in range(shards)])]
  transfers between devices with their start and end apart: 22 -> 22, of which waited for: 10 -> 8; matrix products, arithmetic and copies ran while one was open for 2% -> 3% of each run, Pallas kernels for 9% -> 10%
where the time goes in v6:
time: 75.5 us; the launch traced here: 75.8 us
  starting transfers between devices  36.2 us (48%)
  waiting for transfers between devices  21.7 us (29%)
  Pallas kernels  12.5 us (17%)
  local copies, waits for them, and re-layouts  3.71 us (5%)
  other arithmetic  1.39 us (2%)
    ppermute x22, starting transfers between devices, hop(): return lax.ppermute(x, 'seq', [(i, i ^ distance) for i in range(shards)])  36.2 us
    ppermute x22, waiting for transfers between devices, hop(): return lax.ppermute(x, 'seq', [(i, i ^ distance) for i in range(shards)])  21.7 us
    pallas_call x5, Pallas kernels, attend(): pl.pallas_call(functools.partial(attend_kernel, aways=aways, heads=heads,...  10.2 us
    pallas_call x1, Pallas kernels, pack(): pl.pallas_call(functools.partial(pack_kernel, groups=groups, heads=heads,...  2.25 us
    dynamic_update_slice x9, local copies, waits for them, and re-layouts, per_device(): lax.dynamic_update_index_in_dim(gathered, tiles[away], unit ^ away, 0)  1.89 us
  transfers between devices with their start and end apart: 22, of which 8 were waited for; matrix products, arithmetic and copies ran while one was open for 3% of the time, Pallas kernels for 10%

profile of v6, /device:TPU:0, one launch (start us, length us, event | category | flops | bytes accessed | tf_op | source)
XLA Modules:
  0.0 75.8 jit_solution(1465436809796348489)
XLA Ops:
  0.0 1.2 %maximum_bitcast_fusion = bf16[8,2,128,128]{3,0,2,1:T(8,128)(2,1)S(1)} fusion(bf16[1,128,8,128]{3,2,1,0:T(8,128)(2,1)} %bitcast.76, bf16[1,128,8,128]{3,2,1,0:T(8,128)(2,1)} %bitcast.77), kind=kLoop, calls=%fused_computation.17 | loop fusion | flops 262144 | bytes 1048576 | tf_op jit(solution)/shard_map/transpose | solution.py:170
  1.2 0.1 copy.8
  1.3 0.1 copy-done.1
  1.4 0.4 copy.25
  1.9 5.1 %collective-permute-start.5 = (bf16[6,128,128]{2,1,0:T(8,128)(2,1)S(1)}, bf16[6,128,128]{2,1,0:T(8,128)(2,1)S(1)}, u32[]{:S(2)}, u32[]{:S(2)}) collective-permute-start(bf16[6,128,128]{2,1,0:T(8,128)(2,1)S(1)} %get-tuple-element.27), channel_id=1, source_target_pairs={{0,12},{1,13},{2,14},{3,15},{4,8},{5,9},{6,10},{7,11},{8,4},{9,5},... | collective-permute-start | bytes 589832 | tf_op jit(solution)/shard_map/ppermute | solution.py:175
  7.0 0.4 collective-permute-start.4
  7.3 0.1 fusion.14
  7.4 2.5 %collective-permute-start.6 = (bf16[6,128,128]{2,1,0:T(8,128)(2,1)S(1)}, bf16[6,128,128]{2,1,0:T(8,128)(2,1)S(1)}, u32[]{:S(2)}, u32[]{:S(2)}) collective-permute-start(bf16[6,128,128]{2,1,0:T(8,128)(2,1)S(1)} %get-tuple-element.21), channel_id=1, source_target_pairs={{0,14},{1,15},{2,12},{3,13},{4,10},{5,11},{6,8},{7,9},{8,6},{9,7},... | collective-permute-start | bytes 589832 | tf_op jit(solution)/shard_map/ppermute | solution.py:175
  10.0 1.5 %collective-permute-start = (bf16[6,128,128]{2,1,0:T(8,128)(2,1)S(1)}, bf16[6,128,128]{2,1,0:T(8,128)(2,1)S(1)}, u32[]{:S(2)}, u32[]{:S(2)}) collective-permute-start(bf16[6,128,128]{2,1,0:T(8,128)(2,1)S(1)} %get-tuple-element.23), channel_id=1, source_target_pairs={{0,2},{1,3},{2,0},{3,1},{4,6},{5,7},{6,4},{7,5},{8,10},{9,11},{10,... | collective-permute-start | bytes 589832 | tf_op jit(solution)/shard_map/ppermute | solution.py:175
  11.4 1.6 %collective-permute-start.1 = (bf16[6,128,128]{2,1,0:T(8,128)(2,1)S(1)}, bf16[6,128,128]{2,1,0:T(8,128)(2,1)S(1)}, u32[]{:S(2)}, u32[]{:S(2)}) collective-permute-start(bf16[6,128,128]{2,1,0:T(8,128)(2,1)S(1)} %get-tuple-element.24), channel_id=1, source_target_pairs={{0,4},{1,5},{2,6},{3,7},{4,0},{5,1},{6,2},{7,3},{8,12},{9,13},{10,... | collective-permute-start | bytes 589832 | tf_op jit(solution)/shard_map/ppermute | solution.py:175
  13.0 13.1 %collective-permute-start.2 = (bf16[6,128,128]{2,1,0:T(8,128)(2,1)S(1)}, bf16[6,128,128]{2,1,0:T(8,128)(2,1)S(1)}, u32[]{:S(2)}, u32[]{:S(2)}) collective-permute-start(bf16[6,128,128]{2,1,0:T(8,128)(2,1)S(1)} %get-tuple-element.25), channel_id=1, source_target_pairs={{0,6},{1,7},{2,4},{3,5},{4,2},{5,3},{6,0},{7,1},{8,14},{9,15},{10,... | collective-permute-start | bytes 589832 | tf_op jit(solution)/shard_map/ppermute | solution.py:175
  26.1 3.7 %collective-permute-done.4 = bf16[6,128,128]{2,1,0:T(8,128)(2,1)S(1)} collective-permute-done((bf16[6,128,128]{2,1,0:T(8,128)(2,1)S(1)}, bf16[6,128,128]{2,1,0:T(8,128)(2,1)S(1)}, u32[]{:S(2)}, u32[]{:S(2)}) %collective-permute-start.4) | collective-permute-done | bytes 196640 | tf_op jit(solution)/shard_map/ppermute | solution.py:175
  29.8 0.5 collective-permute-start.13
  30.3 0.1 collective-permute-start.12
  30.4 0.1 pad_add_fusion.place
  30.5 2.3 %collective-permute-done.2 = bf16[6,128,128]{2,1,0:T(8,128)(2,1)S(1)} collective-permute-done((bf16[6,128,128]{2,1,0:T(8,128)(2,1)S(1)}, bf16[6,128,128]{2,1,0:T(8,128)(2,1)S(1)}, u32[]{:S(2)}, u32[]{:S(2)}) %collective-permute-start.2) | collective-permute-done | bytes 196640 | tf_op jit(solution)/shard_map/ppermute | solution.py:175
  32.8 8.7 %collective-permute-done.3 = bf16[6,128,128]{2,1,0:T(8,128)(2,1)S(1)} collective-permute-done((bf16[6,128,128]{2,1,0:T(8,128)(2,1)S(1)}, bf16[6,128,128]{2,1,0:T(8,128)(2,1)S(1)}, u32[]{:S(2)}, u32[]{:S(2)}) %collective-permute-start.3) | collective-permute-done | bytes 196640 | tf_op jit(solution)/shard_map/ppermute | solution.py:175
  41.5 0.5 collective-permute-start.9
  42.0 0.1 collective-permute-start.10
  42.1 0.4 collective-permute-start.11
  42.6 0.4 collective-permute-done.8
  43.0 0.3 collective-permute-done.9
  43.2 0.3 collective-permute-done.10
  43.5 0.3 collective-permute-done.11
  43.8 2.2 %pack_blocks.1 = (bf16[576,8,128]{2,1,0:T(8,128)(2,1)S(1)}, bf16[2,256,8,128]{3,2,1,0:T(8,128)(2,1)S(1)}) custom-call(s32[2]{0:T(128)S(1)} %pad_add_fusion.place, s32[256]{0:T(256)S(1)} %multiply_add_fusion.targets, bf16[96,8,128]{2,1,0:T(8,128)(2,1)S(1)} %bitcast.54, bf16[96,8,128]{2,1,0:T(8,128)(2,1)S(1)} %bitcast.61, bf16[96,8,128]{2,1,0:T(8,128)(2,1)S(1)} %bitcast.62, ...), custom_call_target="tpu_custom_call" | custom-call | flops 1000 | bytes 1000 | tf_op jit(solution)/shard_map/pack_blocks/pallas_call | solution.py:194
  46.1 2.3 %attend.5 = (bf16[4,128,128]{2,1,0:T(8,128)(2,1)S(1)}, bf16[4,128,128]{2,1,0:T(8,128)(2,1)S(1)}) custom-call(s32[2]{0:T(128)S(1)} %pad_add_fusion.place, s32[16]{0:T(128)S(1)} %copy-done, bf16[576,8,128]{2,1,0:T(8,128)(2,1)S(1)} %get-tuple-element.13.q_packed, bf16[2,256,8,128]{3,2,1,0:T(8,128)(2,1)S(1)} %get-tuple-element.14.kv_packed), custom_call_target="tpu_custom_call" | custom-call | flops 1000 | bytes 1000 | tf_op jit(solution)/shard_map/attend/pallas_call | solution.py:214
  48.4 0.5 collective-permute-start.16
  48.9 0.7 collective-permute-start.18
  49.6 1.7 %attend.6 = (bf16[4,128,128]{2,1,0:T(8,128)(2,1)S(1)}, bf16[4,128,128]{2,1,0:T(8,128)(2,1)S(1)}) custom-call(s32[2]{0:T(128)S(1)} %pad_add_fusion.place, s32[16]{0:T(128)S(1)} %copy-done, bf16[576,8,128]{2,1,0:T(8,128)(2,1)S(1)} %get-tuple-element.13.q_packed, bf16[2,256,8,128]{3,2,1,0:T(8,128)(2,1)S(1)} %get-tuple-element.14.kv_packed, ...), custom_call_target="tpu_custom_call" | custom-call | flops 1000 | bytes 1000 | tf_op jit(solution)/shard_map/attend/pallas_call | solution.py:214
  51.3 4.4 %collective-permute-start.15 = (bf16[4,128,128]{2,1,0:T(8,128)(2,1)S(1)}, bf16[4,128,128]{2,1,0:T(8,128)(2,1)S(1)}, u32[]{:S(2)}, u32[]{:S(2)}) collective-permute-start(bf16[4,128,128]{2,1,0:T(8,128)(2,1)S(1)} %get-tuple-element.16), channel_id=1, source_target_pairs={{0,8},{1,9},{2,10},{3,11},{4,12},{5,13},{6,14},{7,15},{8,0},{9,1},... | collective-permute-start | bytes 393224 | tf_op jit(solution)/shard_map/ppermute | solution.py:175
  55.8 0.0 collective-permute-start.17
  55.8 3.9 %attend.9 = (bf16[4,128,128]{2,1,0:T(8,128)(2,1)S(1)}, bf16[4,128,128]{2,1,0:T(8,128)(2,1)S(1)}) custom-call(s32[2]{0:T(128)S(1)} %pad_add_fusion.place, s32[16]{0:T(128)S(1)} %copy-done, bf16[576,8,128]{2,1,0:T(8,128)(2,1)S(1)} %get-tuple-element.13.q_packed, bf16[2,256,8,128]{3,2,1,0:T(8,128)(2,1)S(1)} %get-tuple-element.14.kv_packed, ...), custom_call_target="tpu_custom_call" | custom-call | flops 1000 | bytes 1000 | tf_op jit(solution)/shard_map/attend/pallas_call | solution.py:214
  59.7 0.5 collective-permute-start.20
  60.2 4.2 %collective-permute-start.21 = (bf16[4,128,128]{2,1,0:T(8,128)(2,1)S(1)}, bf16[4,128,128]{2,1,0:T(8,128)(2,1)S(1)}, u32[]{:S(2)}, u32[]{:S(2)}) collective-permute-start(bf16[4,128,128]{2,1,0:T(8,128)(2,1)S(1)} %get-tuple-element.20), channel_id=1, source_target_pairs={{0,14},{1,15},{2,12},{3,13},{4,10},{5,11},{6,8},{7,9},{8,6},{9,7},... | collective-permute-start | bytes 393224 | tf_op jit(solution)/shard_map/ppermute | solution.py:175
  64.5 1.1 %attend.8 = bf16[4,128,128]{2,1,0:T(8,128)(2,1)S(1)} custom-call(s32[2]{0:T(128)S(1)} %pad_add_fusion.place, s32[16]{0:T(128)S(1)} %copy-done, bf16[576,8,128]{2,1,0:T(8,128)(2,1)S(1)} %get-tuple-element.13.q_packed, bf16[2,256,8,128]{3,2,1,0:T(8,128)(2,1)S(1)} %get-tuple-element.14.kv_packed, bf16[4,128,128]{2,1,0:T(8,128)(2,1)S(1)} %collective-permute-done.18.refs_0_), custom_call_target="tpu_custom_call" | custom-call | flops 1000 | bytes 1000 | tf_op jit(solution)/shard_map/attend/pallas_call | solution.py:214
  65.6 0.1 collective-permute-start.19
  65.7 1.1 %attend.7 = bf16[4,128,128]{2,1,0:T(8,128)(2,1)S(1)} custom-call(s32[2]{0:T(128)S(1)} %pad_add_fusion.place, s32[16]{0:T(128)S(1)} %copy-done, bf16[576,8,128]{2,1,0:T(8,128)(2,1)S(1)} %get-tuple-element.13.q_packed, bf16[2,256,8,128]{3,2,1,0:T(8,128)(2,1)S(1)} %get-tuple-element.14.kv_packed, bf16[4,128,128]{2,1,0:T(8,128)(2,1)S(1)} %collective-permute-done.15.refs_0_), custom_call_target="tpu_custom_call" | custom-call | flops 1000 | bytes 1000 | tf_op jit(solution)/shard_map/attend/pallas_call | solution.py:214
  66.8 0.2 broadcast_in_dim.28
  67.1 0.8 %copy.9 = bf16[8,4,128,128]{3,1,0,2:T(4,128)(2,1)S(1)} copy(bf16[8,4,128,128]{3,2,1,0:T(8,128)(2,1)S(1)} %bitcast_dynamic-update-slice_fusion) | data formatting | bytes 2097152 | tf_op jit(solution)/shard_map/jit(dynamic_update_index_in_dim)/dynamic_update_slice | solution.py:246
  67.9 0.2 copy_dynamic-update-slice_fusion.6
  68.1 0.2 copy_dynamic-update-slice_fusion.5
  68.3 5.7 %collective-permute-done.19 = bf16[4,128,128]{2,1,0:T(8,128)(2,1)S(1)} collective-permute-done((bf16[4,128,128]{2,1,0:T(8,128)(2,1)S(1)}, bf16[4,128,128]{2,1,0:T(8,128)(2,1)S(1)}, u32[]{:S(2)}, u32[]{:S(2)}) %collective-permute-start.19) | collective-permute-done | bytes 131104 | tf_op jit(solution)/shard_map/ppermute | solution.py:175
  74.0 0.1 copy_dynamic-update-slice_fusion.4
  74.1 0.2 copy_dynamic-update-slice_fusion.3
  74.3 0.2 copy_dynamic-update-slice_fusion.2
  74.5 0.2 copy_dynamic-update-slice_fusion.1
  74.6 0.2 copy_dynamic-update-slice_fusion
  74.8 1.0 %copy-done.2 = bf16[8,4,128,128]{3,1,0,2:T(4,128)(2,1)} copy-done((bf16[8,4,128,128]{3,1,0,2:T(4,128)(2,1)}, bf16[8,4,128,128]{3,1,0,2:T(4,128)(2,1)S(1)}, u32[]{:S(2)}) %copy-start.2) | copy-done | bytes 1048600
  (29 shorter events, 0.1 us)
Async XLA Ops:
  0.0 1.4 %copy-start.1 = (bf16[128,32,128]{2,1,0:T(8,128)(2,1)S(1)}, bf16[128,32,128]{2,1,0:T(8,128)(2,1)}, u32[]{:S(2)}) copy-start(bf16[128,32,128]{2,1,0:T(8,128)(2,1)} %param.6) | copy-start | bytes 3145732
  1.9 11.2 %collective-permute-start.5 = (bf16[6,128,128]{2,1,0:T(8,128)(2,1)S(1)}, bf16[6,128,128]{2,1,0:T(8,128)(2,1)S(1)}, u32[]{:S(2)}, u32[]{:S(2)}) collective-permute-start(bf16[6,128,128]{2,1,0:T(8,128)(2,1)S(1)} %get-tuple-element.27), channel_id=1, source_target_pairs={{0,12},{1,13},{2,14},{3,15},{4,8},{5,9},{6,10},{7,11},{8,4},{9,5},... | collective-permute-start | bytes 589832 | tf_op jit(solution)/shard_map/ppermute | solution.py:175
  7.0 22.8 %collective-permute-start.4 = (bf16[6,128,128]{2,1,0:T(8,128)(2,1)S(1)}, bf16[6,128,128]{2,1,0:T(8,128)(2,1)S(1)}, u32[]{:S(2)}, u32[]{:S(2)}) collective-permute-start(bf16[6,128,128]{2,1,0:T(8,128)(2,1)S(1)} %get-tuple-element.28), channel_id=1, source_target_pairs={{0,10},{1,11},{2,8},{3,9},{4,14},{5,15},{6,12},{7,13},{8,2},{9,3},... | collective-permute-start | bytes 589832 | tf_op jit(solution)/shard_map/ppermute | solution.py:175
  7.3 35.2 %copy-start.3 = (s32[256]{0:T(256)S(1)}, s32[256]{0:T(256)}, u32[]{:S(2)}) copy-start(s32[256]{0:T(256)} %param.11) | copy-start | bytes 3076
  7.3 35.2 %copy-start.4 = (s32[256]{0:T(256)S(1)}, s32[256]{0:T(256)}, u32[]{:S(2)}) copy-start(s32[256]{0:T(256)} %param.10) | copy-start | bytes 3076
  7.4 22.4 %collective-permute-start.6 = (bf16[6,128,128]{2,1,0:T(8,128)(2,1)S(1)}, bf16[6,128,128]{2,1,0:T(8,128)(2,1)S(1)}, u32[]{:S(2)}, u32[]{:S(2)}) collective-permute-start(bf16[6,128,128]{2,1,0:T(8,128)(2,1)S(1)} %get-tuple-element.21), channel_id=1, source_target_pairs={{0,14},{1,15},{2,12},{3,13},{4,10},{5,11},{6,8},{7,9},{8,6},{9,7},... | collective-permute-start | bytes 589832 | tf_op jit(solution)/shard_map/ppermute | solution.py:175
  10.0 19.9 %collective-permute-start = (bf16[6,128,128]{2,1,0:T(8,128)(2,1)S(1)}, bf16[6,128,128]{2,1,0:T(8,128)(2,1)S(1)}, u32[]{:S(2)}, u32[]{:S(2)}) collective-permute-start(bf16[6,128,128]{2,1,0:T(8,128)(2,1)S(1)} %get-tuple-element.23), channel_id=1, source_target_pairs={{0,2},{1,3},{2,0},{3,1},{4,6},{5,7},{6,4},{7,5},{8,10},{9,11},{10,... | collective-permute-start | bytes 589832 | tf_op jit(solution)/shard_map/ppermute | solution.py:175
  11.4 18.9 %collective-permute-start.1 = (bf16[6,128,128]{2,1,0:T(8,128)(2,1)S(1)}, bf16[6,128,128]{2,1,0:T(8,128)(2,1)S(1)}, u32[]{:S(2)}, u32[]{:S(2)}) collective-permute-start(bf16[6,128,128]{2,1,0:T(8,128)(2,1)S(1)} %get-tuple-element.24), channel_id=1, source_target_pairs={{0,4},{1,5},{2,6},{3,7},{4,0},{5,1},{6,2},{7,3},{8,12},{9,13},{10,... | collective-permute-start | bytes 589832 | tf_op jit(solution)/shard_map/ppermute | solution.py:175
  13.0 19.8 %collective-permute-start.2 = (bf16[6,128,128]{2,1,0:T(8,128)(2,1)S(1)}, bf16[6,128,128]{2,1,0:T(8,128)(2,1)S(1)}, u32[]{:S(2)}, u32[]{:S(2)}) collective-permute-start(bf16[6,128,128]{2,1,0:T(8,128)(2,1)S(1)} %get-tuple-element.25), channel_id=1, source_target_pairs={{0,6},{1,7},{2,4},{3,5},{4,2},{5,3},{6,0},{7,1},{8,14},{9,15},{10,... | collective-permute-start | bytes 589832 | tf_op jit(solution)/shard_map/ppermute | solution.py:175
  29.8 11.7 %collective-permute-start.3 = (bf16[6,128,128]{2,1,0:T(8,128)(2,1)S(1)}, bf16[6,128,128]{2,1,0:T(8,128)(2,1)S(1)}, u32[]{:S(2)}, u32[]{:S(2)}) collective-permute-start(bf16[6,128,128]{2,1,0:T(8,128)(2,1)S(1)} %get-tuple-element.26), channel_id=1, source_target_pairs={{0,8},{1,9},{2,10},{3,11},{4,12},{5,13},{6,14},{7,15},{8,0},{9,1},... | collective-permute-start | bytes 589832 | tf_op jit(solution)/shard_map/ppermute | solution.py:175
  29.8 11.7 %collective-permute-start.7 = (bf16[6,128,128]{2,1,0:T(8,128)(2,1)S(1)}, bf16[6,128,128]{2,1,0:T(8,128)(2,1)S(1)}, u32[]{:S(2)}, u32[]{:S(2)}) collective-permute-start(bf16[6,128,128]{2,1,0:T(8,128)(2,1)S(1)} %bitcast.53), channel_id=1, source_target_pairs={{0,1},{1,0},{2,3},{3,2},{4,5},{5,4},{6,7},{7,6},{8,9},{9,8},{10,11... | collective-permute-start | bytes 589832 | tf_op jit(solution)/shard_map/ppermute | solution.py:175
  29.8 12.2 %collective-permute-start.13 = (bf16[6,128,128]{2,1,0:T(8,128)(2,1)S(1)}, bf16[6,128,128]{2,1,0:T(8,128)(2,1)S(1)}, u32[]{:S(2)}, u32[]{:S(2)}) collective-permute-start(bf16[6,128,128]{2,1,0:T(8,128)(2,1)S(1)} %collective-permute-done.5), channel_id=1, source_target_pairs={{0,1},{1,0},{2,3},{3,2},{4,5},{5,4},{6,7},{7,6},{8,9},{9,8},{10,11... | collective-permute-start | bytes 589832 | tf_op jit(solution)/shard_map/ppermute | solution.py:175
  30.3 11.8 %collective-permute-start.12 = (bf16[6,128,128]{2,1,0:T(8,128)(2,1)S(1)}, bf16[6,128,128]{2,1,0:T(8,128)(2,1)S(1)}, u32[]{:S(2)}, u32[]{:S(2)}) collective-permute-start(bf16[6,128,128]{2,1,0:T(8,128)(2,1)S(1)} %collective-permute-done.4), channel_id=1, source_target_pairs={{0,1},{1,0},{2,3},{3,2},{4,5},{5,4},{6,7},{7,6},{8,9},{9,8},{10,11... | collective-permute-start | bytes 589832 | tf_op jit(solution)/shard_map/ppermute | solution.py:175
  32.8 9.7 %collective-permute-start.14 = (bf16[6,128,128]{2,1,0:T(8,128)(2,1)S(1)}, bf16[6,128,128]{2,1,0:T(8,128)(2,1)S(1)}, u32[]{:S(2)}, u32[]{:S(2)}) collective-permute-start(bf16[6,128,128]{2,1,0:T(8,128)(2,1)S(1)} %collective-permute-done.6), channel_id=1, source_target_pairs={{0,1},{1,0},{2,3},{3,2},{4,5},{5,4},{6,7},{7,6},{8,9},{9,8},{10,11... | collective-permute-start | bytes 589832 | tf_op jit(solution)/shard_map/ppermute | solution.py:175
  41.5 1.4 %collective-permute-start.8 = (bf16[6,128,128]{2,1,0:T(8,128)(2,1)S(1)}, bf16[6,128,128]{2,1,0:T(8,128)(2,1)S(1)}, u32[]{:S(2)}, u32[]{:S(2)}) collective-permute-start(bf16[6,128,128]{2,1,0:T(8,128)(2,1)S(1)} %collective-permute-done), channel_id=1, source_target_pairs={{0,1},{1,0},{2,3},{3,2},{4,5},{5,4},{6,7},{7,6},{8,9},{9,8},{10,11... | collective-permute-start | bytes 589832 | tf_op jit(solution)/shard_map/ppermute | solution.py:175
  41.5 1.7 %collective-permute-start.9 = (bf16[6,128,128]{2,1,0:T(8,128)(2,1)S(1)}, bf16[6,128,128]{2,1,0:T(8,128)(2,1)S(1)}, u32[]{:S(2)}, u32[]{:S(2)}) collective-permute-start(bf16[6,128,128]{2,1,0:T(8,128)(2,1)S(1)} %collective-permute-done.1), channel_id=1, source_target_pairs={{0,1},{1,0},{2,3},{3,2},{4,5},{5,4},{6,7},{7,6},{8,9},{9,8},{10,11... | collective-permute-start | bytes 589832 | tf_op jit(solution)/shard_map/ppermute | solution.py:175
  42.0 1.5 %collective-permute-start.10 = (bf16[6,128,128]{2,1,0:T(8,128)(2,1)S(1)}, bf16[6,128,128]{2,1,0:T(8,128)(2,1)S(1)}, u32[]{:S(2)}, u32[]{:S(2)}) collective-permute-start(bf16[6,128,128]{2,1,0:T(8,128)(2,1)S(1)} %collective-permute-done.2), channel_id=1, source_target_pairs={{0,1},{1,0},{2,3},{3,2},{4,5},{5,4},{6,7},{7,6},{8,9},{9,8},{10,11... | collective-permute-start | bytes 589832 | tf_op jit(solution)/shard_map/ppermute | solution.py:175
  42.1 1.7 %collective-permute-start.11 = (bf16[6,128,128]{2,1,0:T(8,128)(2,1)S(1)}, bf16[6,128,128]{2,1,0:T(8,128)(2,1)S(1)}, u32[]{:S(2)}, u32[]{:S(2)}) collective-permute-start(bf16[6,128,128]{2,1,0:T(8,128)(2,1)S(1)} %collective-permute-done.3), channel_id=1, source_target_pairs={{0,1},{1,0},{2,3},{3,2},{4,5},{5,4},{6,7},{7,6},{8,9},{9,8},{10,11... | collective-permute-start | bytes 589832 | tf_op jit(solution)/shard_map/ppermute | solution.py:175
  43.8 2.3 %copy-start = (s32[16]{0:T(128)S(1)}, s32[16]{0:T(128)}, u32[]{:S(2)}) copy-start(s32[16]{0:T(128)} %lengths.9) | copy-start | bytes 196
  48.4 7.4 %collective-permute-start.16 = (bf16[4,128,128]{2,1,0:T(8,128)(2,1)S(1)}, bf16[4,128,128]{2,1,0:T(8,128)(2,1)S(1)}, u32[]{:S(2)}, u32[]{:S(2)}) collective-permute-start(bf16[4,128,128]{2,1,0:T(8,128)(2,1)S(1)} %get-tuple-element.17), channel_id=1, source_target_pairs={{0,2},{1,3},{2,0},{3,1},{4,6},{5,7},{6,4},{7,5},{8,10},{9,11},{10,... | collective-permute-start | bytes 393224 | tf_op jit(solution)/shard_map/ppermute | solution.py:175
  48.9 15.6 %collective-permute-start.18 = (bf16[4,128,128]{2,1,0:T(8,128)(2,1)S(1)}, bf16[4,128,128]{2,1,0:T(8,128)(2,1)S(1)}, u32[]{:S(2)}, u32[]{:S(2)}) collective-permute-start(bf16[4,128,128]{2,1,0:T(8,128)(2,1)S(1)} %get-tuple-element.15.refs_0_), channel_id=1, source_target_pairs={{0,10},{1,11},{2,8},{3,9},{4,14},{5,15},{6,12},{7,13},{8,2},{9,3},... | collective-permute-start | bytes 393224 | tf_op jit(solution)/shard_map/ppermute | solution.py:175
  51.3 14.4 %collective-permute-start.15 = (bf16[4,128,128]{2,1,0:T(8,128)(2,1)S(1)}, bf16[4,128,128]{2,1,0:T(8,128)(2,1)S(1)}, u32[]{:S(2)}, u32[]{:S(2)}) collective-permute-start(bf16[4,128,128]{2,1,0:T(8,128)(2,1)S(1)} %get-tuple-element.16), channel_id=1, source_target_pairs={{0,8},{1,9},{2,10},{3,11},{4,12},{5,13},{6,14},{7,15},{8,0},{9,1},... | collective-permute-start | bytes 393224 | tf_op jit(solution)/shard_map/ppermute | solution.py:175
  55.8 12.3 %collective-permute-start.17 = (bf16[4,128,128]{2,1,0:T(8,128)(2,1)S(1)}, bf16[4,128,128]{2,1,0:T(8,128)(2,1)S(1)}, u32[]{:S(2)}, u32[]{:S(2)}) collective-permute-start(bf16[4,128,128]{2,1,0:T(8,128)(2,1)S(1)} %get-tuple-element.18), channel_id=1, source_target_pairs={{0,4},{1,5},{2,6},{3,7},{4,0},{5,1},{6,2},{7,3},{8,12},{9,13},{10,... | collective-permute-start | bytes 393224 | tf_op jit(solution)/shard_map/ppermute | solution.py:175
  59.7 14.8 %collective-permute-start.20 = (bf16[4,128,128]{2,1,0:T(8,128)(2,1)S(1)}, bf16[4,128,128]{2,1,0:T(8,128)(2,1)S(1)}, u32[]{:S(2)}, u32[]{:S(2)}) collective-permute-start(bf16[4,128,128]{2,1,0:T(8,128)(2,1)S(1)} %get-tuple-element.19), channel_id=1, source_target_pairs={{0,12},{1,13},{2,14},{3,15},{4,8},{5,9},{6,10},{7,11},{8,4},{9,5},... | collective-permute-start | bytes 393224 | tf_op jit(solution)/shard_map/ppermute | solution.py:175
  60.2 14.4 %collective-permute-start.21 = (bf16[4,128,128]{2,1,0:T(8,128)(2,1)S(1)}, bf16[4,128,128]{2,1,0:T(8,128)(2,1)S(1)}, u32[]{:S(2)}, u32[]{:S(2)}) collective-permute-start(bf16[4,128,128]{2,1,0:T(8,128)(2,1)S(1)} %get-tuple-element.20), channel_id=1, source_target_pairs={{0,14},{1,15},{2,12},{3,13},{4,10},{5,11},{6,8},{7,9},{8,6},{9,7},... | collective-permute-start | bytes 393224 | tf_op jit(solution)/shard_map/ppermute | solution.py:175
  65.6 8.4 %collective-permute-start.19 = (bf16[4,128,128]{2,1,0:T(8,128)(2,1)S(1)}, bf16[4,128,128]{2,1,0:T(8,128)(2,1)S(1)}, u32[]{:S(2)}, u32[]{:S(2)}) collective-permute-start(bf16[4,128,128]{2,1,0:T(8,128)(2,1)S(1)} %attend.8), channel_id=1, source_target_pairs={{0,6},{1,7},{2,4},{3,5},{4,2},{5,3},{6,0},{7,1},{8,14},{9,15},{10,... | collective-permute-start | bytes 393224 | tf_op jit(solution)/shard_map/ppermute | solution.py:175
  74.8 1.0 %copy-start.2 = (bf16[8,4,128,128]{3,1,0,2:T(4,128)(2,1)}, bf16[8,4,128,128]{3,1,0,2:T(4,128)(2,1)S(1)}, u32[]{:S(2)}) copy-start(bf16[8,4,128,128]{3,1,0,2:T(4,128)(2,1)S(1)} %copy_dynamic-update-slice_fusion) | copy-start | bytes 3145732

commit v7 on v6

--- a/solution.py
+++ b/solution.py
@@ -39,7 +39,7 @@
             kv_packed[1, kv_at] = blocks[b + (heads + 1) * shards]
         return carry
 
-    lax.fori_loop(0, shards, pack_block, 0, unroll=2)
+    lax.fori_loop(0, shards, pack_block, 0, unroll=8)
 
 
 def fold(x, op):

time: 75.5 us -> 75.4 us (level)
  transfers between devices with their start and end apart: 22 -> 22, of which waited for: 8 -> 8; matrix products, arithmetic and copies ran while one was open for 3% -> 3% of each run, Pallas kernels for 10% -> 11%
where the time goes in v7:
time: 75.4 us; the launch traced here: 75.6 us
  starting transfers between devices  36.2 us (48%)
  waiting for transfers between devices  21.8 us (29%)
  Pallas kernels  12.2 us (16%)
  local copies, waits for them, and re-layouts  3.71 us (5%)
  other arithmetic  1.39 us (2%)
    ppermute x22, starting transfers between devices, hop(): return lax.ppermute(x, 'seq', [(i, i ^ distance) for i in range(shards)])  36.2 us
    ppermute x22, waiting for transfers between devices, hop(): return lax.ppermute(x, 'seq', [(i, i ^ distance) for i in range(shards)])  21.8 us
    pallas_call x5, Pallas kernels, attend(): pl.pallas_call(functools.partial(attend_kernel, aways=aways, heads=heads,...  10.1 us
    pallas_call x1, Pallas kernels, pack(): pl.pallas_call(functools.partial(pack_kernel, groups=groups, heads=heads,...  2.11 us
    dynamic_update_slice x9, local copies, waits for them, and re-layouts, per_device(): lax.dynamic_update_index_in_dim(gathered, tiles[away], unit ^ away, 0)  1.89 us
  transfers between devices with their start and end apart: 22, of which 8 were waited for; matrix products, arithmetic and copies ran while one was open for 3% of the time, Pallas kernels for 11%

profile of v7, /device:TPU:0, one launch (start us, length us, event | category | flops | bytes accessed | tf_op | source)
XLA Modules:
  0.0 75.6 jit_solution(4967704446336229716)
XLA Ops:
  0.0 1.2 %maximum_bitcast_fusion = bf16[8,2,128,128]{3,0,2,1:T(8,128)(2,1)S(1)} fusion(bf16[1,128,8,128]{3,2,1,0:T(8,128)(2,1)} %bitcast.76, bf16[1,128,8,128]{3,2,1,0:T(8,128)(2,1)} %bitcast.77), kind=kLoop, calls=%fused_computation.17 | loop fusion | flops 262144 | bytes 1048576 | tf_op jit(solution)/shard_map/transpose | solution.py:170
  1.2 0.1 copy.8
  1.3 0.1 copy-done.1
  1.4 0.4 copy.25
  1.9 5.1 %collective-permute-start.5 = (bf16[6,128,128]{2,1,0:T(8,128)(2,1)S(1)}, bf16[6,128,128]{2,1,0:T(8,128)(2,1)S(1)}, u32[]{:S(2)}, u32[]{:S(2)}) collective-permute-start(bf16[6,128,128]{2,1,0:T(8,128)(2,1)S(1)} %get-tuple-element.27), channel_id=1, source_target_pairs={{0,12},{1,13},{2,14},{3,15},{4,8},{5,9},{6,10},{7,11},{8,4},{9,5},... | collective-permute-start | bytes 589832 | tf_op jit(solution)/shard_map/ppermute | solution.py:175
  7.0 0.4 collective-permute-start.4
  7.3 0.1 fusion.14
  7.4 2.5 %collective-permute-start.6 = (bf16[6,128,128]{2,1,0:T(8,128)(2,1)S(1)}, bf16[6,128,128]{2,1,0:T(8,128)(2,1)S(1)}, u32[]{:S(2)}, u32[]{:S(2)}) collective-permute-start(bf16[6,128,128]{2,1,0:T(8,128)(2,1)S(1)} %get-tuple-element.21), channel_id=1, source_target_pairs={{0,14},{1,15},{2,12},{3,13},{4,10},{5,11},{6,8},{7,9},{8,6},{9,7},... | collective-permute-start | bytes 589832 | tf_op jit(solution)/shard_map/ppermute | solution.py:175
  10.0 1.5 %collective-permute-start = (bf16[6,128,128]{2,1,0:T(8,128)(2,1)S(1)}, bf16[6,128,128]{2,1,0:T(8,128)(2,1)S(1)}, u32[]{:S(2)}, u32[]{:S(2)}) collective-permute-start(bf16[6,128,128]{2,1,0:T(8,128)(2,1)S(1)} %get-tuple-element.23), channel_id=1, source_target_pairs={{0,2},{1,3},{2,0},{3,1},{4,6},{5,7},{6,4},{7,5},{8,10},{9,11},{10,... | collective-permute-start | bytes 589832 | tf_op jit(solution)/shard_map/ppermute | solution.py:175
  11.4 1.6 %collective-permute-start.1 = (bf16[6,128,128]{2,1,0:T(8,128)(2,1)S(1)}, bf16[6,128,128]{2,1,0:T(8,128)(2,1)S(1)}, u32[]{:S(2)}, u32[]{:S(2)}) collective-permute-start(bf16[6,128,128]{2,1,0:T(8,128)(2,1)S(1)} %get-tuple-element.24), channel_id=1, source_target_pairs={{0,4},{1,5},{2,6},{3,7},{4,0},{5,1},{6,2},{7,3},{8,12},{9,13},{10,... | collective-permute-start | bytes 589832 | tf_op jit(solution)/shard_map/ppermute | solution.py:175
  13.0 13.1 %collective-permute-start.2 = (bf16[6,128,128]{2,1,0:T(8,128)(2,1)S(1)}, bf16[6,128,128]{2,1,0:T(8,128)(2,1)S(1)}, u32[]{:S(2)}, u32[]{:S(2)}) collective-permute-start(bf16[6,128,128]{2,1,0:T(8,128)(2,1)S(1)} %get-tuple-element.25), channel_id=1, source_target_pairs={{0,6},{1,7},{2,4},{3,5},{4,2},{5,3},{6,0},{7,1},{8,14},{9,15},{10,... | collective-permute-start | bytes 589832 | tf_op jit(solution)/shard_map/ppermute | solution.py:175
  26.1 3.7 %collective-permute-done.4 = bf16[6,128,128]{2,1,0:T(8,128)(2,1)S(1)} collective-permute-done((bf16[6,128,128]{2,1,0:T(8,128)(2,1)S(1)}, bf16[6,128,128]{2,1,0:T(8,128)(2,1)S(1)}, u32[]{:S(2)}, u32[]{:S(2)}) %collective-permute-start.4) | collective-permute-done | bytes 196640 | tf_op jit(solution)/shard_map/ppermute | solution.py:175
  29.8 0.5 collective-permute-start.13
  30.3 0.1 collective-permute-start.12
  30.4 0.1 pad_add_fusion.place
  30.5 2.3 %collective-permute-done.2 = bf16[6,128,128]{2,1,0:T(8,128)(2,1)S(1)} collective-permute-done((bf16[6,128,128]{2,1,0:T(8,128)(2,1)S(1)}, bf16[6,128,128]{2,1,0:T(8,128)(2,1)S(1)}, u32[]{:S(2)}, u32[]{:S(2)}) %collective-permute-start.2) | collective-permute-done | bytes 196640 | tf_op jit(solution)/shard_map/ppermute | solution.py:175
  32.8 8.7 %collective-permute-done.3 = bf16[6,128,128]{2,1,0:T(8,128)(2,1)S(1)} collective-permute-done((bf16[6,128,128]{2,1,0:T(8,128)(2,1)S(1)}, bf16[6,128,128]{2,1,0:T(8,128)(2,1)S(1)}, u32[]{:S(2)}, u32[]{:S(2)}) %collective-permute-start.3) | collective-permute-done | bytes 196640 | tf_op jit(solution)/shard_map/ppermute | solution.py:175
  41.5 0.5 collective-permute-start.9
  42.0 0.1 collective-permute-start.10
  42.1 0.4 collective-permute-start.11
  42.6 0.4 collective-permute-done.8
  43.0 0.3 collective-permute-done.9
  43.2 0.3 collective-permute-done.10
  43.5 0.3 collective-permute-done.11
  43.8 2.1 %pack_blocks.1 = (bf16[576,8,128]{2,1,0:T(8,128)(2,1)S(1)}, bf16[2,256,8,128]{3,2,1,0:T(8,128)(2,1)S(1)}) custom-call(s32[2]{0:T(128)S(1)} %pad_add_fusion.place, s32[256]{0:T(256)S(1)} %multiply_add_fusion.targets, bf16[96,8,128]{2,1,0:T(8,128)(2,1)S(1)} %bitcast.54, bf16[96,8,128]{2,1,0:T(8,128)(2,1)S(1)} %bitcast.61, bf16[96,8,128]{2,1,0:T(8,128)(2,1)S(1)} %bitcast.62, ...), custom_call_target="tpu_custom_call" | custom-call | flops 1000 | bytes 1000 | tf_op jit(solution)/shard_map/pack_blocks/pallas_call | solution.py:194
  45.9 2.0 %attend.5 = (bf16[4,128,128]{2,1,0:T(8,128)(2,1)S(1)}, bf16[4,128,128]{2,1,0:T(8,128)(2,1)S(1)}) custom-call(s32[2]{0:T(128)S(1)} %pad_add_fusion.place, s32[16]{0:T(128)S(1)} %copy-done, bf16[576,8,128]{2,1,0:T(8,128)(2,1)S(1)} %get-tuple-element.13.q_packed, bf16[2,256,8,128]{3,2,1,0:T(8,128)(2,1)S(1)} %get-tuple-element.14.kv_packed), custom_call_target="tpu_custom_call" | custom-call | flops 1000 | bytes 1000 | tf_op jit(solution)/shard_map/attend/pallas_call | solution.py:214
  48.0 0.8 collective-permute-start.16
  48.7 0.4 collective-permute-start.18
  49.2 1.7 %attend.6 = (bf16[4,128,128]{2,1,0:T(8,128)(2,1)S(1)}, bf16[4,128,128]{2,1,0:T(8,128)(2,1)S(1)}) custom-call(s32[2]{0:T(128)S(1)} %pad_add_fusion.place, s32[16]{0:T(128)S(1)} %copy-done, bf16[576,8,128]{2,1,0:T(8,128)(2,1)S(1)} %get-tuple-element.13.q_packed, bf16[2,256,8,128]{3,2,1,0:T(8,128)(2,1)S(1)} %get-tuple-element.14.kv_packed, ...), custom_call_target="tpu_custom_call" | custom-call | flops 1000 | bytes 1000 | tf_op jit(solution)/shard_map/attend/pallas_call | solution.py:214
  50.9 4.4 %collective-permute-start.15 = (bf16[4,128,128]{2,1,0:T(8,128)(2,1)S(1)}, bf16[4,128,128]{2,1,0:T(8,128)(2,1)S(1)}, u32[]{:S(2)}, u32[]{:S(2)}) collective-permute-start(bf16[4,128,128]{2,1,0:T(8,128)(2,1)S(1)} %get-tuple-element.16), channel_id=1, source_target_pairs={{0,8},{1,9},{2,10},{3,11},{4,12},{5,13},{6,14},{7,15},{8,0},{9,1},... | collective-permute-start | bytes 393224 | tf_op jit(solution)/shard_map/ppermute | solution.py:175
  55.3 0.3 collective-permute-start.17
  55.7 3.9 %attend.9 = (bf16[4,128,128]{2,1,0:T(8,128)(2,1)S(1)}, bf16[4,128,128]{2,1,0:T(8,128)(2,1)S(1)}) custom-call(s32[2]{0:T(128)S(1)} %pad_add_fusion.place, s32[16]{0:T(128)S(1)} %copy-done, bf16[576,8,128]{2,1,0:T(8,128)(2,1)S(1)} %get-tuple-element.13.q_packed, bf16[2,256,8,128]{3,2,1,0:T(8,128)(2,1)S(1)} %get-tuple-element.14.kv_packed, ...), custom_call_target="tpu_custom_call" | custom-call | flops 1000 | bytes 1000 | tf_op jit(solution)/shard_map/attend/pallas_call | solution.py:214
  59.5 0.2 collective-permute-start.20
  59.8 4.3 %collective-permute-start.21 = (bf16[4,128,128]{2,1,0:T(8,128)(2,1)S(1)}, bf16[4,128,128]{2,1,0:T(8,128)(2,1)S(1)}, u32[]{:S(2)}, u32[]{:S(2)}) collective-permute-start(bf16[4,128,128]{2,1,0:T(8,128)(2,1)S(1)} %get-tuple-element.20), channel_id=1, source_target_pairs={{0,14},{1,15},{2,12},{3,13},{4,10},{5,11},{6,8},{7,9},{8,6},{9,7},... | collective-permute-start | bytes 393224 | tf_op jit(solution)/shard_map/ppermute | solution.py:175
  64.1 1.1 %attend.8 = bf16[4,128,128]{2,1,0:T(8,128)(2,1)S(1)} custom-call(s32[2]{0:T(128)S(1)} %pad_add_fusion.place, s32[16]{0:T(128)S(1)} %copy-done, bf16[576,8,128]{2,1,0:T(8,128)(2,1)S(1)} %get-tuple-element.13.q_packed, bf16[2,256,8,128]{3,2,1,0:T(8,128)(2,1)S(1)} %get-tuple-element.14.kv_packed, bf16[4,128,128]{2,1,0:T(8,128)(2,1)S(1)} %collective-permute-done.18.refs_0_), custom_call_target="tpu_custom_call" | custom-call | flops 1000 | bytes 1000 | tf_op jit(solution)/shard_map/attend/pallas_call | solution.py:214
  65.2 0.1 collective-permute-start.19
  65.3 1.3 %attend.7 = bf16[4,128,128]{2,1,0:T(8,128)(2,1)S(1)} custom-call(s32[2]{0:T(128)S(1)} %pad_add_fusion.place, s32[16]{0:T(128)S(1)} %copy-done, bf16[576,8,128]{2,1,0:T(8,128)(2,1)S(1)} %get-tuple-element.13.q_packed, bf16[2,256,8,128]{3,2,1,0:T(8,128)(2,1)S(1)} %get-tuple-element.14.kv_packed, bf16[4,128,128]{2,1,0:T(8,128)(2,1)S(1)} %collective-permute-done.15.refs_0_), custom_call_target="tpu_custom_call" | custom-call | flops 1000 | bytes 1000 | tf_op jit(solution)/shard_map/attend/pallas_call | solution.py:214
  66.6 0.2 broadcast_in_dim.28
  66.9 0.8 %copy.9 = bf16[8,4,128,128]{3,1,0,2:T(4,128)(2,1)S(1)} copy(bf16[8,4,128,128]{3,2,1,0:T(8,128)(2,1)S(1)} %bitcast_dynamic-update-slice_fusion) | data formatting | bytes 2097152 | tf_op jit(solution)/shard_map/jit(dynamic_update_index_in_dim)/dynamic_update_slice | solution.py:246
  67.7 0.2 copy_dynamic-update-slice_fusion.6
  67.8 0.2 copy_dynamic-update-slice_fusion.5
  68.0 5.8 %collective-permute-done.19 = bf16[4,128,128]{2,1,0:T(8,128)(2,1)S(1)} collective-permute-done((bf16[4,128,128]{2,1,0:T(8,128)(2,1)S(1)}, bf16[4,128,128]{2,1,0:T(8,128)(2,1)S(1)}, u32[]{:S(2)}, u32[]{:S(2)}) %collective-permute-start.19) | collective-permute-done | bytes 131104 | tf_op jit(solution)/shard_map/ppermute | solution.py:175
  73.8 0.1 copy_dynamic-update-slice_fusion.4
  74.0 0.2 copy_dynamic-update-slice_fusion.3
  74.2 0.2 copy_dynamic-update-slice_fusion.2
  74.3 0.2 copy_dynamic-update-slice_fusion.1
  74.5 0.2 copy_dynamic-update-slice_fusion
  74.7 1.0 %copy-done.2 = bf16[8,4,128,128]{3,1,0,2:T(4,128)(2,1)} copy-done((bf16[8,4,128,128]{3,1,0,2:T(4,128)(2,1)}, bf16[8,4,128,128]{3,1,0,2:T(4,128)(2,1)S(1)}, u32[]{:S(2)}) %copy-start.2) | copy-done | bytes 1048600
  (29 shorter events, 0.1 us)
Async XLA Ops:
  0.0 1.4 %copy-start.1 = (bf16[128,32,128]{2,1,0:T(8,128)(2,1)S(1)}, bf16[128,32,128]{2,1,0:T(8,128)(2,1)}, u32[]{:S(2)}) copy-start(bf16[128,32,128]{2,1,0:T(8,128)(2,1)} %param.6) | copy-start | bytes 3145732
  1.9 11.2 %collective-permute-start.5 = (bf16[6,128,128]{2,1,0:T(8,128)(2,1)S(1)}, bf16[6,128,128]{2,1,0:T(8,128)(2,1)S(1)}, u32[]{:S(2)}, u32[]{:S(2)}) collective-permute-start(bf16[6,128,128]{2,1,0:T(8,128)(2,1)S(1)} %get-tuple-element.27), channel_id=1, source_target_pairs={{0,12},{1,13},{2,14},{3,15},{4,8},{5,9},{6,10},{7,11},{8,4},{9,5},... | collective-permute-start | bytes 589832 | tf_op jit(solution)/shard_map/ppermute | solution.py:175
  7.0 22.8 %collective-permute-start.4 = (bf16[6,128,128]{2,1,0:T(8,128)(2,1)S(1)}, bf16[6,128,128]{2,1,0:T(8,128)(2,1)S(1)}, u32[]{:S(2)}, u32[]{:S(2)}) collective-permute-start(bf16[6,128,128]{2,1,0:T(8,128)(2,1)S(1)} %get-tuple-element.28), channel_id=1, source_target_pairs={{0,10},{1,11},{2,8},{3,9},{4,14},{5,15},{6,12},{7,13},{8,2},{9,3},... | collective-permute-start | bytes 589832 | tf_op jit(solution)/shard_map/ppermute | solution.py:175
  7.3 35.2 %copy-start.3 = (s32[256]{0:T(256)S(1)}, s32[256]{0:T(256)}, u32[]{:S(2)}) copy-start(s32[256]{0:T(256)} %param.11) | copy-start | bytes 3076
  7.3 35.2 %copy-start.4 = (s32[256]{0:T(256)S(1)}, s32[256]{0:T(256)}, u32[]{:S(2)}) copy-start(s32[256]{0:T(256)} %param.10) | copy-start | bytes 3076
  7.4 22.4 %collective-permute-start.6 = (bf16[6,128,128]{2,1,0:T(8,128)(2,1)S(1)}, bf16[6,128,128]{2,1,0:T(8,128)(2,1)S(1)}, u32[]{:S(2)}, u32[]{:S(2)}) collective-permute-start(bf16[6,128,128]{2,1,0:T(8,128)(2,1)S(1)} %get-tuple-element.21), channel_id=1, source_target_pairs={{0,14},{1,15},{2,12},{3,13},{4,10},{5,11},{6,8},{7,9},{8,6},{9,7},... | collective-permute-start | bytes 589832 | tf_op jit(solution)/shard_map/ppermute | solution.py:175
  10.0 19.9 %collective-permute-start = (bf16[6,128,128]{2,1,0:T(8,128)(2,1)S(1)}, bf16[6,128,128]{2,1,0:T(8,128)(2,1)S(1)}, u32[]{:S(2)}, u32[]{:S(2)}) collective-permute-start(bf16[6,128,128]{2,1,0:T(8,128)(2,1)S(1)} %get-tuple-element.23), channel_id=1, source_target_pairs={{0,2},{1,3},{2,0},{3,1},{4,6},{5,7},{6,4},{7,5},{8,10},{9,11},{10,... | collective-permute-start | bytes 589832 | tf_op jit(solution)/shard_map/ppermute | solution.py:175
  11.4 18.9 %collective-permute-start.1 = (bf16[6,128,128]{2,1,0:T(8,128)(2,1)S(1)}, bf16[6,128,128]{2,1,0:T(8,128)(2,1)S(1)}, u32[]{:S(2)}, u32[]{:S(2)}) collective-permute-start(bf16[6,128,128]{2,1,0:T(8,128)(2,1)S(1)} %get-tuple-element.24), channel_id=1, source_target_pairs={{0,4},{1,5},{2,6},{3,7},{4,0},{5,1},{6,2},{7,3},{8,12},{9,13},{10,... | collective-permute-start | bytes 589832 | tf_op jit(solution)/shard_map/ppermute | solution.py:175
  13.0 19.8 %collective-permute-start.2 = (bf16[6,128,128]{2,1,0:T(8,128)(2,1)S(1)}, bf16[6,128,128]{2,1,0:T(8,128)(2,1)S(1)}, u32[]{:S(2)}, u32[]{:S(2)}) collective-permute-start(bf16[6,128,128]{2,1,0:T(8,128)(2,1)S(1)} %get-tuple-element.25), channel_id=1, source_target_pairs={{0,6},{1,7},{2,4},{3,5},{4,2},{5,3},{6,0},{7,1},{8,14},{9,15},{10,... | collective-permute-start | bytes 589832 | tf_op jit(solution)/shard_map/ppermute | solution.py:175
  29.8 11.7 %collective-permute-start.3 = (bf16[6,128,128]{2,1,0:T(8,128)(2,1)S(1)}, bf16[6,128,128]{2,1,0:T(8,128)(2,1)S(1)}, u32[]{:S(2)}, u32[]{:S(2)}) collective-permute-start(bf16[6,128,128]{2,1,0:T(8,128)(2,1)S(1)} %get-tuple-element.26), channel_id=1, source_target_pairs={{0,8},{1,9},{2,10},{3,11},{4,12},{5,13},{6,14},{7,15},{8,0},{9,1},... | collective-permute-start | bytes 589832 | tf_op jit(solution)/shard_map/ppermute | solution.py:175
  29.8 11.7 %collective-permute-start.7 = (bf16[6,128,128]{2,1,0:T(8,128)(2,1)S(1)}, bf16[6,128,128]{2,1,0:T(8,128)(2,1)S(1)}, u32[]{:S(2)}, u32[]{:S(2)}) collective-permute-start(bf16[6,128,128]{2,1,0:T(8,128)(2,1)S(1)} %bitcast.53), channel_id=1, source_target_pairs={{0,1},{1,0},{2,3},{3,2},{4,5},{5,4},{6,7},{7,6},{8,9},{9,8},{10,11... | collective-permute-start | bytes 589832 | tf_op jit(solution)/shard_map/ppermute | solution.py:175
  29.8 12.2 %collective-permute-start.13 = (bf16[6,128,128]{2,1,0:T(8,128)(2,1)S(1)}, bf16[6,128,128]{2,1,0:T(8,128)(2,1)S(1)}, u32[]{:S(2)}, u32[]{:S(2)}) collective-permute-start(bf16[6,128,128]{2,1,0:T(8,128)(2,1)S(1)} %collective-permute-done.5), channel_id=1, source_target_pairs={{0,1},{1,0},{2,3},{3,2},{4,5},{5,4},{6,7},{7,6},{8,9},{9,8},{10,11... | collective-permute-start | bytes 589832 | tf_op jit(solution)/shard_map/ppermute | solution.py:175
  30.3 11.8 %collective-permute-start.12 = (bf16[6,128,128]{2,1,0:T(8,128)(2,1)S(1)}, bf16[6,128,128]{2,1,0:T(8,128)(2,1)S(1)}, u32[]{:S(2)}, u32[]{:S(2)}) collective-permute-start(bf16[6,128,128]{2,1,0:T(8,128)(2,1)S(1)} %collective-permute-done.4), channel_id=1, source_target_pairs={{0,1},{1,0},{2,3},{3,2},{4,5},{5,4},{6,7},{7,6},{8,9},{9,8},{10,11... | collective-permute-start | bytes 589832 | tf_op jit(solution)/shard_map/ppermute | solution.py:175
  32.8 9.7 %collective-permute-start.14 = (bf16[6,128,128]{2,1,0:T(8,128)(2,1)S(1)}, bf16[6,128,128]{2,1,0:T(8,128)(2,1)S(1)}, u32[]{:S(2)}, u32[]{:S(2)}) collective-permute-start(bf16[6,128,128]{2,1,0:T(8,128)(2,1)S(1)} %collective-permute-done.6), channel_id=1, source_target_pairs={{0,1},{1,0},{2,3},{3,2},{4,5},{5,4},{6,7},{7,6},{8,9},{9,8},{10,11... | collective-permute-start | bytes 589832 | tf_op jit(solution)/shard_map/ppermute | solution.py:175
  41.5 1.4 %collective-permute-start.8 = (bf16[6,128,128]{2,1,0:T(8,128)(2,1)S(1)}, bf16[6,128,128]{2,1,0:T(8,128)(2,1)S(1)}, u32[]{:S(2)}, u32[]{:S(2)}) collective-permute-start(bf16[6,128,128]{2,1,0:T(8,128)(2,1)S(1)} %collective-permute-done), channel_id=1, source_target_pairs={{0,1},{1,0},{2,3},{3,2},{4,5},{5,4},{6,7},{7,6},{8,9},{9,8},{10,11... | collective-permute-start | bytes 589832 | tf_op jit(solution)/shard_map/ppermute | solution.py:175
  41.5 1.7 %collective-permute-start.9 = (bf16[6,128,128]{2,1,0:T(8,128)(2,1)S(1)}, bf16[6,128,128]{2,1,0:T(8,128)(2,1)S(1)}, u32[]{:S(2)}, u32[]{:S(2)}) collective-permute-start(bf16[6,128,128]{2,1,0:T(8,128)(2,1)S(1)} %collective-permute-done.1), channel_id=1, source_target_pairs={{0,1},{1,0},{2,3},{3,2},{4,5},{5,4},{6,7},{7,6},{8,9},{9,8},{10,11... | collective-permute-start | bytes 589832 | tf_op jit(solution)/shard_map/ppermute | solution.py:175
  42.0 1.5 %collective-permute-start.10 = (bf16[6,128,128]{2,1,0:T(8,128)(2,1)S(1)}, bf16[6,128,128]{2,1,0:T(8,128)(2,1)S(1)}, u32[]{:S(2)}, u32[]{:S(2)}) collective-permute-start(bf16[6,128,128]{2,1,0:T(8,128)(2,1)S(1)} %collective-permute-done.2), channel_id=1, source_target_pairs={{0,1},{1,0},{2,3},{3,2},{4,5},{5,4},{6,7},{7,6},{8,9},{9,8},{10,11... | collective-permute-start | bytes 589832 | tf_op jit(solution)/shard_map/ppermute | solution.py:175
  42.1 1.7 %collective-permute-start.11 = (bf16[6,128,128]{2,1,0:T(8,128)(2,1)S(1)}, bf16[6,128,128]{2,1,0:T(8,128)(2,1)S(1)}, u32[]{:S(2)}, u32[]{:S(2)}) collective-permute-start(bf16[6,128,128]{2,1,0:T(8,128)(2,1)S(1)} %collective-permute-done.3), channel_id=1, source_target_pairs={{0,1},{1,0},{2,3},{3,2},{4,5},{5,4},{6,7},{7,6},{8,9},{9,8},{10,11... | collective-permute-start | bytes 589832 | tf_op jit(solution)/shard_map/ppermute | solution.py:175
  43.8 2.1 %copy-start = (s32[16]{0:T(128)S(1)}, s32[16]{0:T(128)}, u32[]{:S(2)}) copy-start(s32[16]{0:T(128)} %lengths.9) | copy-start | bytes 196
  48.0 7.7 %collective-permute-start.16 = (bf16[4,128,128]{2,1,0:T(8,128)(2,1)S(1)}, bf16[4,128,128]{2,1,0:T(8,128)(2,1)S(1)}, u32[]{:S(2)}, u32[]{:S(2)}) collective-permute-start(bf16[4,128,128]{2,1,0:T(8,128)(2,1)S(1)} %get-tuple-element.17), channel_id=1, source_target_pairs={{0,2},{1,3},{2,0},{3,1},{4,6},{5,7},{6,4},{7,5},{8,10},{9,11},{10,... | collective-permute-start | bytes 393224 | tf_op jit(solution)/shard_map/ppermute | solution.py:175
  48.7 15.3 %collective-permute-start.18 = (bf16[4,128,128]{2,1,0:T(8,128)(2,1)S(1)}, bf16[4,128,128]{2,1,0:T(8,128)(2,1)S(1)}, u32[]{:S(2)}, u32[]{:S(2)}) collective-permute-start(bf16[4,128,128]{2,1,0:T(8,128)(2,1)S(1)} %get-tuple-element.15.refs_0_), channel_id=1, source_target_pairs={{0,10},{1,11},{2,8},{3,9},{4,14},{5,15},{6,12},{7,13},{8,2},{9,3},... | collective-permute-start | bytes 393224 | tf_op jit(solution)/shard_map/ppermute | solution.py:175
  50.9 14.4 %collective-permute-start.15 = (bf16[4,128,128]{2,1,0:T(8,128)(2,1)S(1)}, bf16[4,128,128]{2,1,0:T(8,128)(2,1)S(1)}, u32[]{:S(2)}, u32[]{:S(2)}) collective-permute-start(bf16[4,128,128]{2,1,0:T(8,128)(2,1)S(1)} %get-tuple-element.16), channel_id=1, source_target_pairs={{0,8},{1,9},{2,10},{3,11},{4,12},{5,13},{6,14},{7,15},{8,0},{9,1},... | collective-permute-start | bytes 393224 | tf_op jit(solution)/shard_map/ppermute | solution.py:175
  55.3 12.5 %collective-permute-start.17 = (bf16[4,128,128]{2,1,0:T(8,128)(2,1)S(1)}, bf16[4,128,128]{2,1,0:T(8,128)(2,1)S(1)}, u32[]{:S(2)}, u32[]{:S(2)}) collective-permute-start(bf16[4,128,128]{2,1,0:T(8,128)(2,1)S(1)} %get-tuple-element.18), channel_id=1, source_target_pairs={{0,4},{1,5},{2,6},{3,7},{4,0},{5,1},{6,2},{7,3},{8,12},{9,13},{10,... | collective-permute-start | bytes 393224 | tf_op jit(solution)/shard_map/ppermute | solution.py:175
  59.5 14.8 %collective-permute-start.20 = (bf16[4,128,128]{2,1,0:T(8,128)(2,1)S(1)}, bf16[4,128,128]{2,1,0:T(8,128)(2,1)S(1)}, u32[]{:S(2)}, u32[]{:S(2)}) collective-permute-start(bf16[4,128,128]{2,1,0:T(8,128)(2,1)S(1)} %get-tuple-element.19), channel_id=1, source_target_pairs={{0,12},{1,13},{2,14},{3,15},{4,8},{5,9},{6,10},{7,11},{8,4},{9,5},... | collective-permute-start | bytes 393224 | tf_op jit(solution)/shard_map/ppermute | solution.py:175
  59.8 14.7 %collective-permute-start.21 = (bf16[4,128,128]{2,1,0:T(8,128)(2,1)S(1)}, bf16[4,128,128]{2,1,0:T(8,128)(2,1)S(1)}, u32[]{:S(2)}, u32[]{:S(2)}) collective-permute-start(bf16[4,128,128]{2,1,0:T(8,128)(2,1)S(1)} %get-tuple-element.20), channel_id=1, source_target_pairs={{0,14},{1,15},{2,12},{3,13},{4,10},{5,11},{6,8},{7,9},{8,6},{9,7},... | collective-permute-start | bytes 393224 | tf_op jit(solution)/shard_map/ppermute | solution.py:175
  65.2 8.7 %collective-permute-start.19 = (bf16[4,128,128]{2,1,0:T(8,128)(2,1)S(1)}, bf16[4,128,128]{2,1,0:T(8,128)(2,1)S(1)}, u32[]{:S(2)}, u32[]{:S(2)}) collective-permute-start(bf16[4,128,128]{2,1,0:T(8,128)(2,1)S(1)} %attend.8), channel_id=1, source_target_pairs={{0,6},{1,7},{2,4},{3,5},{4,2},{5,3},{6,0},{7,1},{8,14},{9,15},{10,... | collective-permute-start | bytes 393224 | tf_op jit(solution)/shard_map/ppermute | solution.py:175
  74.7 1.0 %copy-start.2 = (bf16[8,4,128,128]{3,1,0,2:T(4,128)(2,1)}, bf16[8,4,128,128]{3,1,0,2:T(4,128)(2,1)S(1)}, u32[]{:S(2)}) copy-start(bf16[8,4,128,128]{3,1,0,2:T(4,128)(2,1)S(1)} %copy_dynamic-update-slice_fusion) | copy-start | bytes 3145732

commit v8 on v6

--- a/solution.py
+++ b/solution.py
@@ -233,7 +233,7 @@
             raw[away] = out
             tiles[away] = hop(out, 2 * away) if away else out
 
-    far_tiles = [half + 1, half] + list(reversed(range(half + 2, units)))
+    far_tiles = [half, half + 1] + list(reversed(range(half + 2, units)))
     attend((far_tiles[0], 1), [])
     attend((far_tiles[1], 2), [raw[far_tiles[0]]])
     for i in range(2, half, 2):

time: 75.5 us -> 75.4 us (level)
  transfers between devices with their start and end apart: 22 -> 22, of which waited for: 8 -> 9; matrix products, arithmetic and copies ran while one was open for 3% -> 3% of each run, Pallas kernels for 10% -> 11%
where the time goes in v8:
time: 75.4 us; the launch traced here: 75.5 us
  starting transfers between devices  35.7 us (47%)
  waiting for transfers between devices  22.3 us (30%)
  Pallas kernels  12.2 us (16%)
  local copies, waits for them, and re-layouts  3.71 us (5%)
  other arithmetic  1.39 us (2%)
    ppermute x22, starting transfers between devices, hop(): return lax.ppermute(x, 'seq', [(i, i ^ distance) for i in range(shards)])  35.7 us
    ppermute x22, waiting for transfers between devices, hop(): return lax.ppermute(x, 'seq', [(i, i ^ distance) for i in range(shards)])  22.3 us
    pallas_call x5, Pallas kernels, attend(): pl.pallas_call(functools.partial(attend_kernel, aways=aways, heads=heads,...  9.91 us
    pallas_call x1, Pallas kernels, pack(): pl.pallas_call(functools.partial(pack_kernel, groups=groups, heads=heads,...  2.25 us
    dynamic_update_slice x9, local copies, waits for them, and re-layouts, per_device(): lax.dynamic_update_index_in_dim(gathered, tiles[away], unit ^ away, 0)  1.89 us
  transfers between devices with their start and end apart: 22, of which 9 were waited for; matrix products, arithmetic and copies ran while one was open for 3% of the time, Pallas kernels for 11%

profile of v8, /device:TPU:0, one launch (start us, length us, event | category | flops | bytes accessed | tf_op | source)
XLA Modules:
  0.0 75.5 jit_solution(4448857065739489450)
XLA Ops:
  0.0 1.2 %maximum_bitcast_fusion = bf16[8,2,128,128]{3,0,2,1:T(8,128)(2,1)S(1)} fusion(bf16[1,128,8,128]{3,2,1,0:T(8,128)(2,1)} %bitcast.76, bf16[1,128,8,128]{3,2,1,0:T(8,128)(2,1)} %bitcast.77), kind=kLoop, calls=%fused_computation.17 | loop fusion | flops 262144 | bytes 1048576 | tf_op jit(solution)/shard_map/transpose | solution.py:170
  1.2 0.1 copy.8
  1.3 0.1 copy-done.1
  1.4 0.4 copy.25
  1.9 5.1 %collective-permute-start.5 = (bf16[6,128,128]{2,1,0:T(8,128)(2,1)S(1)}, bf16[6,128,128]{2,1,0:T(8,128)(2,1)S(1)}, u32[]{:S(2)}, u32[]{:S(2)}) collective-permute-start(bf16[6,128,128]{2,1,0:T(8,128)(2,1)S(1)} %get-tuple-element.27), channel_id=1, source_target_pairs={{0,12},{1,13},{2,14},{3,15},{4,8},{5,9},{6,10},{7,11},{8,4},{9,5},... | collective-permute-start | bytes 589832 | tf_op jit(solution)/shard_map/ppermute | solution.py:175
  7.0 0.4 collective-permute-start.4
  7.3 0.1 fusion.14
  7.4 2.5 %collective-permute-start.6 = (bf16[6,128,128]{2,1,0:T(8,128)(2,1)S(1)}, bf16[6,128,128]{2,1,0:T(8,128)(2,1)S(1)}, u32[]{:S(2)}, u32[]{:S(2)}) collective-permute-start(bf16[6,128,128]{2,1,0:T(8,128)(2,1)S(1)} %get-tuple-element.21), channel_id=1, source_target_pairs={{0,14},{1,15},{2,12},{3,13},{4,10},{5,11},{6,8},{7,9},{8,6},{9,7},... | collective-permute-start | bytes 589832 | tf_op jit(solution)/shard_map/ppermute | solution.py:175
  10.0 1.5 %collective-permute-start = (bf16[6,128,128]{2,1,0:T(8,128)(2,1)S(1)}, bf16[6,128,128]{2,1,0:T(8,128)(2,1)S(1)}, u32[]{:S(2)}, u32[]{:S(2)}) collective-permute-start(bf16[6,128,128]{2,1,0:T(8,128)(2,1)S(1)} %get-tuple-element.23), channel_id=1, source_target_pairs={{0,2},{1,3},{2,0},{3,1},{4,6},{5,7},{6,4},{7,5},{8,10},{9,11},{10,... | collective-permute-start | bytes 589832 | tf_op jit(solution)/shard_map/ppermute | solution.py:175
  11.4 1.6 %collective-permute-start.1 = (bf16[6,128,128]{2,1,0:T(8,128)(2,1)S(1)}, bf16[6,128,128]{2,1,0:T(8,128)(2,1)S(1)}, u32[]{:S(2)}, u32[]{:S(2)}) collective-permute-start(bf16[6,128,128]{2,1,0:T(8,128)(2,1)S(1)} %get-tuple-element.24), channel_id=1, source_target_pairs={{0,4},{1,5},{2,6},{3,7},{4,0},{5,1},{6,2},{7,3},{8,12},{9,13},{10,... | collective-permute-start | bytes 589832 | tf_op jit(solution)/shard_map/ppermute | solution.py:175
  13.0 13.1 %collective-permute-start.2 = (bf16[6,128,128]{2,1,0:T(8,128)(2,1)S(1)}, bf16[6,128,128]{2,1,0:T(8,128)(2,1)S(1)}, u32[]{:S(2)}, u32[]{:S(2)}) collective-permute-start(bf16[6,128,128]{2,1,0:T(8,128)(2,1)S(1)} %get-tuple-element.25), channel_id=1, source_target_pairs={{0,6},{1,7},{2,4},{3,5},{4,2},{5,3},{6,0},{7,1},{8,14},{9,15},{10,... | collective-permute-start | bytes 589832 | tf_op jit(solution)/shard_map/ppermute | solution.py:175
  26.1 3.7 %collective-permute-done.4 = bf16[6,128,128]{2,1,0:T(8,128)(2,1)S(1)} collective-permute-done((bf16[6,128,128]{2,1,0:T(8,128)(2,1)S(1)}, bf16[6,128,128]{2,1,0:T(8,128)(2,1)S(1)}, u32[]{:S(2)}, u32[]{:S(2)}) %collective-permute-start.4) | collective-permute-done | bytes 196640 | tf_op jit(solution)/shard_map/ppermute | solution.py:175
  29.8 0.5 collective-permute-start.13
  30.3 0.1 collective-permute-start.12
  30.4 0.1 pad_add_fusion.place
  30.5 2.3 %collective-permute-done.2 = bf16[6,128,128]{2,1,0:T(8,128)(2,1)S(1)} collective-permute-done((bf16[6,128,128]{2,1,0:T(8,128)(2,1)S(1)}, bf16[6,128,128]{2,1,0:T(8,128)(2,1)S(1)}, u32[]{:S(2)}, u32[]{:S(2)}) %collective-permute-start.2) | collective-permute-done | bytes 196640 | tf_op jit(solution)/shard_map/ppermute | solution.py:175
  32.8 8.7 %collective-permute-done.3 = bf16[6,128,128]{2,1,0:T(8,128)(2,1)S(1)} collective-permute-done((bf16[6,128,128]{2,1,0:T(8,128)(2,1)S(1)}, bf16[6,128,128]{2,1,0:T(8,128)(2,1)S(1)}, u32[]{:S(2)}, u32[]{:S(2)}) %collective-permute-start.3) | collective-permute-done | bytes 196640 | tf_op jit(solution)/shard_map/ppermute | solution.py:175
  41.5 0.5 collective-permute-start.9
  42.0 0.1 collective-permute-start.10
  42.1 0.4 collective-permute-start.11
  42.6 0.4 collective-permute-done.8
  43.0 0.3 collective-permute-done.9
  43.2 0.3 collective-permute-done.10
  43.5 0.3 collective-permute-done.11
  43.8 2.3 %pack_blocks.1 = (bf16[576,8,128]{2,1,0:T(8,128)(2,1)S(1)}, bf16[2,256,8,128]{3,2,1,0:T(8,128)(2,1)S(1)}) custom-call(s32[2]{0:T(128)S(1)} %pad_add_fusion.place, s32[256]{0:T(256)S(1)} %multiply_add_fusion.targets, bf16[96,8,128]{2,1,0:T(8,128)(2,1)S(1)} %bitcast.54, bf16[96,8,128]{2,1,0:T(8,128)(2,1)S(1)} %bitcast.61, bf16[96,8,128]{2,1,0:T(8,128)(2,1)S(1)} %bitcast.62, ...), custom_call_target="tpu_custom_call" | custom-call | flops 1000 | bytes 1000 | tf_op jit(solution)/shard_map/pack_blocks/pallas_call | solution.py:194
  46.1 1.7 %attend.5 = (bf16[4,128,128]{2,1,0:T(8,128)(2,1)S(1)}, bf16[4,128,128]{2,1,0:T(8,128)(2,1)S(1)}) custom-call(s32[2]{0:T(128)S(1)} %pad_add_fusion.place, s32[16]{0:T(128)S(1)} %copy-done, bf16[576,8,128]{2,1,0:T(8,128)(2,1)S(1)} %get-tuple-element.13.q_packed, bf16[2,256,8,128]{3,2,1,0:T(8,128)(2,1)S(1)} %get-tuple-element.14.kv_packed), custom_call_target="tpu_custom_call" | custom-call | flops 1000 | bytes 1000 | tf_op jit(solution)/shard_map/attend/pallas_call | solution.py:214
  47.8 1.4 %collective-permute-start.16 = (bf16[4,128,128]{2,1,0:T(8,128)(2,1)S(1)}, bf16[4,128,128]{2,1,0:T(8,128)(2,1)S(1)}, u32[]{:S(2)}, u32[]{:S(2)}) collective-permute-start(bf16[4,128,128]{2,1,0:T(8,128)(2,1)S(1)} %get-tuple-element.17), channel_id=1, source_target_pairs={{0,2},{1,3},{2,0},{3,1},{4,6},{5,7},{6,4},{7,5},{8,10},{9,11},{10,... | collective-permute-start | bytes 393224 | tf_op jit(solution)/shard_map/ppermute | solution.py:175
  49.2 2.1 %attend.6 = (bf16[4,128,128]{2,1,0:T(8,128)(2,1)S(1)}, bf16[4,128,128]{2,1,0:T(8,128)(2,1)S(1)}) custom-call(s32[2]{0:T(128)S(1)} %pad_add_fusion.place, s32[16]{0:T(128)S(1)} %copy-done, bf16[576,8,128]{2,1,0:T(8,128)(2,1)S(1)} %get-tuple-element.13.q_packed, bf16[2,256,8,128]{3,2,1,0:T(8,128)(2,1)S(1)} %get-tuple-element.14.kv_packed, ...), custom_call_target="tpu_custom_call" | custom-call | flops 1000 | bytes 1000 | tf_op jit(solution)/shard_map/attend/pallas_call | solution.py:214
  51.3 3.9 %collective-permute-start.15 = (bf16[4,128,128]{2,1,0:T(8,128)(2,1)S(1)}, bf16[4,128,128]{2,1,0:T(8,128)(2,1)S(1)}, u32[]{:S(2)}, u32[]{:S(2)}) collective-permute-start(bf16[4,128,128]{2,1,0:T(8,128)(2,1)S(1)} %get-tuple-element.16), channel_id=1, source_target_pairs={{0,10},{1,11},{2,8},{3,9},{4,14},{5,15},{6,12},{7,13},{8,2},{9,3},... | collective-permute-start | bytes 393224 | tf_op jit(solution)/shard_map/ppermute | solution.py:175
  55.2 0.3 collective-permute-start.17
  55.5 3.9 %attend.9 = (bf16[4,128,128]{2,1,0:T(8,128)(2,1)S(1)}, bf16[4,128,128]{2,1,0:T(8,128)(2,1)S(1)}) custom-call(s32[2]{0:T(128)S(1)} %pad_add_fusion.place, s32[16]{0:T(128)S(1)} %copy-done, bf16[576,8,128]{2,1,0:T(8,128)(2,1)S(1)} %get-tuple-element.13.q_packed, bf16[2,256,8,128]{3,2,1,0:T(8,128)(2,1)S(1)} %get-tuple-element.14.kv_packed, ...), custom_call_target="tpu_custom_call" | custom-call | flops 1000 | bytes 1000 | tf_op jit(solution)/shard_map/attend/pallas_call | solution.py:214
  59.4 0.5 collective-permute-start.20
  59.9 3.8 %collective-permute-start.21 = (bf16[4,128,128]{2,1,0:T(8,128)(2,1)S(1)}, bf16[4,128,128]{2,1,0:T(8,128)(2,1)S(1)}, u32[]{:S(2)}, u32[]{:S(2)}) collective-permute-start(bf16[4,128,128]{2,1,0:T(8,128)(2,1)S(1)} %get-tuple-element.20), channel_id=1, source_target_pairs={{0,14},{1,15},{2,12},{3,13},{4,10},{5,11},{6,8},{7,9},{8,6},{9,7},... | collective-permute-start | bytes 393224 | tf_op jit(solution)/shard_map/ppermute | solution.py:175
  63.7 1.1 %attend.8 = bf16[4,128,128]{2,1,0:T(8,128)(2,1)S(1)} custom-call(s32[2]{0:T(128)S(1)} %pad_add_fusion.place, s32[16]{0:T(128)S(1)} %copy-done, bf16[576,8,128]{2,1,0:T(8,128)(2,1)S(1)} %get-tuple-element.13.q_packed, bf16[2,256,8,128]{3,2,1,0:T(8,128)(2,1)S(1)} %get-tuple-element.14.kv_packed, bf16[4,128,128]{2,1,0:T(8,128)(2,1)S(1)} %collective-permute-done.18.refs_0_), custom_call_target="tpu_custom_call" | custom-call | flops 1000 | bytes 1000 | tf_op jit(solution)/shard_map/attend/pallas_call | solution.py:214
  64.8 0.1 collective-permute-start.19
  64.9 0.1 collective-permute-done.15.refs_0_
  65.0 1.1 %attend.7 = bf16[4,128,128]{2,1,0:T(8,128)(2,1)S(1)} custom-call(s32[2]{0:T(128)S(1)} %pad_add_fusion.place, s32[16]{0:T(128)S(1)} %copy-done, bf16[576,8,128]{2,1,0:T(8,128)(2,1)S(1)} %get-tuple-element.13.q_packed, bf16[2,256,8,128]{3,2,1,0:T(8,128)(2,1)S(1)} %get-tuple-element.14.kv_packed, bf16[4,128,128]{2,1,0:T(8,128)(2,1)S(1)} %collective-permute-done.15.refs_0_), custom_call_target="tpu_custom_call" | custom-call | flops 1000 | bytes 1000 | tf_op jit(solution)/shard_map/attend/pallas_call | solution.py:214
  66.1 0.2 broadcast_in_dim.28
  66.4 0.8 %copy.9 = bf16[8,4,128,128]{3,1,0,2:T(4,128)(2,1)S(1)} copy(bf16[8,4,128,128]{3,2,1,0:T(8,128)(2,1)S(1)} %bitcast_dynamic-update-slice_fusion) | data formatting | bytes 2097152 | tf_op jit(solution)/shard_map/jit(dynamic_update_index_in_dim)/dynamic_update_slice | solution.py:246
  67.2 0.2 copy_dynamic-update-slice_fusion.6
  67.4 0.2 copy_dynamic-update-slice_fusion.5
  67.5 6.2 %collective-permute-done.19 = bf16[4,128,128]{2,1,0:T(8,128)(2,1)S(1)} collective-permute-done((bf16[4,128,128]{2,1,0:T(8,128)(2,1)S(1)}, bf16[4,128,128]{2,1,0:T(8,128)(2,1)S(1)}, u32[]{:S(2)}, u32[]{:S(2)}) %collective-permute-start.19) | collective-permute-done | bytes 131104 | tf_op jit(solution)/shard_map/ppermute | solution.py:175
  73.7 0.1 copy_dynamic-update-slice_fusion.4
  73.9 0.2 copy_dynamic-update-slice_fusion.3
  74.1 0.2 copy_dynamic-update-slice_fusion.2
  74.2 0.2 copy_dynamic-update-slice_fusion.1
  74.4 0.2 copy_dynamic-update-slice_fusion
  74.6 1.0 %copy-done.2 = bf16[8,4,128,128]{3,1,0,2:T(4,128)(2,1)} copy-done((bf16[8,4,128,128]{3,1,0,2:T(4,128)(2,1)}, bf16[8,4,128,128]{3,1,0,2:T(4,128)(2,1)S(1)}, u32[]{:S(2)}) %copy-start.2) | copy-done | bytes 1048600
  (29 shorter events, 0.1 us)
Async XLA Ops:
  0.0 1.4 %copy-start.1 = (bf16[128,32,128]{2,1,0:T(8,128)(2,1)S(1)}, bf16[128,32,128]{2,1,0:T(8,128)(2,1)}, u32[]{:S(2)}) copy-start(bf16[128,32,128]{2,1,0:T(8,128)(2,1)} %param.6) | copy-start | bytes 3145732
  1.9 11.2 %collective-permute-start.5 = (bf16[6,128,128]{2,1,0:T(8,128)(2,1)S(1)}, bf16[6,128,128]{2,1,0:T(8,128)(2,1)S(1)}, u32[]{:S(2)}, u32[]{:S(2)}) collective-permute-start(bf16[6,128,128]{2,1,0:T(8,128)(2,1)S(1)} %get-tuple-element.27), channel_id=1, source_target_pairs={{0,12},{1,13},{2,14},{3,15},{4,8},{5,9},{6,10},{7,11},{8,4},{9,5},... | collective-permute-start | bytes 589832 | tf_op jit(solution)/shard_map/ppermute | solution.py:175
  7.0 22.8 %collective-permute-start.4 = (bf16[6,128,128]{2,1,0:T(8,128)(2,1)S(1)}, bf16[6,128,128]{2,1,0:T(8,128)(2,1)S(1)}, u32[]{:S(2)}, u32[]{:S(2)}) collective-permute-start(bf16[6,128,128]{2,1,0:T(8,128)(2,1)S(1)} %get-tuple-element.28), channel_id=1, source_target_pairs={{0,10},{1,11},{2,8},{3,9},{4,14},{5,15},{6,12},{7,13},{8,2},{9,3},... | collective-permute-start | bytes 589832 | tf_op jit(solution)/shard_map/ppermute | solution.py:175
  7.3 35.2 %copy-start.3 = (s32[256]{0:T(256)S(1)}, s32[256]{0:T(256)}, u32[]{:S(2)}) copy-start(s32[256]{0:T(256)} %param.11) | copy-start | bytes 3076
  7.3 35.2 %copy-start.4 = (s32[256]{0:T(256)S(1)}, s32[256]{0:T(256)}, u32[]{:S(2)}) copy-start(s32[256]{0:T(256)} %param.10) | copy-start | bytes 3076
  7.4 22.4 %collective-permute-start.6 = (bf16[6,128,128]{2,1,0:T(8,128)(2,1)S(1)}, bf16[6,128,128]{2,1,0:T(8,128)(2,1)S(1)}, u32[]{:S(2)}, u32[]{:S(2)}) collective-permute-start(bf16[6,128,128]{2,1,0:T(8,128)(2,1)S(1)} %get-tuple-element.21), channel_id=1, source_target_pairs={{0,14},{1,15},{2,12},{3,13},{4,10},{5,11},{6,8},{7,9},{8,6},{9,7},... | collective-permute-start | bytes 589832 | tf_op jit(solution)/shard_map/ppermute | solution.py:175
  10.0 19.9 %collective-permute-start = (bf16[6,128,128]{2,1,0:T(8,128)(2,1)S(1)}, bf16[6,128,128]{2,1,0:T(8,128)(2,1)S(1)}, u32[]{:S(2)}, u32[]{:S(2)}) collective-permute-start(bf16[6,128,128]{2,1,0:T(8,128)(2,1)S(1)} %get-tuple-element.23), channel_id=1, source_target_pairs={{0,2},{1,3},{2,0},{3,1},{4,6},{5,7},{6,4},{7,5},{8,10},{9,11},{10,... | collective-permute-start | bytes 589832 | tf_op jit(solution)/shard_map/ppermute | solution.py:175
  11.4 18.9 %collective-permute-start.1 = (bf16[6,128,128]{2,1,0:T(8,128)(2,1)S(1)}, bf16[6,128,128]{2,1,0:T(8,128)(2,1)S(1)}, u32[]{:S(2)}, u32[]{:S(2)}) collective-permute-start(bf16[6,128,128]{2,1,0:T(8,128)(2,1)S(1)} %get-tuple-element.24), channel_id=1, source_target_pairs={{0,4},{1,5},{2,6},{3,7},{4,0},{5,1},{6,2},{7,3},{8,12},{9,13},{10,... | collective-permute-start | bytes 589832 | tf_op jit(solution)/shard_map/ppermute | solution.py:175
  13.0 19.8 %collective-permute-start.2 = (bf16[6,128,128]{2,1,0:T(8,128)(2,1)S(1)}, bf16[6,128,128]{2,1,0:T(8,128)(2,1)S(1)}, u32[]{:S(2)}, u32[]{:S(2)}) collective-permute-start(bf16[6,128,128]{2,1,0:T(8,128)(2,1)S(1)} %get-tuple-element.25), channel_id=1, source_target_pairs={{0,6},{1,7},{2,4},{3,5},{4,2},{5,3},{6,0},{7,1},{8,14},{9,15},{10,... | collective-permute-start | bytes 589832 | tf_op jit(solution)/shard_map/ppermute | solution.py:175
  29.8 11.7 %collective-permute-start.3 = (bf16[6,128,128]{2,1,0:T(8,128)(2,1)S(1)}, bf16[6,128,128]{2,1,0:T(8,128)(2,1)S(1)}, u32[]{:S(2)}, u32[]{:S(2)}) collective-permute-start(bf16[6,128,128]{2,1,0:T(8,128)(2,1)S(1)} %get-tuple-element.26), channel_id=1, source_target_pairs={{0,8},{1,9},{2,10},{3,11},{4,12},{5,13},{6,14},{7,15},{8,0},{9,1},... | collective-permute-start | bytes 589832 | tf_op jit(solution)/shard_map/ppermute | solution.py:175
  29.8 11.7 %collective-permute-start.7 = (bf16[6,128,128]{2,1,0:T(8,128)(2,1)S(1)}, bf16[6,128,128]{2,1,0:T(8,128)(2,1)S(1)}, u32[]{:S(2)}, u32[]{:S(2)}) collective-permute-start(bf16[6,128,128]{2,1,0:T(8,128)(2,1)S(1)} %bitcast.53), channel_id=1, source_target_pairs={{0,1},{1,0},{2,3},{3,2},{4,5},{5,4},{6,7},{7,6},{8,9},{9,8},{10,11... | collective-permute-start | bytes 589832 | tf_op jit(solution)/shard_map/ppermute | solution.py:175
  29.8 12.2 %collective-permute-start.13 = (bf16[6,128,128]{2,1,0:T(8,128)(2,1)S(1)}, bf16[6,128,128]{2,1,0:T(8,128)(2,1)S(1)}, u32[]{:S(2)}, u32[]{:S(2)}) collective-permute-start(bf16[6,128,128]{2,1,0:T(8,128)(2,1)S(1)} %collective-permute-done.5), channel_id=1, source_target_pairs={{0,1},{1,0},{2,3},{3,2},{4,5},{5,4},{6,7},{7,6},{8,9},{9,8},{10,11... | collective-permute-start | bytes 589832 | tf_op jit(solution)/shard_map/ppermute | solution.py:175
  30.3 11.8 %collective-permute-start.12 = (bf16[6,128,128]{2,1,0:T(8,128)(2,1)S(1)}, bf16[6,128,128]{2,1,0:T(8,128)(2,1)S(1)}, u32[]{:S(2)}, u32[]{:S(2)}) collective-permute-start(bf16[6,128,128]{2,1,0:T(8,128)(2,1)S(1)} %collective-permute-done.4), channel_id=1, source_target_pairs={{0,1},{1,0},{2,3},{3,2},{4,5},{5,4},{6,7},{7,6},{8,9},{9,8},{10,11... | collective-permute-start | bytes 589832 | tf_op jit(solution)/shard_map/ppermute | solution.py:175
  32.8 9.7 %collective-permute-start.14 = (bf16[6,128,128]{2,1,0:T(8,128)(2,1)S(1)}, bf16[6,128,128]{2,1,0:T(8,128)(2,1)S(1)}, u32[]{:S(2)}, u32[]{:S(2)}) collective-permute-start(bf16[6,128,128]{2,1,0:T(8,128)(2,1)S(1)} %collective-permute-done.6), channel_id=1, source_target_pairs={{0,1},{1,0},{2,3},{3,2},{4,5},{5,4},{6,7},{7,6},{8,9},{9,8},{10,11... | collective-permute-start | bytes 589832 | tf_op jit(solution)/shard_map/ppermute | solution.py:175
  41.5 1.4 %collective-permute-start.8 = (bf16[6,128,128]{2,1,0:T(8,128)(2,1)S(1)}, bf16[6,128,128]{2,1,0:T(8,128)(2,1)S(1)}, u32[]{:S(2)}, u32[]{:S(2)}) collective-permute-start(bf16[6,128,128]{2,1,0:T(8,128)(2,1)S(1)} %collective-permute-done), channel_id=1, source_target_pairs={{0,1},{1,0},{2,3},{3,2},{4,5},{5,4},{6,7},{7,6},{8,9},{9,8},{10,11... | collective-permute-start | bytes 589832 | tf_op jit(solution)/shard_map/ppermute | solution.py:175
  41.5 1.7 %collective-permute-start.9 = (bf16[6,128,128]{2,1,0:T(8,128)(2,1)S(1)}, bf16[6,128,128]{2,1,0:T(8,128)(2,1)S(1)}, u32[]{:S(2)}, u32[]{:S(2)}) collective-permute-start(bf16[6,128,128]{2,1,0:T(8,128)(2,1)S(1)} %collective-permute-done.1), channel_id=1, source_target_pairs={{0,1},{1,0},{2,3},{3,2},{4,5},{5,4},{6,7},{7,6},{8,9},{9,8},{10,11... | collective-permute-start | bytes 589832 | tf_op jit(solution)/shard_map/ppermute | solution.py:175
  42.0 1.5 %collective-permute-start.10 = (bf16[6,128,128]{2,1,0:T(8,128)(2,1)S(1)}, bf16[6,128,128]{2,1,0:T(8,128)(2,1)S(1)}, u32[]{:S(2)}, u32[]{:S(2)}) collective-permute-start(bf16[6,128,128]{2,1,0:T(8,128)(2,1)S(1)} %collective-permute-done.2), channel_id=1, source_target_pairs={{0,1},{1,0},{2,3},{3,2},{4,5},{5,4},{6,7},{7,6},{8,9},{9,8},{10,11... | collective-permute-start | bytes 589832 | tf_op jit(solution)/shard_map/ppermute | solution.py:175
  42.1 1.7 %collective-permute-start.11 = (bf16[6,128,128]{2,1,0:T(8,128)(2,1)S(1)}, bf16[6,128,128]{2,1,0:T(8,128)(2,1)S(1)}, u32[]{:S(2)}, u32[]{:S(2)}) collective-permute-start(bf16[6,128,128]{2,1,0:T(8,128)(2,1)S(1)} %collective-permute-done.3), channel_id=1, source_target_pairs={{0,1},{1,0},{2,3},{3,2},{4,5},{5,4},{6,7},{7,6},{8,9},{9,8},{10,11... | collective-permute-start | bytes 589832 | tf_op jit(solution)/shard_map/ppermute | solution.py:175
  43.8 2.3 %copy-start = (s32[16]{0:T(128)S(1)}, s32[16]{0:T(128)}, u32[]{:S(2)}) copy-start(s32[16]{0:T(128)} %lengths.9) | copy-start | bytes 196
  47.8 7.7 %collective-permute-start.16 = (bf16[4,128,128]{2,1,0:T(8,128)(2,1)S(1)}, bf16[4,128,128]{2,1,0:T(8,128)(2,1)S(1)}, u32[]{:S(2)}, u32[]{:S(2)}) collective-permute-start(bf16[4,128,128]{2,1,0:T(8,128)(2,1)S(1)} %get-tuple-element.17), channel_id=1, source_target_pairs={{0,2},{1,3},{2,0},{3,1},{4,6},{5,7},{6,4},{7,5},{8,10},{9,11},{10,... | collective-permute-start | bytes 393224 | tf_op jit(solution)/shard_map/ppermute | solution.py:175
  49.2 14.5 %collective-permute-start.18 = (bf16[4,128,128]{2,1,0:T(8,128)(2,1)S(1)}, bf16[4,128,128]{2,1,0:T(8,128)(2,1)S(1)}, u32[]{:S(2)}, u32[]{:S(2)}) collective-permute-start(bf16[4,128,128]{2,1,0:T(8,128)(2,1)S(1)} %get-tuple-element.15.refs_0_), channel_id=1, source_target_pairs={{0,8},{1,9},{2,10},{3,11},{4,12},{5,13},{6,14},{7,15},{8,0},{9,1},... | collective-permute-start | bytes 393224 | tf_op jit(solution)/shard_map/ppermute | solution.py:175
  51.3 13.7 %collective-permute-start.15 = (bf16[4,128,128]{2,1,0:T(8,128)(2,1)S(1)}, bf16[4,128,128]{2,1,0:T(8,128)(2,1)S(1)}, u32[]{:S(2)}, u32[]{:S(2)}) collective-permute-start(bf16[4,128,128]{2,1,0:T(8,128)(2,1)S(1)} %get-tuple-element.16), channel_id=1, source_target_pairs={{0,10},{1,11},{2,8},{3,9},{4,14},{5,15},{6,12},{7,13},{8,2},{9,3},... | collective-permute-start | bytes 393224 | tf_op jit(solution)/shard_map/ppermute | solution.py:175
  55.2 12.2 %collective-permute-start.17 = (bf16[4,128,128]{2,1,0:T(8,128)(2,1)S(1)}, bf16[4,128,128]{2,1,0:T(8,128)(2,1)S(1)}, u32[]{:S(2)}, u32[]{:S(2)}) collective-permute-start(bf16[4,128,128]{2,1,0:T(8,128)(2,1)S(1)} %get-tuple-element.18), channel_id=1, source_target_pairs={{0,4},{1,5},{2,6},{3,7},{4,0},{5,1},{6,2},{7,3},{8,12},{9,13},{10,... | collective-permute-start | bytes 393224 | tf_op jit(solution)/shard_map/ppermute | solution.py:175
  59.4 14.8 %collective-permute-start.20 = (bf16[4,128,128]{2,1,0:T(8,128)(2,1)S(1)}, bf16[4,128,128]{2,1,0:T(8,128)(2,1)S(1)}, u32[]{:S(2)}, u32[]{:S(2)}) collective-permute-start(bf16[4,128,128]{2,1,0:T(8,128)(2,1)S(1)} %get-tuple-element.19), channel_id=1, source_target_pairs={{0,12},{1,13},{2,14},{3,15},{4,8},{5,9},{6,10},{7,11},{8,4},{9,5},... | collective-permute-start | bytes 393224 | tf_op jit(solution)/shard_map/ppermute | solution.py:175
  59.9 14.5 %collective-permute-start.21 = (bf16[4,128,128]{2,1,0:T(8,128)(2,1)S(1)}, bf16[4,128,128]{2,1,0:T(8,128)(2,1)S(1)}, u32[]{:S(2)}, u32[]{:S(2)}) collective-permute-start(bf16[4,128,128]{2,1,0:T(8,128)(2,1)S(1)} %get-tuple-element.20), channel_id=1, source_target_pairs={{0,14},{1,15},{2,12},{3,13},{4,10},{5,11},{6,8},{7,9},{8,6},{9,7},... | collective-permute-start | bytes 393224 | tf_op jit(solution)/shard_map/ppermute | solution.py:175
  64.8 8.9 %collective-permute-start.19 = (bf16[4,128,128]{2,1,0:T(8,128)(2,1)S(1)}, bf16[4,128,128]{2,1,0:T(8,128)(2,1)S(1)}, u32[]{:S(2)}, u32[]{:S(2)}) collective-permute-start(bf16[4,128,128]{2,1,0:T(8,128)(2,1)S(1)} %attend.8), channel_id=1, source_target_pairs={{0,6},{1,7},{2,4},{3,5},{4,2},{5,3},{6,0},{7,1},{8,14},{9,15},{10,... | collective-permute-start | bytes 393224 | tf_op jit(solution)/shard_map/ppermute | solution.py:175
  74.6 1.0 %copy-start.2 = (bf16[8,4,128,128]{3,1,0,2:T(4,128)(2,1)}, bf16[8,4,128,128]{3,1,0,2:T(4,128)(2,1)S(1)}, u32[]{:S(2)}) copy-start(bf16[8,4,128,128]{3,1,0,2:T(4,128)(2,1)S(1)} %copy_dynamic-update-slice_fusion) | copy-start | bytes 3145732
